TPU v7x, 32 devices: a whole 2x2x4 slice. The times are simulated.
32 devices in a mesh: dp: 8 (over z, y), expert: 4 (over x, core).
Axes of the slice: x: 2, y: 2, z: 4, core: 2. Of those that a mesh axis runs over, the one named last changes fastest.
Arguments:
- inputs: bfloat16 [8192, 1024], P(('dp', 'expert')), may hold values from -6 to 6
- lengths: int32 [32], P(('dp', 'expert')), may hold values from 129 to 256, as said below
- routes: int32 [8192, 8], P(('dp', 'expert')), may hold values from 0 to 15, all different within a row; in each aligned block of 256 rows (0 to 255, 256 to 511, ...) at most 192 rows name the same one
- adapter_of_sequence: int32 [32], P(('dp', 'expert')), may hold values from 0 to 7
- first_norm_gain: float32 [1024], replicated, may hold values from 0.5 to 1.5
- query_weight: bfloat16 [1024, 1024], replicated, may hold values from -0.1875 to 0.1875
- key_value_weight: bfloat16 [1024, 1024], replicated, may hold values from -0.1875 to 0.1875
- output_weight: bfloat16 [1024, 1024], replicated, may hold values from -0.75 to 0.75
- second_norm_gain: float32 [1024], replicated, may hold values from 0.5 to 1.5
- router_weight: bfloat16 [1024, 16], replicated, may hold values from -0.09375 to 0.09375
- expert_input_weight: bfloat16 [16, 1024, 1024], P('expert'), may hold values from -0.1875 to 0.1875
- expert_down_weight: bfloat16 [16, 512, 1024], P('expert'), may hold values from -0.75 to 0.75
- attention_first_factors: bfloat16 [1024, 384], replicated, may hold values from -0.1875 to 0.1875
- query_second_factors: bfloat16 [128, 1024], replicated, may hold values from -0.59765625 to 0.59765625
- key_value_second_factors: bfloat16 [2, 128, 512], replicated, may hold values from -0.59765625 to 0.59765625
- output_first_factors: bfloat16 [1024, 128], replicated, may hold values from -0.75 to 0.75
- output_second_factors: bfloat16 [128, 1024], replicated, may hold values from -1.5 to 1.5
- expert_input_first_factors: bfloat16 [16, 1024, 256], P('expert'), may hold values from -0.1875 to 0.1875
- expert_input_second_factors: bfloat16 [16, 2, 128, 512], P('expert'), may hold values from -0.59765625 to 0.59765625
- expert_down_first_factors: bfloat16 [16, 512, 128], P('expert'), may hold values from -0.25 to 0.25
- expert_down_second_factors: bfloat16 [16, 128, 1024], P('expert'), may hold values from -1.796875 to 1.796875
- output_gradient: bfloat16 [8192, 1024], P(('dp', 'expert')), may hold values from -6 to 6
Outputs:
- output: bfloat16 [8192, 1024], P(('dp', 'expert'))
- grad_input: float32 [8192, 1024], P(('dp', 'expert'))
- grad_attn_lora_a: float32 [1024, 384], replicated
- grad_q_lora_b: float32 [128, 1024], replicated
- grad_kv_lora_b: float32 [2, 128, 512], replicated
- grad_o_lora_a: float32 [1024, 128], replicated
- grad_o_lora_b: float32 [128, 1024], replicated
- grad_exp_lora_a_in: float32 [16, 1024, 256], P('expert')
- grad_exp_lora_b_in: float32 [16, 2, 128, 512], P('expert')
- grad_exp_lora_a_down: float32 [16, 512, 128], P('expert')
- grad_exp_lora_b_down: float32 [16, 128, 1024], P('expert')
Inputs may be any that keep to these rules, and one draw needn't show every extreme that they name: `lengths`: every sequence holds more than half of its 256 slots; some sequence in every draw fills all 256. `routes`: the 8 experts of a row differ. In each aligned block of 256 rows (one sequence) no expert is named by more than 192 rows, a bound that some block reaches.
All inputs are finite; a program needn't handle non-finite values.
Results may differ from a plain program's by a relative error of at most 0.02.
Values may be sent and summed in bfloat16 or wider, within the bound.
No kernel may reach another device: no remote copies, remote signals or barrier semaphores. Data moves between devices by JAX's collectives and lax.ppermute only.
A program may use at most 192 MiB of HBM per device.

v0:
```python
import jax
import jax.numpy as jnp
from jax import lax
from jax.sharding import PartitionSpec as P

MODEL_WIDTH = 1024
QUERY_HEAD_COUNT = 16
KEY_VALUE_HEADS = 8
HEAD_WIDTH = 64
HIDDEN_UNITS = 512
TOP = 8
EXP_DEV = 4
ADAPTER_COUNT = 8
ADAPTER_RANK = 16
TOK_DEV = 256


norm_eps = 1e-06
rope_base = 10000.0


def rms_norm(value_rows, gain):
    factor = lax.rsqrt(jnp.mean(value_rows * value_rows, axis=-1, keepdims=True) + norm_eps)
    return value_rows * factor * gain


def rope_tables(row_count, head_dim):
    half_dim = head_dim // 2
    positions = jnp.arange(row_count, dtype=jnp.float32)
    inverse = rope_base ** (-2.0 * jnp.arange(half_dim, dtype=jnp.float32) / head_dim)
    angles = positions[:, None] * inverse[None, :]
    cosine_table = jnp.concatenate([jnp.cos(angles), jnp.cos(angles)], axis=1)
    sine_table = jnp.concatenate([jnp.sin(angles), jnp.sin(angles)], axis=1)
    return (cosine_table, sine_table)


def rotate(value_rows, cosine_table, sine_table, head_dim):
    row_count = value_rows.shape[0]
    head_values = value_rows.reshape(row_count, -1, head_dim)
    half_dim = head_dim // 2
    turned = jnp.concatenate([-head_values[..., half_dim:], head_values[..., :half_dim]], axis=-1)
    result = head_values * cosine_table[:, None, :] + turned * sine_table[:, None, :]
    return result.reshape(row_count, -1)


def rotate_back(grads, cosine_table, sine_table, head_dim):
    unused_value, pullback = jax.vjp(
        lambda value_rows: rotate(value_rows, cosine_table, sine_table, head_dim),
        jnp.zeros_like(grads),
    )
    return pullback(grads)[0]


def slot_tables(route_rows, expert_count, capacity):
    row_count = route_rows.shape[0]
    top_count = route_rows.shape[1]
    pair_count = row_count * top_count
    flat_routes = route_rows.reshape(-1)
    onehot = (flat_routes[:, None] == jnp.arange(expert_count, dtype=jnp.int32)[None, :]).astype(
        jnp.int32
    )
    before = jnp.cumsum(onehot, axis=0, dtype=jnp.int32) - onehot
    slot_rank = jnp.sum(before * onehot, axis=1, dtype=jnp.int32)
    slot_flat = flat_routes * capacity + slot_rank
    slot_pair = (
        jnp.full((expert_count * capacity,), pair_count, jnp.int32)
        .at[slot_flat]
        .set(jnp.arange(pair_count, dtype=jnp.int32))
    )
    slot_token = slot_pair // top_count
    return (slot_flat.reshape(row_count, top_count), slot_pair, slot_token)


def adapter_masks(adapter_rows):
    columns = jnp.arange(ADAPTER_COUNT * ADAPTER_RANK, dtype=jnp.int32) // ADAPTER_RANK
    return (columns[None, None, :] == adapter_rows[..., None]).astype(jnp.bfloat16)


def expert_forward(rows_in, rank_masks, portion_list):
    w_in, w_down, a_in, b_in, a_down, b_down = portion_list
    rank_total_width = ADAPTER_COUNT * ADAPTER_RANK
    combined_masks = jnp.concatenate([rank_masks, rank_masks], axis=-1)
    rank_projection = (
        jnp.einsum("emd,edr->emr", rows_in, a_in, preferred_element_type=jnp.float32)
        * combined_masks
    ).astype(jnp.bfloat16)
    gate_and_up = jnp.einsum("emd,edf->emf", rows_in, w_in, preferred_element_type=jnp.float32)
    gate_preactivation = gate_and_up[..., :HIDDEN_UNITS] + jnp.einsum(
        "emr,erf->emf",
        rank_projection[..., :rank_total_width],
        b_in[:, 0],
        preferred_element_type=jnp.float32,
    )
    upward_projection = gate_and_up[..., HIDDEN_UNITS:] + jnp.einsum(
        "emr,erf->emf",
        rank_projection[..., rank_total_width:],
        b_in[:, 1],
        preferred_element_type=jnp.float32,
    )
    active_adapter = (jax.nn.silu(gate_preactivation) * upward_projection).astype(jnp.bfloat16)
    down_rank_values = (
        jnp.einsum("emf,efr->emr", active_adapter, a_down, preferred_element_type=jnp.float32)
        * rank_masks
    ).astype(jnp.bfloat16)
    result = jnp.einsum("emf,efd->emd", active_adapter, w_down, preferred_element_type=jnp.float32)
    result = (
        result
        + jnp.einsum("emr,erd->emd", down_rank_values, b_down, preferred_element_type=jnp.float32)
    ).astype(jnp.bfloat16)
    return (
        rank_projection,
        gate_preactivation,
        upward_projection,
        active_adapter,
        down_rank_values,
        result,
    )


def expert_backward(rows_in, rank_masks, grad_in, portion_list):
    w_in, w_down, a_in, b_in, a_down, b_down = portion_list
    rank_total_width = ADAPTER_COUNT * ADAPTER_RANK
    (
        rank_projection,
        gate_preactivation,
        upward_projection,
        active_adapter,
        down_rank_values,
        unused_result,
    ) = expert_forward(rows_in, rank_masks, portion_list)
    grad_b_down = jnp.einsum(
        "emr,emd->erd", down_rank_values, grad_in, preferred_element_type=jnp.float32
    )
    grad_down_rank = (
        jnp.einsum("emd,erd->emr", grad_in, b_down, preferred_element_type=jnp.float32).astype(
            jnp.bfloat16
        )
        * rank_masks
    )
    grad_a_down = jnp.einsum(
        "emf,emr->efr", active_adapter, grad_down_rank, preferred_element_type=jnp.float32
    )
    grad_active = jnp.einsum("emd,efd->emf", grad_in, w_down, preferred_element_type=jnp.float32)
    grad_active = (
        grad_active
        + jnp.einsum("emr,efr->emf", grad_down_rank, a_down, preferred_element_type=jnp.float32)
    ).astype(jnp.bfloat16)
    sigmoid_gate = jax.nn.sigmoid(gate_preactivation)
    grad_gate = (
        grad_active
        * (upward_projection * sigmoid_gate * (1.0 + gate_preactivation * (1.0 - sigmoid_gate)))
    ).astype(jnp.bfloat16)
    grad_up = (grad_active * (gate_preactivation * sigmoid_gate)).astype(jnp.bfloat16)
    grad_b_in = jnp.stack(
        [
            jnp.einsum(
                "emr,emf->erf",
                rank_projection[..., :rank_total_width],
                grad_gate,
                preferred_element_type=jnp.float32,
            ),
            jnp.einsum(
                "emr,emf->erf",
                rank_projection[..., rank_total_width:],
                grad_up,
                preferred_element_type=jnp.float32,
            ),
        ],
        axis=1,
    )
    grad_lowrank = jnp.concatenate(
        [
            jnp.einsum("emf,erf->emr", grad_gate, b_in[:, 0], preferred_element_type=jnp.float32),
            jnp.einsum("emf,erf->emr", grad_up, b_in[:, 1], preferred_element_type=jnp.float32),
        ],
        axis=-1,
    ).astype(jnp.bfloat16)
    grad_lowrank = grad_lowrank * jnp.concatenate([rank_masks, rank_masks], axis=-1)
    grad_a_in = jnp.einsum(
        "emd,emr->edr", rows_in, grad_lowrank, preferred_element_type=jnp.float32
    )
    grad_rows = jnp.einsum(
        "emf,edf->emd",
        jnp.concatenate([grad_gate, grad_up], axis=-1),
        w_in,
        preferred_element_type=jnp.float32,
    )
    grad_rows = (
        grad_rows
        + jnp.einsum("emr,edr->emd", grad_lowrank, a_in, preferred_element_type=jnp.float32)
    ).astype(jnp.bfloat16)
    return (grad_rows, grad_a_in, grad_b_in, grad_a_down, grad_b_down)


def on_device(
    inputs,
    lengths,
    routes,
    adapter_of_sequence,
    first_norm_gain,
    query_weight,
    key_value_weight,
    output_weight,
    second_norm_gain,
    router_weight,
    expert_input_weight,
    expert_down_weight,
    attention_first_factors,
    query_second_factors,
    key_value_second_factors,
    output_first_factors,
    output_second_factors,
    expert_input_first_factors,
    expert_input_second_factors,
    expert_down_first_factors,
    expert_down_second_factors,
    output_gradient,
):
    experts = EXP_DEV * lax.axis_size("expert")
    capacity = 3 * TOK_DEV * TOP // (2 * experts)
    rank_total_width = ADAPTER_COUNT * ADAPTER_RANK
    key_value_width = KEY_VALUE_HEADS * HEAD_WIDTH
    groups = QUERY_HEAD_COUNT // KEY_VALUE_HEADS
    score_scale = HEAD_WIDTH ** (-0.5)
    block_rows = min(512, TOK_DEV)
    length = lengths[0]
    adapter = adapter_of_sequence[0]
    start_offset = adapter * ADAPTER_RANK
    positions = jnp.arange(TOK_DEV, dtype=jnp.int32)
    live = (positions < length).astype(jnp.float32)[:, None]
    source = inputs.astype(jnp.float32)
    portion_list = (
        expert_input_weight,
        expert_down_weight,
        expert_input_first_factors,
        expert_input_second_factors,
        expert_down_first_factors,
        expert_down_second_factors,
    )
    normalized_input = rms_norm(source, first_norm_gain).astype(jnp.bfloat16)
    adapter_input = jnp.concatenate(
        [
            lax.dynamic_slice_in_dim(
                attention_first_factors,
                portion_index * rank_total_width + start_offset,
                ADAPTER_RANK,
                1,
            )
            for portion_index in range(3)
        ],
        axis=1,
    )
    query_second_factor = lax.dynamic_slice_in_dim(
        query_second_factors, start_offset, ADAPTER_RANK, 0
    )
    key_second_factor = lax.dynamic_slice_in_dim(
        key_value_second_factors[0], start_offset, ADAPTER_RANK, 0
    )
    value_second_factor = lax.dynamic_slice_in_dim(
        key_value_second_factors[1], start_offset, ADAPTER_RANK, 0
    )
    output_first_factor = lax.dynamic_slice_in_dim(
        output_first_factors, start_offset, ADAPTER_RANK, 1
    )
    output_second_factor = lax.dynamic_slice_in_dim(
        output_second_factors, start_offset, ADAPTER_RANK, 0
    )
    rank_projection = jnp.dot(
        normalized_input, adapter_input, preferred_element_type=jnp.float32
    ).astype(jnp.bfloat16)
    rank_query = rank_projection[:, :ADAPTER_RANK]
    rank_key = rank_projection[:, ADAPTER_RANK : 2 * ADAPTER_RANK]
    rank_value = rank_projection[:, 2 * ADAPTER_RANK :]
    query_preactivation = jnp.dot(
        normalized_input, query_weight, preferred_element_type=jnp.float32
    ) + jnp.dot(rank_query, query_second_factor, preferred_element_type=jnp.float32)
    key_value_base = jnp.dot(normalized_input, key_value_weight, preferred_element_type=jnp.float32)
    key_preactivation = key_value_base[:, :key_value_width] + jnp.dot(
        rank_key, key_second_factor, preferred_element_type=jnp.float32
    )
    value_rows = (
        key_value_base[:, key_value_width:]
        + jnp.dot(rank_value, value_second_factor, preferred_element_type=jnp.float32)
    ).astype(jnp.bfloat16)
    cosine_table, sine_table = rope_tables(TOK_DEV, HEAD_WIDTH)
    queries = rotate(query_preactivation, cosine_table, sine_table, HEAD_WIDTH).astype(jnp.bfloat16)
    key_rows = rotate(key_preactivation, cosine_table, sine_table, HEAD_WIDTH).astype(jnp.bfloat16)
    query_heads = queries.reshape(TOK_DEV, KEY_VALUE_HEADS, groups, HEAD_WIDTH)
    key_heads = key_rows.reshape(TOK_DEV, KEY_VALUE_HEADS, HEAD_WIDTH)
    value_heads = value_rows.reshape(TOK_DEV, KEY_VALUE_HEADS, HEAD_WIDTH)

    def block_scores(row_start):
        raw_scores = (
            jnp.einsum("qjgd,kjd->jgqk", query_heads, key_heads, preferred_element_type=jnp.float32)
            * score_scale
        )
        block_positions = row_start + jnp.arange(block_rows, dtype=jnp.int32)
        allowed = (positions[None, :] <= block_positions[:, None]) & (positions[None, :] < length)
        return (query_heads, jnp.where(allowed, raw_scores, -1e30))

    row_start = 0
    query_block, masked = block_scores(row_start)
    top_score = jnp.max(masked, axis=-1, keepdims=True)
    exponent = jnp.exp(masked - top_score)
    row_total = jnp.sum(exponent, axis=-1, keepdims=True)
    probs_block = (exponent / row_total).astype(jnp.bfloat16)
    log_totals = [top_score + jnp.log(row_total)]
    attended_parts = jnp.einsum(
        "jgqk,kjd->qjgd", probs_block, value_heads, preferred_element_type=jnp.float32
    ).astype(jnp.bfloat16)
    attention_result = attended_parts.reshape(TOK_DEV, QUERY_HEAD_COUNT * HEAD_WIDTH)
    output_rank_values = jnp.dot(
        attention_result, output_first_factor, preferred_element_type=jnp.float32
    ).astype(jnp.bfloat16)
    hidden = (
        source
        + jnp.dot(attention_result, output_weight, preferred_element_type=jnp.float32)
        + jnp.dot(output_rank_values, output_second_factor, preferred_element_type=jnp.float32)
    )
    normed2 = rms_norm(hidden, second_norm_gain).astype(jnp.bfloat16)
    logits = jnp.dot(normed2, router_weight, preferred_element_type=jnp.float32)
    chosen = jnp.take_along_axis(logits, routes, axis=1)
    chosen_exp = jnp.exp(chosen - jnp.max(chosen, axis=1, keepdims=True))
    softened = chosen_exp / jnp.sum(chosen_exp, axis=1, keepdims=True)
    pair_gates = softened * live
    grad_output = output_gradient.astype(jnp.float32) * live
    slot_of = slot_tables(routes, experts, capacity)[0]
    slot_numbers = jnp.arange(experts * capacity, dtype=jnp.int32)
    pair_slots = (slot_of[:, :, None] == slot_numbers[None, None, :]).astype(jnp.bfloat16)
    token_slots = jnp.sum(pair_slots, axis=1)
    send_rows = (
        jnp.einsum("ts,td->sd", token_slots, normed2, preferred_element_type=jnp.float32)
        .astype(jnp.bfloat16)
        .reshape(experts, capacity, MODEL_WIDTH)
    )
    send_ids = jnp.full((experts, capacity), adapter, jnp.int32)
    recv_rows, recv_ids = (
        lax.all_to_all(send_rows, "expert", split_axis=0, concat_axis=1, tiled=True),
        lax.all_to_all(send_ids, "expert", split_axis=0, concat_axis=1, tiled=True),
    )
    expert_result = expert_forward(recv_rows, adapter_masks(recv_ids), portion_list)[-1]
    returned = lax.all_to_all(expert_result, "expert", split_axis=1, concat_axis=0, tiled=True)
    flat_back = returned.reshape(experts * capacity, MODEL_WIDTH)
    picked = jnp.einsum("tks,sd->tkd", pair_slots, flat_back, preferred_element_type=jnp.float32)
    mixture = hidden + jnp.sum(pair_gates[:, :, None] * picked, axis=1)
    grad_chosen = jnp.sum(grad_output[:, None, :] * picked, axis=-1)
    slot_gates = jnp.einsum(
        "tks,tk->s", pair_slots.astype(jnp.float32), pair_gates, precision=lax.Precision.HIGHEST
    )
    slot_grad_rows = jnp.einsum(
        "ts,td->sd", token_slots.astype(jnp.float32), grad_output, precision=lax.Precision.HIGHEST
    )
    grad_send = (
        (slot_gates[:, None] * slot_grad_rows)
        .astype(jnp.bfloat16)
        .reshape(experts, capacity, MODEL_WIDTH)
    )
    output = (live * mixture).astype(jnp.bfloat16)
    grad_sel = softened * (grad_chosen - jnp.sum(softened * grad_chosen, axis=1, keepdims=True))
    expert_numbers = jnp.arange(experts, dtype=jnp.int32)
    grad_logits = jnp.sum(
        (routes[:, :, None] == expert_numbers[None, None, :]).astype(jnp.float32)
        * grad_sel[:, :, None],
        axis=1,
    )
    grad_normed2 = jnp.dot(
        grad_logits, router_weight.astype(jnp.float32).T, precision=lax.Precision.HIGHEST
    )
    grad_in, rows_again, ids_again = (
        lax.all_to_all(grad_send, "expert", split_axis=0, concat_axis=1, tiled=True),
        lax.all_to_all(send_rows, "expert", split_axis=0, concat_axis=1, tiled=True),
        lax.all_to_all(send_ids, "expert", split_axis=0, concat_axis=1, tiled=True),
    )
    grad_local, local_a_in, local_b_in, local_a_down, local_b_down = expert_backward(
        rows_again, adapter_masks(ids_again), grad_in, portion_list
    )
    grad_back = lax.all_to_all(grad_local, "expert", split_axis=1, concat_axis=0, tiled=True)
    expert_grads = (local_a_in, local_b_in, local_a_down, local_b_down)
    flat_grad = grad_back.reshape(experts * capacity, MODEL_WIDTH)
    grad_normed2 = grad_normed2 + jnp.einsum(
        "tks,sd->td", pair_slots, flat_grad, preferred_element_type=jnp.float32
    )
    summed_experts = (
        lax.psum(expert_grads[0].astype(jnp.bfloat16), "dp").astype(jnp.float32),
        lax.psum(expert_grads[1].astype(jnp.bfloat16), "dp").astype(jnp.float32),
        lax.psum(expert_grads[2].astype(jnp.bfloat16), "dp").astype(jnp.float32),
        lax.psum(expert_grads[3].astype(jnp.bfloat16), "dp").astype(jnp.float32),
    )
    unused_hidden, norm2_back = jax.vjp(
        lambda values_in: rms_norm(values_in, second_norm_gain), hidden
    )
    grad_hidden = grad_output + norm2_back(grad_normed2)[0]
    grad_branch = grad_hidden.astype(jnp.bfloat16)
    grad_b_out = jnp.dot(output_rank_values.T, grad_branch, preferred_element_type=jnp.float32)
    grad_out_rank = jnp.dot(
        grad_branch, output_second_factor.T, preferred_element_type=jnp.float32
    ).astype(jnp.bfloat16)
    grad_a_out = jnp.dot(attention_result.T, grad_out_rank, preferred_element_type=jnp.float32)
    grad_attended = jnp.dot(grad_branch, output_weight.T, preferred_element_type=jnp.float32)
    grad_attended = (
        grad_attended
        + jnp.dot(grad_out_rank, output_first_factor.T, preferred_element_type=jnp.float32)
    ).astype(jnp.bfloat16)
    grad_heads = grad_attended.reshape(TOK_DEV, KEY_VALUE_HEADS, groups, HEAD_WIDTH)
    grad_keys = jnp.zeros((TOK_DEV, KEY_VALUE_HEADS, HEAD_WIDTH), jnp.float32)
    grad_values = jnp.zeros((TOK_DEV, KEY_VALUE_HEADS, HEAD_WIDTH), jnp.float32)
    query_parts = []
    for block_index, row_start in enumerate(range(0, TOK_DEV, block_rows)):
        query_block, masked = block_scores(row_start)
        probs_exact = jnp.exp(masked - log_totals[block_index])
        probs_block = probs_exact.astype(jnp.bfloat16)
        grad_values = jnp.einsum(
            "jgqk,qjgd->kjd", probs_block, grad_heads, preferred_element_type=jnp.float32
        )
        grad_probs = jnp.einsum(
            "qjgd,kjd->jgqk", grad_heads, value_heads, preferred_element_type=jnp.float32
        ).astype(jnp.bfloat16)
        row_inner = jnp.sum(grad_probs * probs_exact, axis=-1, keepdims=True)
        grad_scores = (probs_exact * (grad_probs - row_inner)).astype(jnp.bfloat16)
        query_parts.append(
            jnp.einsum("jgqk,kjd->qjgd", grad_scores, key_heads, preferred_element_type=jnp.float32)
            * score_scale
        )
        grad_keys = (
            jnp.einsum(
                "jgqk,qjgd->kjd", grad_scores, query_block, preferred_element_type=jnp.float32
            )
            * score_scale
        )
    grad_query = query_parts[0].reshape(TOK_DEV, QUERY_HEAD_COUNT * HEAD_WIDTH)
    grad_query_pre = rotate_back(grad_query, cosine_table, sine_table, HEAD_WIDTH).astype(
        jnp.bfloat16
    )
    grad_key_pre = rotate_back(
        grad_keys.reshape(TOK_DEV, key_value_width), cosine_table, sine_table, HEAD_WIDTH
    ).astype(jnp.bfloat16)
    grad_value = grad_values.reshape(TOK_DEV, key_value_width).astype(jnp.bfloat16)
    grad_b_query = jnp.dot(rank_query.T, grad_query_pre, preferred_element_type=jnp.float32)
    grad_b_key = jnp.dot(rank_key.T, grad_key_pre, preferred_element_type=jnp.float32)
    grad_b_value = jnp.dot(rank_value.T, grad_value, preferred_element_type=jnp.float32)
    gradient_rank_values = jnp.concatenate(
        [
            jnp.dot(grad_query_pre, query_second_factor.T, preferred_element_type=jnp.float32),
            jnp.dot(grad_key_pre, key_second_factor.T, preferred_element_type=jnp.float32),
            jnp.dot(grad_value, value_second_factor.T, preferred_element_type=jnp.float32),
        ],
        axis=1,
    ).astype(jnp.bfloat16)
    gradient_adapter_input = jnp.dot(
        normalized_input.T, gradient_rank_values, preferred_element_type=jnp.float32
    )
    gradient_of_normed = jnp.dot(grad_query_pre, query_weight.T, preferred_element_type=jnp.float32)
    gradient_of_normed = gradient_of_normed + jnp.dot(
        jnp.concatenate([grad_key_pre, grad_value], axis=1),
        key_value_weight.T,
        preferred_element_type=jnp.float32,
    )
    gradient_of_normed = gradient_of_normed + jnp.dot(
        gradient_rank_values, adapter_input.T, preferred_element_type=jnp.float32
    )
    unused_source, norm1_back = jax.vjp(
        lambda values_in: rms_norm(values_in, first_norm_gain), source
    )
    grad_input = grad_hidden + norm1_back(gradient_of_normed)[0]
    gathered_adapter_input = jnp.zeros((MODEL_WIDTH, 3 * rank_total_width), jnp.float32)
    for portion_index in range(3):
        gathered_adapter_input = lax.dynamic_update_slice_in_dim(
            gathered_adapter_input,
            gradient_adapter_input[
                :, portion_index * ADAPTER_RANK : (portion_index + 1) * ADAPTER_RANK
            ],
            portion_index * rank_total_width + start_offset,
            1,
        )
    gathered_query_second = lax.dynamic_update_slice_in_dim(
        jnp.zeros((rank_total_width, QUERY_HEAD_COUNT * HEAD_WIDTH), jnp.float32),
        grad_b_query,
        start_offset,
        0,
    )
    gathered_key_value_second = jnp.stack(
        [
            lax.dynamic_update_slice_in_dim(
                jnp.zeros((rank_total_width, key_value_width), jnp.float32),
                grad_b_key,
                start_offset,
                0,
            ),
            lax.dynamic_update_slice_in_dim(
                jnp.zeros((rank_total_width, key_value_width), jnp.float32),
                grad_b_value,
                start_offset,
                0,
            ),
        ],
        axis=0,
    )
    gathered_output_first = lax.dynamic_update_slice_in_dim(
        jnp.zeros((QUERY_HEAD_COUNT * HEAD_WIDTH, rank_total_width), jnp.float32),
        grad_a_out,
        start_offset,
        1,
    )
    gathered_output_second = lax.dynamic_update_slice_in_dim(
        jnp.zeros((rank_total_width, MODEL_WIDTH), jnp.float32), grad_b_out, start_offset, 0
    )
    summed_attention = lax.psum(
        (
            gathered_adapter_input,
            gathered_query_second,
            gathered_key_value_second,
            gathered_output_first,
            gathered_output_second,
        ),
        ("dp", "expert"),
    )
    return (
        output,
        grad_input,
        summed_attention[0],
        summed_attention[1],
        summed_attention[2],
        summed_attention[3],
        summed_attention[4],
        summed_experts[0],
        summed_experts[1],
        summed_experts[2],
        summed_experts[3],
    )


def solution(mesh):
    placed = (
        P(("dp", "expert"), None),
        P(("dp", "expert")),
        P(("dp", "expert"), None),
        P(("dp", "expert")),
        P(),
        P(),
        P(),
        P(),
        P(),
        P(),
        P("expert", None, None),
        P("expert", None, None),
        P(),
        P(),
        P(),
        P(),
        P(),
        P("expert", None, None),
        P("expert", None, None, None),
        P("expert", None, None),
        P("expert", None, None),
        P(("dp", "expert"), None),
    )
    return jax.shard_map(
        on_device,
        mesh=mesh,
        in_specs=placed,
        out_specs=(
            P(("dp", "expert"), None),
            P(("dp", "expert"), None),
            P(),
            P(),
            P(),
            P(),
            P(),
            P("expert", None, None),
            P("expert", None, None, None),
            P("expert", None, None),
            P("expert", None, None),
        ),
        check_vma=False,
    )
```

profile of v0, /device:TPU:0, one launch (start us, length us, event | category | flops | bytes accessed | tf_op | source)
XLA Modules:
  0.0 725.6 jit_solution(7825902596796956320)
XLA Ops:
  8.6 4.2 all-to-all-start.1
  20.3 2.6 fusion.120
  44.0 2.5 copy.292
  48.9 2.5 copy.293
  55.1 2.9 add_convert_fusion.3
  66.7 4.7 reduce-window.6
  72.5 3.6 convert_reduce_fusion
  78.4 4.5 convolution_convert_fusion
  82.9 5.6 all-to-all-start
  89.2 16.8 %gather_fusion = f32[2048]{0:T(1024)S(1)} fusion(f32[256,16]{0,1:T(8,128)S(1)} %fusion.115, s32[2048]{0:T(1024)S(1)} %reshape.259), kind=kCustom, calls=%fused_computation | custom fusion | bytes 32768 | tf_op jit(solution)/shard_map/jit(take_along_axis)/gather | solution.py:322
  106.3 7.9 %fusion = f32[1,3072,1]{1,0,2:T(1,128)S(1)} fusion(s32[256,8]{0,1:T(8,128)S(1)} %copy-done.99, f32[256,8,1]{0,1,2:T(8,128)S(1)} %fusion.199), kind=kOutput, calls=%fused_computation.3 | convolution fusion | flops 81788928 | bytes 28672 | tf_op jit(solution)/shard_map/tks,tk->s/dot_general | solution.py:347
  114.2 8.3 %multiply_convert_fusion = bf16[3072,1024]{1,0:T(8,128)(2,1)} fusion(f32[3072]{0:T(1024)S(1)} %bitcast.263, bf16[256,3072]{1,0:T(8,128)(2,1)S(1)} %copy-done.13, bf16[256,1024]{1,0:T(8,128)(2,1)S(1)} %copy-done.43, f32[256]{0:T(256)S(1)} %copy-done.105), kind=kOutput, calls=%fused_computation.7 | convolution fusion | flops 9670492160 | bytes 8401920 | tf_op jit(solution)/shard_map/ts,td->sd/dot_general | solution.py:350
  122.5 37.0 %all-to-all-done = bf16[16,192,1024]{2,1,0:T(8,128)(2,1)} async-done(((bf16[16,192,1024]{2,1,0:T(8,128)(2,1)}), bf16[16,192,1024]{2,1,0:T(8,128)(2,1)}, u32[]{:S(2)}, u32[]{:S(2)}) %all-to-all-start) | async-done | bytes 6291488 | tf_op jit(solution)/shard_map/all_to_all | solution.py:338
  159.5 5.4 all-to-all-start.3
  166.4 4.0 copy.301
  173.0 9.6 %fusion.128 = f32[4,768,1024]{2,1,0:T(8,128)S(1)} fusion(bf16[4,768,1024]{2,1,0:T(8,128)(2,1)S(1)} %bitcast.224, bf16[4,1024,1024]{2,1,0:T(8,128)(2,1)} %param.32), kind=kOutput, calls=%fused_computation.239 | convolution fusion | flops 6442450944 | bytes 27262976 | tf_op jit(solution)/shard_map/emd,edf->emf/dot_general | solution.py:87
  182.7 3.6 slice_add_fusion.1
  186.2 3.5 slice_add_fusion
  189.8 45.8 %all-to-all-done.3 = bf16[16,192,1024]{2,1,0:T(8,128)(2,1)} async-done(((bf16[16,192,1024]{2,1,0:T(8,128)(2,1)}), bf16[16,192,1024]{2,1,0:T(8,128)(2,1)}, u32[]{:S(2)}, u32[]{:S(2)}) %all-to-all-start.3) | async-done | bytes 6291488 | tf_op jit(solution)/shard_map/all_to_all | solution.py:370
  235.6 3.7 copy.309
  239.6 5.4 fusion.130
  247.3 8.6 %fusion.5 = (bf16[4,768,512]{2,1,0:T(8,128)(2,1)S(1)}, bf16[4,768,512]{2,1,0:T(8,128)(2,1)}, bf16[4,768,512]{2,1,0:T(8,128)(2,1)S(1)}) fusion(f32[4,768,512]{2,1,0:T(8,128)S(1)} %bitcast.230, f32[4,768,512]{2,1,0:T(8,128)} %slice_add_fusion, f32[4,768,512]{2,1,0:T(8,128)} %fusion.130, bf16[4,768,128]{2,1,0:T(8,128)(2,1)S(1)} %compare_select_fusion, ...), kind=kOutput, calls=%fused_computation.15 | convolution fusion | flops 430964736 | bytes 29622272 | tf_op jit(solution)/shard_map/emr,efr->emf/dot_general | solution.py:146
  259.3 13.4 %fusion.7 = f32[4,768,1024]{2,1,0:T(8,128)} fusion(bf16[4,1024,1024]{2,1,0:T(8,128)(2,1)} %param.32, bf16[4,768,512]{2,1,0:T(8,128)(2,1)} %copy-done.37, bf16[4,768,512]{2,1,0:T(8,128)(2,1)S(1)} %get-tuple-element.90), kind=kOutput, calls=%fused_computation.19 | convolution fusion | flops 6455033856 | bytes 27262976 | tf_op jit(solution)/shard_map/emf,edf->emd/dot_general | solution.py:182
  275.8 7.3 %add_convert_fusion = bf16[4,768,1024]{2,1,0:T(8,128)(2,1)} fusion(f32[4,768,1024]{2,1,0:T(8,128)} %fusion.7, bf16[4,1024,256]{2,1,0:T(8,128)(2,1)S(1)} %copy-done, bf16[4,768,128]{2,1,0:T(8,128)(2,1)S(1)} %copy-done.60, bf16[4,768,128]{2,1,0:T(8,128)(2,1)S(1)} %convolution_convert_fusion.5, bf16[4,768,128]{2,1,0:T(8,128)(2,1)S(1)} %copy-done.32), kind=kOutput, calls=%fused_computation.6 | convolution fusion | flops 1623195648 | bytes 23330816 | tf_op jit(solution)/shard_map/emr,edr->emd/dot_general | solution.py:190
  283.0 10.2 %copy.316 = bf16[4,768,1024]{2,0,1:T(4,128)(2,1)} copy(bf16[4,768,1024]{2,1,0:T(8,128)(2,1)} %add_convert_fusion) | data formatting | bytes 12582912 | tf_op jit(solution)/shard_map/convert_element_type | solution.py:191
  293.3 5.8 all-to-all-start.4
  299.1 3.0 multiply_convert_fusion.3
  302.1 5.5 fusion.129
  307.7 4.5 add_convert_fusion.1
  312.1 10.3 %copy.307 = bf16[4,768,1024]{2,0,1:T(4,128)(2,1)} copy(bf16[4,768,1024]{2,1,0:T(8,128)(2,1)} %add_convert_fusion.1) | data formatting | bytes 12582912 | tf_op jit(solution)/shard_map/convert_element_type | solution.py:109
  322.5 47.2 %all-to-all-done.4 = bf16[4,768,1024]{2,0,1:T(4,128)(2,1)} async-done(((bf16[4,768,1024]{2,0,1:T(4,128)(2,1)}), bf16[4,768,1024]{2,0,1:T(4,128)(2,1)}, u32[]{:S(2)}, u32[]{:S(2)}) %all-to-all-start.4) | async-done | bytes 6291488 | tf_op jit(solution)/shard_map/all_to_all | solution.py:377
  369.7 5.2 all-to-all-start.2
  376.9 2.7 fusion.26
  381.9 3.4 convolution_convert_fusion.7
  387.4 3.8 convolution_convert_fusion.1
  391.5 4.9 copy.317
  399.7 45.9 %all-to-all-done.2 = bf16[4,768,1024]{2,0,1:T(4,128)(2,1)} async-done(((bf16[4,768,1024]{2,0,1:T(4,128)(2,1)}), bf16[4,768,1024]{2,0,1:T(4,128)(2,1)}, u32[]{:S(2)}, u32[]{:S(2)}) %all-to-all-start.2) | async-done | bytes 6291488 | tf_op jit(solution)/shard_map/all_to_all | solution.py:342
  445.6 5.2 copy.308
  450.9 14.5 %multiply_reduce_fusion = (f32[256,8]{0,1:T(8,128)S(1)}, f32[256,1024]{1,0:T(8,128)S(1)}) fusion(f32[256,1024]{1,0:T(8,128)S(1)} %copy-done.53, f32[256,8]{0,1:T(8,128)S(1)} %copy-done.114, bf16[3072,1024,1]{1,0,2:T(8,128)(2,1)S(1)} %bitcast.231, s32[256,8]{0,1:T(8,128)S(1)} %copy-done.100), kind=kOutput, calls=%fused_computation.11 | convolution fusion | flops 12899317760 | bytes 8413184 | tf_op jit(solution)/shard_map/tks,sd->tkd/dot_general | solution.py:344
  470.2 3.5 fusion.12
  485.0 3.7 dynamic_update_slice.26
  488.7 3.6 dynamic_update_slice.27
  492.3 3.0 dynamic_update_slice.28
  496.4 3.9 dynamic_update_slice.32
  503.1 60.4 %all-reduce.11.cloned.1.call-done = (bf16[4,2,128,512]{3,2,0,1:T(8,128)(2,1)}, bf16[4,1024,256]{2,1,0:T(8,128)(2,1)}, bf16[4,512,128]{2,1,0:T(8,128)(2,1)}, bf16[4,128,1024]{2,1,0:T(8,128)(2,1)}) async-done(((bf16[4,2,128,512]{3,2,0,1:T(8,128)(2,1)}, bf16[4,1024,256]{2,1,0:T(8,128)(2,1)}, bf16[4,512,128]{2,1,0:T(8,128)(2,1)}, bf16[4,128,1024]{2,1,0:T(8,128)(2,1)}), (bf16[4,2,128,512]{3,2,0,1:T(8,128)(2,1)}, ...) | async-done | bytes 4718608 | tf_op jit(solution)/shard_map/psum | solution.py:385
  563.5 4.1 convert_element_type.243
  575.3 135.9 %all-reduce.9.cloned.1.call-done = (f32[1024,384]{1,0:T(8,128)}, f32[128,1024]{1,0:T(8,128)}, f32[2,128,512]{2,1,0:T(8,128)}, f32[1024,128]{1,0:T(8,128)}, f32[128,1024]{1,0:T(8,128)}) async-done(((f32[1024,384]{1,0:T(8,128)}, f32[128,1024]{1,0:T(8,128)}, f32[2,128,512]{2,1,0:T(8,128)}, f32[1024,128]{1,0:T(8,128)}, f32[128,1024]{1,0:T(8,128)}), (f32[1024,384]{1,0:T(8,128)}, f32[128,1024]{1,0:T(8,128)}, ...) | async-done | bytes 3670032 | tf_op jit(solution)/shard_map/psum | solution.py:507
  711.2 2.8 copy.384
  (384 shorter events, 101.1 us)
Async XLA Ops:
  7.2 163.3 %copy-start = (bf16[4,1024,256]{2,1,0:T(8,128)(2,1)S(1)}, bf16[4,1024,256]{2,1,0:T(8,128)(2,1)}, u32[]{:S(2)}) copy-start(bf16[4,1024,256]{2,1,0:T(8,128)(2,1)} %param.39) | copy-start | bytes 6291460
  7.2 15.7 %copy-start.7 = (bf16[256,1024]{1,0:T(8,128)(2,1)S(1)}, bf16[256,1024]{1,0:T(8,128)(2,1)}, u32[]{:S(2)}) copy-start(bf16[256,1024]{1,0:T(8,128)(2,1)} %param.22) | copy-start | bytes 1572868
  7.2 15.7 %copy-start.84 = (f32[1024]{0:T(1024)S(1)}, f32[1024]{0:T(1024)}, u32[]{:S(2)}) copy-start(f32[1024]{0:T(1024)} %param.26) | copy-start | bytes 12292
  8.6 74.3 %all-to-all-start.1 = ((s32[4,4,192]{2,1,0:T(4,128)}), s32[4,4,192]{2,1,0:T(4,128)}, u32[]{:S(2)}, u32[]{:S(2)}) async-start(s32[4,4,192]{2,1,0:T(4,128)} %broadcast_in_dim.27), calls=%async_computation.1 | async-start | bytes 32768 | tf_op jit(solution)/shard_map/all_to_all | solution.py:339
  16.3 23.2 %copy-start.86 = (f32[256]{0:T(256)}, f32[256]{0:T(256)S(1)}, u32[]{:S(2)}) copy-start(f32[256]{0:T(256)S(1)} %fusion.103) | copy-start | bytes 3076
  30.6 17.2 %copy-start.51 = (f32[256,64]{0,1:T(8,128)}, f32[256,64]{0,1:T(8,128)S(1)}, u32[]{:S(2)}) copy-start(f32[256,64]{0,1:T(8,128)S(1)} %get-tuple-element.114) | copy-start | bytes 196612
  30.6 20.9 %copy-start.56 = (f32[256,64]{0,1:T(8,128)}, f32[256,64]{0,1:T(8,128)S(1)}, u32[]{:S(2)}) copy-start(f32[256,64]{0,1:T(8,128)S(1)} %get-tuple-element.129) | copy-start | bytes 196612
  39.5 21.1 %copy-start.38 = (bf16[256,512]{0,1:T(8,128)(2,1)}, bf16[256,512]{0,1:T(8,128)(2,1)S(1)}, u32[]{:S(2)}) copy-start(bf16[256,512]{0,1:T(8,128)(2,1)S(1)} %copy.290) | copy-start | bytes 786436
  64.6 13.8 %copy-start.94 = (f32[1024]{0:T(1024)S(1)}, f32[1024]{0:T(1024)}, u32[]{:S(2)}) copy-start(f32[1024]{0:T(1024)} %param.30) | copy-start | bytes 12292
  66.7 16.2 %copy-start.90 = (bf16[256,16]{0,1:T(8,128)(2,1)}, bf16[256,16]{0,1:T(8,128)(2,1)S(1)}, u32[]{:S(2)}) copy-start(bf16[256,16]{0,1:T(8,128)(2,1)S(1)} %convolution_convert_fusion.13) | copy-start | bytes 24580
  72.4 10.5 %copy-start.98 = (s32[256,8]{0,1:T(8,128)}, s32[256,8]{0,1:T(8,128)S(1)}, u32[]{:S(2)}) copy-start(s32[256,8]{0,1:T(8,128)S(1)} %multiply_add_fusion) | copy-start | bytes 24580
  78.3 10.5 %copy-start.4 = (f32[256,1024]{1,0:T(8,128)}, f32[256,1024]{1,0:T(8,128)S(1)}, u32[]{:S(2)}) copy-start(f32[256,1024]{1,0:T(8,128)S(1)} %get-tuple-element.120) | copy-start | bytes 3145732
  78.4 10.5 %copy-start.108 = (f32[256]{0:T(256)}, f32[256]{0:T(256)S(1)}, u32[]{:S(2)}) copy-start(f32[256]{0:T(256)S(1)} %fusion.104) | copy-start | bytes 3076
  82.9 76.6 %all-to-all-start = ((bf16[16,192,1024]{2,1,0:T(8,128)(2,1)}), bf16[16,192,1024]{2,1,0:T(8,128)(2,1)}, u32[]{:S(2)}, u32[]{:S(2)}) async-start(bf16[16,192,1024]{2,1,0:T(8,128)(2,1)} %bitcast.213), calls=%async_computation | async-start | bytes 12582912 | tf_op jit(solution)/shard_map/all_to_all | solution.py:338
  89.2 17.1 %copy-start.105 = (f32[256]{0:T(256)S(1)}, f32[256]{0:T(256)}, u32[]{:S(2)}) copy-start(f32[256]{0:T(256)} %get-tuple-element.132) | copy-start | bytes 3076
  89.2 17.1 %copy-start.99 = (s32[256,8]{0,1:T(8,128)S(1)}, s32[256,8]{0,1:T(8,128)}, u32[]{:S(2)}) copy-start(s32[256,8]{0,1:T(8,128)} %copy-done.98) | copy-start | bytes 24580
  106.2 269.0 %copy-start.96 = (f32[256]{0:T(256)}, f32[256]{0:T(256)S(1)}, u32[]{:S(2)}) copy-start(f32[256]{0:T(256)S(1)} %get-tuple-element.88) | copy-start | bytes 3076
  106.2 16.3 %copy-start.102 = (f32[256]{0:T(256)}, f32[256]{0:T(256)S(1)}, u32[]{:S(2)}) copy-start(f32[256]{0:T(256)S(1)} %fusion.86) | copy-start | bytes 3076
  159.5 76.1 %all-to-all-start.3 = ((bf16[16,192,1024]{2,1,0:T(8,128)(2,1)}), bf16[16,192,1024]{2,1,0:T(8,128)(2,1)}, u32[]{:S(2)}, u32[]{:S(2)}) async-start(bf16[16,192,1024]{2,1,0:T(8,128)(2,1)} %bitcast.228), calls=%async_computation.3 | async-start | bytes 12582912 | tf_op jit(solution)/shard_map/all_to_all | solution.py:370
  173.0 13.2 %copy-start.20 = (bf16[4,768,256]{2,1,0:T(8,128)(2,1)}, bf16[4,768,256]{2,1,0:T(8,128)(2,1)S(1)}, u32[]{:S(2)}) copy-start(bf16[4,768,256]{2,1,0:T(8,128)(2,1)S(1)} %multiply_convert_fusion.2) | copy-start | bytes 4718596
  173.0 9.7 %copy-start.58 = (bf16[4,2,128,512]{3,2,1,0:T(8,128)(2,1)S(1)}, bf16[4,2,128,512]{3,2,1,0:T(8,128)(2,1)}, u32[]{:S(2)}) copy-start(bf16[4,2,128,512]{3,2,1,0:T(8,128)(2,1)} %param.40) | copy-start | bytes 3145732
  235.6 11.6 %slice-start.4 = ((s8[6291456]{0:T(1024)(128)(4,1)}), s8[4194304]{0:T(1024)(128)(4,1)S(1)}, s32[]{:S(2)}) async-start(s8[6291456]{0:T(1024)(128)(4,1)} %bitcast.229), calls=%async_computation.11 | async-start | bytes 8388608
  247.3 10.2 %copy-start.59 = (bf16[4,2,128,512]{3,2,1,0:T(8,128)(2,1)S(1)}, bf16[4,2,128,512]{3,2,1,0:T(8,128)(2,1)}, u32[]{:S(2)}) copy-start(bf16[4,2,128,512]{3,2,1,0:T(8,128)(2,1)} %param.40) | copy-start | bytes 3145732
  255.8 16.9 %copy-start.35 = (bf16[4,768,512]{2,1,0:T(8,128)(2,1)}, bf16[4,768,512]{2,1,0:T(8,128)(2,1)S(1)}, u32[]{:S(2)}) copy-start(bf16[4,768,512]{2,1,0:T(8,128)(2,1)S(1)} %get-tuple-element.90) | copy-start | bytes 9437188
  293.3 76.4 %all-to-all-start.4 = ((bf16[4,768,1024]{2,0,1:T(4,128)(2,1)}), bf16[4,768,1024]{2,0,1:T(4,128)(2,1)}, u32[]{:S(2)}, u32[]{:S(2)}) async-start(bf16[4,768,1024]{2,0,1:T(4,128)(2,1)} %copy.316), calls=%async_computation.4 | async-start | bytes 12582912 | tf_op jit(solution)/shard_map/all_to_all | solution.py:377
  322.5 52.7 %copy-start.103 = (f32[256]{0:T(256)S(1)}, f32[256]{0:T(256)}, u32[]{:S(2)}) copy-start(f32[256]{0:T(256)} %copy-done.102) | copy-start | bytes 3076
  322.5 52.7 %copy-start.106 = (f32[256]{0:T(256)S(1)}, f32[256]{0:T(256)}, u32[]{:S(2)}) copy-start(f32[256]{0:T(256)} %get-tuple-element.132) | copy-start | bytes 3076
  322.5 53.3 %copy-start.75 = (f32[8,2,256]{2,1,0:T(2,128)S(1)}, f32[8,2,256]{2,1,0:T(2,128)}, u32[]{:S(2)}) copy-start(f32[8,2,256]{2,1,0:T(2,128)} %copy-done.74) | copy-start | bytes 49156
  322.5 53.3 %copy-start.93 = (f32[8,2,256]{2,1,0:T(2,128)S(1)}, f32[8,2,256]{2,1,0:T(2,128)}, u32[]{:S(2)}) copy-start(f32[8,2,256]{2,1,0:T(2,128)} %copy-done.92) | copy-start | bytes 49156
  322.5 54.5 %copy-start.21 = (bf16[4,768,256]{2,1,0:T(8,128)(2,1)S(1)}, bf16[4,768,256]{2,1,0:T(8,128)(2,1)}, u32[]{:S(2)}) copy-start(bf16[4,768,256]{2,1,0:T(8,128)(2,1)} %copy-done.20) | copy-start | bytes 4718596
  369.7 75.9 %all-to-all-start.2 = ((bf16[4,768,1024]{2,0,1:T(4,128)(2,1)}), bf16[4,768,1024]{2,0,1:T(4,128)(2,1)}, u32[]{:S(2)}, u32[]{:S(2)}) async-start(bf16[4,768,1024]{2,0,1:T(4,128)(2,1)} %copy.307), calls=%async_computation.2 | async-start | bytes 12582912 | tf_op jit(solution)/shard_map/all_to_all | solution.py:342
  374.9 188.6 %all-reduce.11.cloned.1.call-start = ((), (), s32[]{:S(2)}) async-start(), calls=%async_computation.6 | async-start | bytes 9437184 | tf_op jit(solution)/shard_map/psum | solution.py:385
  391.3 319.9 %all-reduce.9.cloned.1.call-start = ((), (), s32[]{:S(2)}) async-start(), calls=%async_computation.5 | async-start | bytes 7340032 | tf_op jit(solution)/shard_map/psum | solution.py:507
  450.8 14.6 %copy-start.97 = (f32[256]{0:T(256)S(1)}, f32[256]{0:T(256)}, u32[]{:S(2)}) copy-start(f32[256]{0:T(256)} %copy-done.96) | copy-start | bytes 3076
  450.8 14.6 %copy-start.104 = (f32[256]{0:T(256)S(1)}, f32[256]{0:T(256)}, u32[]{:S(2)}) copy-start(f32[256]{0:T(256)} %copy-done.102) | copy-start | bytes 3076
  450.9 14.7 %copy-start.73 = (s32[256,8]{0,1:T(8,128)S(1)}, s32[256,8]{0,1:T(8,128)}, u32[]{:S(2)}) copy-start(s32[256,8]{0,1:T(8,128)} %param.24) | copy-start | bytes 24580
  450.9 14.7 %copy-start.5 = (f32[256,1024]{1,0:T(8,128)S(1)}, f32[256,1024]{1,0:T(8,128)}, u32[]{:S(2)}) copy-start(f32[256,1024]{1,0:T(8,128)} %copy-done.4) | copy-start | bytes 3145732
  450.9 14.7 %copy-start.77 = (bf16[1024,16]{0,1:T(8,128)(2,1)S(1)}, bf16[1024,16]{0,1:T(8,128)(2,1)}, u32[]{:S(2)}) copy-start(bf16[1024,16]{0,1:T(8,128)(2,1)} %param.31) | copy-start | bytes 98308
  450.9 14.7 %copy-start.95 = (f32[1024]{0:T(1024)S(1)}, f32[1024]{0:T(1024)}, u32[]{:S(2)}) copy-start(f32[1024]{0:T(1024)} %param.30) | copy-start | bytes 12292
  450.9 15.5 %copy-start.113 = (f32[256]{0:T(256)S(1)}, f32[256]{0:T(256)}, u32[]{:S(2)}) copy-start(f32[256]{0:T(256)} %copy-done.112) | copy-start | bytes 3076
  450.9 15.5 %copy-start.44 = (bf16[256,1024]{1,0:T(8,128)(2,1)S(1)}, bf16[256,1024]{1,0:T(8,128)(2,1)}, u32[]{:S(2)}) copy-start(bf16[256,1024]{1,0:T(8,128)(2,1)} %param.43) | copy-start | bytes 1572868
  450.9 15.5 %copy-start.107 = (f32[256]{0:T(256)S(1)}, f32[256]{0:T(256)}, u32[]{:S(2)}) copy-start(f32[256]{0:T(256)} %get-tuple-element.132) | copy-start | bytes 3076
  450.9 15.5 %copy-start.109 = (f32[256]{0:T(256)S(1)}, f32[256]{0:T(256)}, u32[]{:S(2)}) copy-start(f32[256]{0:T(256)} %copy-done.108) | copy-start | bytes 3076
  479.4 16.0 %copy-start.25 = (bf16[8,64,2,256]{3,1,2,0:T(8,128)(2,1)S(1)}, bf16[8,64,2,256]{3,1,2,0:T(8,128)(2,1)}, u32[]{:S(2)}) copy-start(bf16[8,64,2,256]{3,1,2,0:T(8,128)(2,1)} %copy-done.24) | copy-start | bytes 1572868
  482.7 17.7 %copy-start.89 = (bf16[256,48]{0,1:T(8,128)(2,1)S(1)}, bf16[256,48]{0,1:T(8,128)(2,1)}, u32[]{:S(2)}) copy-start(bf16[256,48]{0,1:T(8,128)(2,1)} %copy-done.88) | copy-start | bytes 73732
  483.7 16.9 %copy-start.28 = (bf16[256,8,64]{0,2,1:T(8,128)(2,1)S(1)}, bf16[256,8,64]{0,2,1:T(8,128)(2,1)}, u32[]{:S(2)}) copy-start(bf16[256,8,64]{0,2,1:T(8,128)(2,1)} %copy-done.27) | copy-start | bytes 786436
  488.7 13.4 %copy-start.91 = (bf16[256,16]{0,1:T(8,128)(2,1)S(1)}, bf16[256,16]{0,1:T(8,128)(2,1)}, u32[]{:S(2)}) copy-start(bf16[256,16]{0,1:T(8,128)(2,1)} %copy-done.90) | copy-start | bytes 24580
  574.0 144.2 %copy-start.1 = (bf16[4,1024,256]{2,1,0:T(8,128)(2,1)S(1)}, bf16[4,1024,256]{2,1,0:T(8,128)(2,1)}, u32[]{:S(2)}) copy-start(bf16[4,1024,256]{2,1,0:T(8,128)(2,1)} %param.39) | copy-start | bytes 6291460
  (84 other events, 312.4 us)
Sparse Core Ops, SparseCore 0:
  391.4 172.0 all-reduce.10
  570.4 140.7 all-reduce.8
where the time goes:
time: 734 us; the launch traced here: 726 us
  waiting for transfers between devices  372 us (51%)
  matrix products  153 us (21%)
  local copies, waits for them, and re-layouts  118 us (16%)
  other arithmetic  37.7 us (5%)
  starting transfers between devices  26.8 us (4%)
  between operations  17.7 us (2%)
    psum x1, waiting for transfers between devices, on_device(): lax.psum((gathered_adapter_input, gathered_query_second, gathered_key_val...  136 us
    psum x1, waiting for transfers between devices, on_device(): lax.psum(expert_grads[1].astype(jnp.bfloat16), 'dp').astype(jnp.float32)  60.4 us
    all_to_all x1, waiting for transfers between devices, on_device(): lax.all_to_all(grad_local, 'expert', split_axis=1, concat_axis=0, tiled=T...  47.2 us
    all_to_all x1, waiting for transfers between devices, on_device(): lax.all_to_all(expert_result, 'expert', split_axis=1, concat_axis=0, tile...  45.9 us
    all_to_all x1, waiting for transfers between devices, on_device(): lax.all_to_all(grad_send, 'expert', split_axis=0, concat_axis=1, tiled=True)  45.8 us
    all_to_all x1, waiting for transfers between devices, on_device(): lax.all_to_all(send_rows, 'expert', split_axis=0, concat_axis=1, tiled=True)  37 us
    unnamed x260, local copies, waits for them, and re-layouts  18.8 us
    gather x5, local copies, waits for them, and re-layouts, on_device(): chosen = jnp.take_along_axis(logits, routes, axis=1)  17.2 us
  transfers between devices with their start and end apart: 7, of which 6 were waited for; matrix products, arithmetic and copies ran while one was open for 33% of the time, Pallas kernels for 0%

commit v1 on v0

v1 whole, which is shorter than its diff:
```python
import functools

import jax
import jax.numpy as jnp
from jax import lax
from jax.experimental import pallas as pl
from jax.experimental.pallas import tpu as pltpu
from jax.sharding import PartitionSpec as P

MODEL_WIDTH = 1024
QUERY_HEAD_COUNT = 16
KEY_VALUE_HEADS = 8
HEAD_WIDTH = 64
HIDDEN_UNITS = 512
TOP = 8
EXP_DEV = 4
ADAPTER_COUNT = 8
ADAPTER_RANK = 16
TOK_DEV = 256


norm_eps = 1e-06
rope_base = 10000.0


def rms_norm(value_rows, gain):
    factor = lax.rsqrt(jnp.mean(value_rows * value_rows, axis=-1, keepdims=True) + norm_eps)
    return value_rows * factor * gain


def rope_tables(row_count, head_dim):
    half_dim = head_dim // 2
    positions = jnp.arange(row_count, dtype=jnp.float32)
    inverse = rope_base ** (-2.0 * jnp.arange(half_dim, dtype=jnp.float32) / head_dim)
    angles = positions[:, None] * inverse[None, :]
    cosine_table = jnp.concatenate([jnp.cos(angles), jnp.cos(angles)], axis=1)
    sine_table = jnp.concatenate([jnp.sin(angles), jnp.sin(angles)], axis=1)
    return (cosine_table, sine_table)


def rotate(value_rows, cosine_table, sine_table, head_dim):
    row_count = value_rows.shape[0]
    head_values = value_rows.reshape(row_count, -1, head_dim)
    half_dim = head_dim // 2
    turned = jnp.concatenate([-head_values[..., half_dim:], head_values[..., :half_dim]], axis=-1)
    result = head_values * cosine_table[:, None, :] + turned * sine_table[:, None, :]
    return result.reshape(row_count, -1)


def rotate_back(grads, cosine_table, sine_table, head_dim):
    unused_value, pullback = jax.vjp(
        lambda value_rows: rotate(value_rows, cosine_table, sine_table, head_dim),
        jnp.zeros_like(grads),
    )
    return pullback(grads)[0]


def swap(values, axis, bit):
    size = lax.axis_size(axis)
    return lax.ppermute(values, axis, [(i, i ^ (1 << bit)) for i in range(size)])


def axis_bits(axis):
    return lax.axis_size(axis).bit_length() - 1


def gather_blocks(values):
    blocks = [values]
    for bit in reversed(range(axis_bits("expert"))):
        blocks = blocks + [swap(block, "expert", bit) for block in blocks]
    return jnp.concatenate(blocks, axis=0)


def scatter_blocks(partial):
    for bit in range(axis_bits("expert")):
        half = partial.shape[0] // 2
        got = swap(partial[half:], "expert", bit)
        total = partial[:half].astype(F32) + got.astype(F32)
        partial = total if half == TOK_DEV else total.astype(BF)
    return partial


def cube_sum(values, stages):
    done = []
    for axis, bit in stages:
        rows, width = values.shape
        if rows % 16 == 0:
            side = (lax.axis_index(axis) >> bit) & 1
            halves = values.reshape(2, rows // 2, width)
            keep = lax.dynamic_index_in_dim(halves, side, 0, keepdims=False)
            send = lax.dynamic_index_in_dim(halves, 1 - side, 0, keepdims=False)
            done.append((axis, bit, side))
        else:
            keep = send = values
        got = swap(send, axis, bit)
        values = (keep.astype(F32) + got.astype(F32)).astype(BF)
    for axis, bit, side in reversed(done):
        got = swap(values, axis, bit)
        low = jnp.where(side == 0, values, got)
        high = jnp.where(side == 0, got, values)
        values = jnp.concatenate([low, high], axis=0)
    return values


F32=jnp.float32; BF=jnp.bfloat16

def nt(a,b): return lax.dot_general(a,b,(((1,),(1,)),((),())),preferred_element_type=F32)
def nn(a,b): return lax.dot_general(a,b,(((1,),(0,)),((),())),preferred_element_type=F32)
def tn(a,b): return lax.dot_general(a,b,(((0,),(0,)),((),())),preferred_element_type=F32)

def expert_body(eid_ref, xm_ref, g_ref, win_ref, wdn_ref, ain_ref, bin_ref, adn_ref, bdn_ref, *rest, first, last, row_blocks, experts):
    if first:
        f_in=b_in_=c_in=None; rest=rest
    else:
        f_in,b_in_,c_in=rest[:3]; rest=rest[3:]
    if last:
        wr_ref=rest[0]; rest=rest[1:]
        f_out,b_out,pack_ref=rest[:3]; rest=rest[3:]
    else:
        f_out,b_out,c_out,pack_ref=rest[:4]; rest=rest[4:]
    acc_a,acc_bi,acc_ad,acc_bd=rest
    step=pl.program_id(0)
    eid=eid_ref[0]
    rows=xm_ref.shape[0]
    x=xm_ref[:, :1024]
    meta=xm_ref[:, 1024:1152].astype(F32)
    lane=lax.broadcasted_iota(jnp.int32,(rows,128),1)
    adapter=meta[:, 96:97].astype(jnp.int32)
    mask=(lane//16==adapter)
    low=pltpu.roll(meta,96,1)
    gates=jnp.where(lane<experts, meta+low, 0.0)
    here=lane==eid
    g_e=jnp.sum(jnp.where(here,gates,0.0),axis=1,keepdims=True)
    grad=g_ref[...]
    lr=nn(x,ain_ref[0])
    lrg=jnp.where(mask,lr[:, :128],0.0).astype(BF)
    lru=jnp.where(mask,lr[:,128:],0.0).astype(BF)
    gate=nn(x,win_ref[0,:, :512])+nn(lrg,bin_ref[0,0])
    up=nn(x,win_ref[0,:,512:])+nn(lru,bin_ref[0,1])
    sig=1.0/(1.0+jnp.exp(-gate))
    silu=gate*sig
    act=(silu*up).astype(BF)
    dr=jnp.where(mask,nn(act,adn_ref[0]),0.0).astype(BF)
    gradf=grad.astype(F32)
    eo=nn(act,wdn_ref[0])+nn(dr,bdn_ref[0])
    gg=jnp.sum(eo*gradf,axis=1,keepdims=True)
    fo=g_e*eo
    if not first: fo=fo+f_in[...].astype(F32)
    f_out[...]=fo.astype(f_out.dtype)
    gs=(g_e*gradf).astype(BF)
    gdr=jnp.where(mask,nt(gs,bdn_ref[0]),0.0).astype(BF)
    ga=(nt(gs,wdn_ref[0])+nt(gdr,adn_ref[0]))
    gate_grad=(ga*up*sig*(1.0+gate*(1.0-sig))).astype(BF)
    up_grad=(ga*silu).astype(BF)
    glg=jnp.where(mask,nt(gate_grad,bin_ref[0,0]),0.0).astype(BF)
    glu=jnp.where(mask,nt(up_grad,bin_ref[0,1]),0.0).astype(BF)
    grow=nt(gate_grad,win_ref[0,:, :512])+nt(up_grad,win_ref[0,:,512:])+nt(glg,ain_ref[0,:, :128])+nt(glu,ain_ref[0,:,128:])
    c=(g_e*gg)*(jnp.where(here,1.0,0.0)-gates)
    if not first:
        grow=grow+b_in_[...].astype(F32); c=c+c_in[...]
    if last:
        grow=grow+nt(c.astype(BF),wr_ref[...])
    else:
        c_out[...]=c
    b_out[...]=grow.astype(b_out.dtype)
    ga_t=jnp.concatenate([tn(glg,x),tn(glu,x)],axis=0)
    gbi=jnp.concatenate([tn(lrg,gate_grad),tn(lru,up_grad)],axis=1)
    gad=tn(gdr,act)
    gbd=tn(dr,gs)
    @pl.when(step==0)
    def _():
        acc_a[...]=ga_t; acc_bi[...]=gbi; acc_ad[...]=gad; acc_bd[...]=gbd
    @pl.when(step>0)
    def _():
        acc_a[...]+=ga_t; acc_bi[...]+=gbi; acc_ad[...]+=gad; acc_bd[...]+=gbd
    @pl.when(step==row_blocks-1)
    def _():
        pack_ref[0:256,:]=acc_a[...].astype(BF)
        pack_ref[256:384,:]=acc_bi[...].astype(BF)
        pack_ref[384:512,:]=acc_bd[...].astype(BF)
        pack_ref[512:576,0:512]=acc_ad[0:64,:].astype(BF)
        pack_ref[512:576,512:1024]=acc_ad[64:128,:].astype(BF)

def expert_call(e, eid, xm, grad, win,wdn,ain,bin_,adn,bdn, prev, wr, experts, rows=256, acc_dtype=F32):
    total=xm.shape[0]; n=total//rows
    first=prev is None; last=wr is not None
    one=pl.Buffered(1)
    rb=lambda w: pl.BlockSpec((rows,w),lambda i,*_:(i,0))
    wspec=lambda *s: pl.BlockSpec((1,)+s,lambda i,*_:(e,)+(0,)*len(s),pipeline_mode=one)
    in_specs=[rb(1152),rb(1024),wspec(1024,1024),wspec(512,1024),wspec(1024,256),wspec(2,128,512),wspec(512,128),wspec(128,1024)]
    args=[xm,grad,win,wdn,ain,bin_,adn,bdn]
    if not first:
        in_specs+= [rb(1024),rb(1024),rb(128)]
        args+=list(prev)
    if last:
        in_specs.append(pl.BlockSpec((1024,128),lambda i,*_:(0,0),pipeline_mode=one)); args.append(wr)
    S=jax.ShapeDtypeStruct
    od=BF if last else acc_dtype
    outs=[S((total,1024),od),S((total,1024),od)]; ospecs=[rb(1024),rb(1024)]
    if not last:
        outs.append(S((total,128),F32)); ospecs.append(rb(128))
    outs.append(S((576,1024),BF)); ospecs.append(pl.BlockSpec((576,1024),lambda i,*_:(0,0)))
    return pl.pallas_call(
        functools.partial(expert_body,first=first,last=last,row_blocks=n,experts=experts),
        out_shape=outs,
        grid_spec=pltpu.PrefetchScalarGridSpec(num_scalar_prefetch=1,grid=(n,),in_specs=in_specs,out_specs=ospecs,
            scratch_shapes=[pltpu.VMEM((256,1024),F32),pltpu.VMEM((128,1024),F32),pltpu.VMEM((128,512),F32),pltpu.VMEM((128,1024),F32)]),
        compiler_params=pltpu.CompilerParams(dimension_semantics=("arbitrary",),vmem_limit_bytes=60*1024*1024),
        cost_estimate=pl.CostEstimate(flops=total*9_800_000,bytes_accessed=20_000_000,transcendentals=total*512),
        name="expert_step",
    )(eid,*args)


def on_device(
    inputs,
    lengths,
    routes,
    adapter_of_sequence,
    first_norm_gain,
    query_weight,
    key_value_weight,
    output_weight,
    second_norm_gain,
    router_weight,
    expert_input_weight,
    expert_down_weight,
    attention_first_factors,
    query_second_factors,
    key_value_second_factors,
    output_first_factors,
    output_second_factors,
    expert_input_first_factors,
    expert_input_second_factors,
    expert_down_first_factors,
    expert_down_second_factors,
    output_gradient,
):
    experts = EXP_DEV * lax.axis_size("expert")
    rank_total_width = ADAPTER_COUNT * ADAPTER_RANK
    key_value_width = KEY_VALUE_HEADS * HEAD_WIDTH
    groups = QUERY_HEAD_COUNT // KEY_VALUE_HEADS
    score_scale = HEAD_WIDTH ** (-0.5)
    block_rows = min(512, TOK_DEV)
    length = lengths[0]
    adapter = adapter_of_sequence[0]
    start_offset = adapter * ADAPTER_RANK
    positions = jnp.arange(TOK_DEV, dtype=jnp.int32)
    live = (positions < length).astype(jnp.float32)[:, None]
    source = inputs.astype(jnp.float32)
    normalized_input = rms_norm(source, first_norm_gain).astype(jnp.bfloat16)
    adapter_input = jnp.concatenate(
        [
            lax.dynamic_slice_in_dim(
                attention_first_factors,
                portion_index * rank_total_width + start_offset,
                ADAPTER_RANK,
                1,
            )
            for portion_index in range(3)
        ],
        axis=1,
    )
    query_second_factor = lax.dynamic_slice_in_dim(
        query_second_factors, start_offset, ADAPTER_RANK, 0
    )
    key_second_factor = lax.dynamic_slice_in_dim(
        key_value_second_factors[0], start_offset, ADAPTER_RANK, 0
    )
    value_second_factor = lax.dynamic_slice_in_dim(
        key_value_second_factors[1], start_offset, ADAPTER_RANK, 0
    )
    output_first_factor = lax.dynamic_slice_in_dim(
        output_first_factors, start_offset, ADAPTER_RANK, 1
    )
    output_second_factor = lax.dynamic_slice_in_dim(
        output_second_factors, start_offset, ADAPTER_RANK, 0
    )
    rank_projection = jnp.dot(
        normalized_input, adapter_input, preferred_element_type=jnp.float32
    ).astype(jnp.bfloat16)
    rank_query = rank_projection[:, :ADAPTER_RANK]
    rank_key = rank_projection[:, ADAPTER_RANK : 2 * ADAPTER_RANK]
    rank_value = rank_projection[:, 2 * ADAPTER_RANK :]
    query_preactivation = jnp.dot(
        normalized_input, query_weight, preferred_element_type=jnp.float32
    ) + jnp.dot(rank_query, query_second_factor, preferred_element_type=jnp.float32)
    key_value_base = jnp.dot(normalized_input, key_value_weight, preferred_element_type=jnp.float32)
    key_preactivation = key_value_base[:, :key_value_width] + jnp.dot(
        rank_key, key_second_factor, preferred_element_type=jnp.float32
    )
    value_rows = (
        key_value_base[:, key_value_width:]
        + jnp.dot(rank_value, value_second_factor, preferred_element_type=jnp.float32)
    ).astype(jnp.bfloat16)
    cosine_table, sine_table = rope_tables(TOK_DEV, HEAD_WIDTH)
    queries = rotate(query_preactivation, cosine_table, sine_table, HEAD_WIDTH).astype(jnp.bfloat16)
    key_rows = rotate(key_preactivation, cosine_table, sine_table, HEAD_WIDTH).astype(jnp.bfloat16)
    query_heads = queries.reshape(TOK_DEV, KEY_VALUE_HEADS, groups, HEAD_WIDTH)
    key_heads = key_rows.reshape(TOK_DEV, KEY_VALUE_HEADS, HEAD_WIDTH)
    value_heads = value_rows.reshape(TOK_DEV, KEY_VALUE_HEADS, HEAD_WIDTH)

    def block_scores(row_start):
        raw_scores = (
            jnp.einsum("qjgd,kjd->jgqk", query_heads, key_heads, preferred_element_type=jnp.float32)
            * score_scale
        )
        block_positions = row_start + jnp.arange(block_rows, dtype=jnp.int32)
        allowed = (positions[None, :] <= block_positions[:, None]) & (positions[None, :] < length)
        return (query_heads, jnp.where(allowed, raw_scores, -1e30))

    row_start = 0
    query_block, masked = block_scores(row_start)
    top_score = jnp.max(masked, axis=-1, keepdims=True)
    exponent = jnp.exp(masked - top_score)
    row_total = jnp.sum(exponent, axis=-1, keepdims=True)
    probs_block = (exponent / row_total).astype(jnp.bfloat16)
    log_totals = [top_score + jnp.log(row_total)]
    attended_parts = jnp.einsum(
        "jgqk,kjd->qjgd", probs_block, value_heads, preferred_element_type=jnp.float32
    ).astype(jnp.bfloat16)
    attention_result = attended_parts.reshape(TOK_DEV, QUERY_HEAD_COUNT * HEAD_WIDTH)
    output_rank_values = jnp.dot(
        attention_result, output_first_factor, preferred_element_type=jnp.float32
    ).astype(jnp.bfloat16)
    hidden = (
        source
        + jnp.dot(attention_result, output_weight, preferred_element_type=jnp.float32)
        + jnp.dot(output_rank_values, output_second_factor, preferred_element_type=jnp.float32)
    )
    normed2 = rms_norm(hidden, second_norm_gain).astype(jnp.bfloat16)
    logits = jnp.dot(normed2, router_weight, preferred_element_type=jnp.float32)
    expert_numbers = jnp.arange(experts, dtype=jnp.int32)
    selected = jnp.any(routes[:, :, None] == expert_numbers[None, None, :], axis=1)
    top_logit = jnp.max(jnp.where(selected, logits, -1e30), axis=1, keepdims=True)
    chosen_exp = jnp.where(selected, jnp.exp(jnp.minimum(logits - top_logit, 0.0)), 0.0)
    gates = chosen_exp / jnp.sum(chosen_exp, axis=1, keepdims=True) * live
    gate_high = gates.astype(jnp.bfloat16)
    gate_low = (gates - gate_high.astype(jnp.float32)).astype(jnp.bfloat16)
    spare = jnp.zeros((TOK_DEV, 32 - experts), jnp.bfloat16)
    adapter_lane = jnp.full((TOK_DEV, 32), adapter, jnp.bfloat16)
    payload = jnp.concatenate(
        [
            normed2,
            gate_high,
            spare,
            gate_low,
            spare,
            jnp.zeros((TOK_DEV, 32), jnp.bfloat16),
            adapter_lane,
        ],
        axis=1,
    )
    grad_output = output_gradient.astype(jnp.float32) * live
    all_grads = gather_blocks(output_gradient)
    all_rows = gather_blocks(payload)
    router_wide = jnp.concatenate(
        [router_weight, jnp.zeros((MODEL_WIDTH, 128 - experts), jnp.bfloat16)], axis=1
    )
    carried = None
    packs = []
    first_expert = EXP_DEV * lax.axis_index("expert")
    for local in range(EXP_DEV):
        results = expert_call(
            local,
            (first_expert + local)[None],
            all_rows,
            all_grads,
            expert_input_weight,
            expert_down_weight,
            expert_input_first_factors,
            expert_input_second_factors,
            expert_down_first_factors,
            expert_down_second_factors,
            carried,
            router_wide if local == EXP_DEV - 1 else None,
            experts,
        )
        packs.append(results[-1])
        carried = results[:-1]
    mixture_part, row_part = carried
    grad_normed2 = scatter_blocks(row_part)
    mixture = hidden + scatter_blocks(mixture_part)
    output = (live * mixture).astype(jnp.bfloat16)
    dp_stages = [("dp", bit) for bit in range(axis_bits("dp"))]
    packs = [cube_sum(pack, dp_stages) for pack in packs]
    stacked = jnp.stack(packs).astype(jnp.float32)
    summed_experts = (
        jnp.swapaxes(stacked[:, :256], 1, 2),
        jnp.stack(
            [stacked[:, 256:384, :HIDDEN_UNITS], stacked[:, 256:384, HIDDEN_UNITS:]], axis=1
        ),
        jnp.swapaxes(
            jnp.concatenate(
                [stacked[:, 512:, :HIDDEN_UNITS], stacked[:, 512:, HIDDEN_UNITS:]], axis=1
            ),
            1,
            2,
        ),
        stacked[:, 384:512],
    )
    unused_hidden, norm2_back = jax.vjp(
        lambda values_in: rms_norm(values_in, second_norm_gain), hidden
    )
    grad_hidden = grad_output + norm2_back(grad_normed2)[0]
    grad_branch = grad_hidden.astype(jnp.bfloat16)
    grad_b_out = jnp.dot(output_rank_values.T, grad_branch, preferred_element_type=jnp.float32)
    grad_out_rank = jnp.dot(
        grad_branch, output_second_factor.T, preferred_element_type=jnp.float32
    ).astype(jnp.bfloat16)
    grad_a_out = jnp.dot(grad_out_rank.T, attention_result, preferred_element_type=jnp.float32)
    grad_attended = jnp.dot(grad_branch, output_weight.T, preferred_element_type=jnp.float32)
    grad_attended = (
        grad_attended
        + jnp.dot(grad_out_rank, output_first_factor.T, preferred_element_type=jnp.float32)
    ).astype(jnp.bfloat16)
    grad_heads = grad_attended.reshape(TOK_DEV, KEY_VALUE_HEADS, groups, HEAD_WIDTH)
    grad_keys = jnp.zeros((TOK_DEV, KEY_VALUE_HEADS, HEAD_WIDTH), jnp.float32)
    grad_values = jnp.zeros((TOK_DEV, KEY_VALUE_HEADS, HEAD_WIDTH), jnp.float32)
    query_parts = []
    for block_index, row_start in enumerate(range(0, TOK_DEV, block_rows)):
        query_block, masked = block_scores(row_start)
        probs_exact = jnp.exp(masked - log_totals[block_index])
        probs_block = probs_exact.astype(jnp.bfloat16)
        grad_values = jnp.einsum(
            "jgqk,qjgd->kjd", probs_block, grad_heads, preferred_element_type=jnp.float32
        )
        grad_probs = jnp.einsum(
            "qjgd,kjd->jgqk", grad_heads, value_heads, preferred_element_type=jnp.float32
        ).astype(jnp.bfloat16)
        row_inner = jnp.sum(grad_probs * probs_exact, axis=-1, keepdims=True)
        grad_scores = (probs_exact * (grad_probs - row_inner)).astype(jnp.bfloat16)
        query_parts.append(
            jnp.einsum("jgqk,kjd->qjgd", grad_scores, key_heads, preferred_element_type=jnp.float32)
            * score_scale
        )
        grad_keys = (
            jnp.einsum(
                "jgqk,qjgd->kjd", grad_scores, query_block, preferred_element_type=jnp.float32
            )
            * score_scale
        )
    grad_query = query_parts[0].reshape(TOK_DEV, QUERY_HEAD_COUNT * HEAD_WIDTH)
    grad_query_pre = rotate_back(grad_query, cosine_table, sine_table, HEAD_WIDTH).astype(
        jnp.bfloat16
    )
    grad_key_pre = rotate_back(
        grad_keys.reshape(TOK_DEV, key_value_width), cosine_table, sine_table, HEAD_WIDTH
    ).astype(jnp.bfloat16)
    grad_value = grad_values.reshape(TOK_DEV, key_value_width).astype(jnp.bfloat16)
    grad_b_query = jnp.dot(rank_query.T, grad_query_pre, preferred_element_type=jnp.float32)
    grad_b_key = jnp.dot(rank_key.T, grad_key_pre, preferred_element_type=jnp.float32)
    grad_b_value = jnp.dot(rank_value.T, grad_value, preferred_element_type=jnp.float32)
    gradient_rank_values = jnp.concatenate(
        [
            jnp.dot(grad_query_pre, query_second_factor.T, preferred_element_type=jnp.float32),
            jnp.dot(grad_key_pre, key_second_factor.T, preferred_element_type=jnp.float32),
            jnp.dot(grad_value, value_second_factor.T, preferred_element_type=jnp.float32),
        ],
        axis=1,
    ).astype(jnp.bfloat16)
    gradient_adapter_input = jnp.dot(
        gradient_rank_values.T, normalized_input, preferred_element_type=jnp.float32
    )
    gradient_of_normed = jnp.dot(grad_query_pre, query_weight.T, preferred_element_type=jnp.float32)
    gradient_of_normed = gradient_of_normed + jnp.dot(
        jnp.concatenate([grad_key_pre, grad_value], axis=1),
        key_value_weight.T,
        preferred_element_type=jnp.float32,
    )
    gradient_of_normed = gradient_of_normed + jnp.dot(
        gradient_rank_values, adapter_input.T, preferred_element_type=jnp.float32
    )
    unused_source, norm1_back = jax.vjp(
        lambda values_in: rms_norm(values_in, first_norm_gain), source
    )
    grad_input = grad_hidden + norm1_back(gradient_of_normed)[0]
    compact = jnp.concatenate(
        [
            gradient_adapter_input,
            grad_b_query,
            jnp.concatenate([grad_b_key, grad_b_value], axis=1),
            grad_a_out,
            grad_b_out,
        ],
        axis=0,
    ).reshape(7, 1, ADAPTER_RANK, MODEL_WIDTH)
    owned = (jnp.arange(ADAPTER_COUNT, dtype=jnp.int32) == adapter)[None, :, None, None]
    spread = jnp.where(owned, compact, 0.0).astype(jnp.bfloat16)
    stages = [("expert", bit) for bit in range(axis_bits("expert"))] + dp_stages
    summed = cube_sum(spread.reshape(7 * rank_total_width, MODEL_WIDTH), stages).astype(jnp.float32)
    return (
        output,
        grad_input,
        summed[:384].T,
        summed[384:512],
        jnp.stack([summed[512:640, :key_value_width], summed[512:640, key_value_width:]]),
        summed[640:768].T,
        summed[768:896],
        *summed_experts,
    )


def solution(mesh):
    placed = (
        P(("dp", "expert"), None),
        P(("dp", "expert")),
        P(("dp", "expert"), None),
        P(("dp", "expert")),
        P(),
        P(),
        P(),
        P(),
        P(),
        P(),
        P("expert", None, None),
        P("expert", None, None),
        P(),
        P(),
        P(),
        P(),
        P(),
        P("expert", None, None),
        P("expert", None, None, None),
        P("expert", None, None),
        P("expert", None, None),
        P(("dp", "expert"), None),
    )
    return jax.shard_map(
        on_device,
        mesh=mesh,
        in_specs=placed,
        out_specs=(
            P(("dp", "expert"), None),
            P(("dp", "expert"), None),
            P(),
            P(),
            P(),
            P(),
            P(),
            P("expert", None, None),
            P("expert", None, None, None),
            P("expert", None, None),
            P("expert", None, None),
        ),
        check_vma=False,
    )
```

time: 734 us -> 445 us (0.61)
  waiting for transfers between devices: 372 us -> 156 us
  matrix products: 153 us -> 28.5 us
  Pallas kernels: 0 us -> 84.9 us
  local copies, waits for them, and re-layouts: 118 us -> 66.8 us
  starting transfers between devices: 26.8 us -> 49 us
  between operations: 17.7 us -> 3.82 us
  other arithmetic: 37.7 us -> 47.9 us
    psum x2 -> x0, waiting for transfers between devices: 196 us -> none  [the longest x1 136 us: on_device(): lax.psum((gathered_adapter_input, gathered_query_second, gathered_key_val...]
    all_to_all x5 -> x0, waiting for transfers between devices: 176 us -> none  [the longest x1 47.2 us: on_device(): lax.all_to_all(grad_local, 'expert', split_axis=1, concat_axis=0, tiled=T...]
    ppermute x0 -> x43, waiting for transfers between devices: none -> 156 us  [swap(): return lax.ppermute(values, axis, [(i, i ^ 1 << bit) for i in range(size)])]
    dot_general x27 -> x2, matrix products: 124 us -> 0.57 us  [the longest x1 0.34 us: on_device(): jnp.dot(gradient_rank_values.T, normalized_input, preferred_element_type=...]
    pallas_call x0 -> x4, Pallas kernels: none -> 84.9 us  [expert_call(): pl.pallas_call(functools.partial(expert_body, first=first, last=last, row...]
    ppermute x0 -> x43, starting transfers between devices: none -> 49 us  [swap(): return lax.ppermute(values, axis, [(i, i ^ 1 << bit) for i in range(size)])]
    all_to_all x5 -> x0, starting transfers between devices: 26.3 us -> none  [the longest x1 5.76 us: on_device(): lax.all_to_all(grad_local, 'expert', split_axis=1, concat_axis=0, tiled=T...]
    convert_element_type x2 -> x0, local copies, waits for them, and re-layouts: 20.6 us -> none  [the longest x1 10.3 us: expert_forward(): result = (result + jnp.einsum('emr,erd->emd', down_rank_values, b_down, p...]
  transfers between devices with their start and end apart: 7 -> 43, of which waited for: 6 -> 25; matrix products, arithmetic and copies ran while one was open for 33% -> 15% of each run, Pallas kernels for 0% -> 0%
where the time goes in v1:
time: 445 us; the launch traced here: 437 us
  waiting for transfers between devices  156 us (35%)
  Pallas kernels  84.9 us (19%)
  local copies, waits for them, and re-layouts  66.8 us (15%)
  starting transfers between devices  49 us (11%)
  other arithmetic  47.9 us (11%)
  matrix products  28.5 us (6%)
    ppermute x43, waiting for transfers between devices, swap(): return lax.ppermute(values, axis, [(i, i ^ 1 << bit) for i in range(size)])  156 us
    pallas_call x4, Pallas kernels, expert_call(): pl.pallas_call(functools.partial(expert_body, first=first, last=last, row...  84.9 us
    ppermute x43, starting transfers between devices, swap(): return lax.ppermute(values, axis, [(i, i ^ 1 << bit) for i in range(size)])  49 us
    unnamed x170, local copies, waits for them, and re-layouts  30 us
  transfers between devices with their start and end apart: 43, of which 25 were waited for; matrix products, arithmetic and copies ran while one was open for 15% of the time, Pallas kernels for 0%

profile of v1, /device:TPU:0, one launch (start us, length us, event | category | flops | bytes accessed | tf_op | source)
XLA Modules:
  0.0 436.8 jit_solution(16100737671616054828)
XLA Ops:
  6.8 2.3 fusion.99
  25.9 2.4 fusion.96
  30.4 2.5 copy.143
  35.3 2.6 copy.144
  38.9 2.5 copy.142
  41.5 2.9 add_convert_fusion.2
  56.4 2.4 concatenate.96
  58.8 3.0 collective-permute-start
  61.8 24.8 %collective-permute-done.3 = bf16[256,1024]{1,0:T(8,128)(2,1)} collective-permute-done((bf16[256,1024]{1,0:T(8,128)(2,1)}, bf16[256,1024]{1,0:T(8,128)(2,1)}, u32[]{:S(2)}, u32[]{:S(2)}) %collective-permute-start.3) | collective-permute-done | bytes 524320 | tf_op jit(solution)/shard_map/ppermute | solution.py:60
  96.5 3.0 pad_maximum_fusion.xm_ref
  99.5 20.2 %expert_step.4 = (f32[1024,1024]{1,0:T(8,128)}, f32[1024,1024]{1,0:T(8,128)}, f32[1024,128]{1,0:T(8,128)}, bf16[576,1024]{1,0:T(8,128)(2,1)}) custom-call(s32[1]{0:T(128)} %bitcast.24.eid_ref, bf16[1024,1152]{1,0:T(8,128)(2,1)} %pad_maximum_fusion.xm_ref, bf16[1024,1024]{1,0:T(8,128)(2,1)} %constant_dynamic-update-slice_fusion.g_ref, ...), custom_call_target="tpu_custom_call" | custom-call | flops 10035200000 | bytes 20000000 | tf_op jit(solution)/shard_map/expert_step/pallas_call | solution.py:203
  119.7 21.5 %expert_step.5 = (f32[1024,1024]{1,0:T(8,128)}, f32[1024,1024]{1,0:T(8,128)}, f32[1024,128]{1,0:T(8,128)}, bf16[576,1024]{1,0:T(8,128)(2,1)}) custom-call(s32[1]{0:T(128)} %bitcast.23.eid_ref, bf16[1024,1152]{1,0:T(8,128)(2,1)} %pad_maximum_fusion.xm_ref, bf16[1024,1024]{1,0:T(8,128)(2,1)} %constant_dynamic-update-slice_fusion.g_ref, ...), custom_call_target="tpu_custom_call" | custom-call | flops 10035200000 | bytes 20000000 | tf_op jit(solution)/shard_map/expert_step/pallas_call | solution.py:203
  141.1 21.4 %expert_step.6 = (f32[1024,1024]{1,0:T(8,128)}, f32[1024,1024]{1,0:T(8,128)}, f32[1024,128]{1,0:T(8,128)}, bf16[576,1024]{1,0:T(8,128)(2,1)}) custom-call(s32[1]{0:T(128)} %bitcast.22.eid_ref, bf16[1024,1152]{1,0:T(8,128)(2,1)} %pad_maximum_fusion.xm_ref, bf16[1024,1024]{1,0:T(8,128)(2,1)} %constant_dynamic-update-slice_fusion.g_ref, ...), custom_call_target="tpu_custom_call" | custom-call | flops 10035200000 | bytes 20000000 | tf_op jit(solution)/shard_map/expert_step/pallas_call | solution.py:203
  162.6 21.9 %expert_step.7 = (bf16[1024,1024]{1,0:T(8,128)(2,1)}, bf16[1024,1024]{1,0:T(8,128)(2,1)}, bf16[576,1024]{1,0:T(8,128)(2,1)}) custom-call(s32[1]{0:T(128)} %bitcast.21.eid_ref, bf16[1024,1152]{1,0:T(8,128)(2,1)} %pad_maximum_fusion.xm_ref, bf16[1024,1024]{1,0:T(8,128)(2,1)} %constant_dynamic-update-slice_fusion.g_ref, bf16[4,1024,1024]{2,1,0:T(8,128)(2,1)} %win_ref.7, ...), custom_call_target="tpu_custom_call" | custom-call | flops 10035200000 | bytes 20000000 | tf_op jit(solution)/shard_map/expert_step/pallas_call | solution.py:203
  192.0 10.0 %collective-permute-done.37 = bf16[288,1024]{1,0:T(8,128)(2,1)S(1)} collective-permute-done((bf16[288,1024]{1,0:T(8,128)(2,1)S(1)}, bf16[288,1024]{1,0:T(8,128)(2,1)S(1)}, u32[]{:S(2)}, u32[]{:S(2)}) %collective-permute-start.37) | collective-permute-done | bytes 589856 | tf_op jit(solution)/shard_map/ppermute | solution.py:60
  204.0 10.6 %collective-permute-done.31 = bf16[288,1024]{1,0:T(8,128)(2,1)S(1)} collective-permute-done((bf16[288,1024]{1,0:T(8,128)(2,1)S(1)}, bf16[288,1024]{1,0:T(8,128)(2,1)S(1)}, u32[]{:S(2)}, u32[]{:S(2)}) %collective-permute-start.31) | collective-permute-done | bytes 589856 | tf_op jit(solution)/shard_map/ppermute | solution.py:60
  216.7 10.6 %collective-permute-done.25 = bf16[288,1024]{1,0:T(8,128)(2,1)S(1)} collective-permute-done((bf16[288,1024]{1,0:T(8,128)(2,1)S(1)}, bf16[288,1024]{1,0:T(8,128)(2,1)S(1)}, u32[]{:S(2)}, u32[]{:S(2)}) %collective-permute-start.25) | collective-permute-done | bytes 589856 | tf_op jit(solution)/shard_map/ppermute | solution.py:60
  229.3 10.1 %collective-permute-done.19 = bf16[288,1024]{1,0:T(8,128)(2,1)S(1)} collective-permute-done((bf16[288,1024]{1,0:T(8,128)(2,1)S(1)}, bf16[288,1024]{1,0:T(8,128)(2,1)S(1)}, u32[]{:S(2)}, u32[]{:S(2)}) %collective-permute-start.19) | collective-permute-done | bytes 589856 | tf_op jit(solution)/shard_map/ppermute | solution.py:60
  242.0 2.9 collective-permute-start.39
  244.9 7.6 %collective-permute-done.26 = bf16[144,1024]{1,0:T(8,128)(2,1)S(1)} collective-permute-done((bf16[144,1024]{1,0:T(8,128)(2,1)S(1)}, bf16[144,1024]{1,0:T(8,128)(2,1)S(1)}, u32[]{:S(2)}, u32[]{:S(2)}) %collective-permute-start.26) | collective-permute-done | bytes 294944 | tf_op jit(solution)/shard_map/ppermute | solution.py:60
  254.5 5.2 %collective-permute-done.20 = bf16[144,1024]{1,0:T(8,128)(2,1)S(1)} collective-permute-done((bf16[144,1024]{1,0:T(8,128)(2,1)S(1)}, bf16[144,1024]{1,0:T(8,128)(2,1)S(1)}, u32[]{:S(2)}, u32[]{:S(2)}) %collective-permute-start.20) | collective-permute-done | bytes 294944 | tf_op jit(solution)/shard_map/ppermute | solution.py:60
  260.6 2.2 collective-permute-start.21
  262.9 8.5 %collective-permute-done.33 = bf16[72,1024]{1,0:T(8,128)(2,1)S(1)} collective-permute-done((bf16[72,1024]{1,0:T(8,128)(2,1)S(1)}, bf16[72,1024]{1,0:T(8,128)(2,1)S(1)}, u32[]{:S(2)}, u32[]{:S(2)}) %collective-permute-start.33) | collective-permute-done | bytes 147488 | tf_op jit(solution)/shard_map/ppermute | solution.py:60
  271.4 4.7 %collective-permute-done.27 = bf16[72,1024]{1,0:T(8,128)(2,1)S(1)} collective-permute-done((bf16[72,1024]{1,0:T(8,128)(2,1)S(1)}, bf16[72,1024]{1,0:T(8,128)(2,1)S(1)}, u32[]{:S(2)}, u32[]{:S(2)}) %collective-permute-start.27) | collective-permute-done | bytes 147488 | tf_op jit(solution)/shard_map/ppermute | solution.py:60
  276.1 6.3 %collective-permute-done.21 = bf16[72,1024]{1,0:T(8,128)(2,1)S(1)} collective-permute-done((bf16[72,1024]{1,0:T(8,128)(2,1)S(1)}, bf16[72,1024]{1,0:T(8,128)(2,1)S(1)}, u32[]{:S(2)}, u32[]{:S(2)}) %collective-permute-start.21) | collective-permute-done | bytes 147488 | tf_op jit(solution)/shard_map/ppermute | solution.py:60
  282.5 3.0 collective-permute-start.22
  288.2 2.1 collective-permute-done.40
  293.5 3.3 collective-permute-start.41
  296.8 2.9 collective-permute-done.28
  299.7 2.3 collective-permute-done.22
  302.1 5.3 %collective-permute-done.41 = bf16[144,1024]{1,0:T(8,128)(2,1)S(1)} collective-permute-done((bf16[144,1024]{1,0:T(8,128)(2,1)S(1)}, bf16[144,1024]{1,0:T(8,128)(2,1)S(1)}, u32[]{:S(2)}, u32[]{:S(2)}) %collective-permute-start.41) | collective-permute-done | bytes 294944 | tf_op jit(solution)/shard_map/ppermute | solution.py:60
  308.5 5.2 %collective-permute-done.35 = bf16[144,1024]{1,0:T(8,128)(2,1)S(1)} collective-permute-done((bf16[144,1024]{1,0:T(8,128)(2,1)S(1)}, bf16[144,1024]{1,0:T(8,128)(2,1)S(1)}, u32[]{:S(2)}, u32[]{:S(2)}) %collective-permute-start.35) | collective-permute-done | bytes 294944 | tf_op jit(solution)/shard_map/ppermute | solution.py:60
  316.5 3.6 collective-permute-done.29
  328.9 2.6 fusion.24
  336.5 3.6 fusion
  360.0 7.5 %collective-permute-done.11 = bf16[224,1024]{1,0:T(8,128)(2,1)S(1)} collective-permute-done((bf16[224,1024]{1,0:T(8,128)(2,1)S(1)}, bf16[224,1024]{1,0:T(8,128)(2,1)S(1)}, u32[]{:S(2)}, u32[]{:S(2)}) %collective-permute-start.11) | collective-permute-done | bytes 458784 | tf_op jit(solution)/shard_map/ppermute | solution.py:60
  370.8 3.2 collective-permute-done.12
  374.2 4.7 %collective-permute-done.13 = bf16[56,1024]{1,0:T(8,128)(2,1)S(1)} collective-permute-done((bf16[56,1024]{1,0:T(8,128)(2,1)S(1)}, bf16[56,1024]{1,0:T(8,128)(2,1)S(1)}, u32[]{:S(2)}, u32[]{:S(2)}) %collective-permute-start.13) | collective-permute-done | bytes 114720 | tf_op jit(solution)/shard_map/ppermute | solution.py:60
  378.9 4.0 collective-permute-start.14
  383.0 3.9 collective-permute-done.14
  388.1 3.6 collective-permute-done.15
  394.3 3.6 collective-permute-done.16
  400.3 6.3 %collective-permute-done.17 = bf16[224,1024]{1,0:T(8,128)(2,1)S(1)} collective-permute-done((bf16[224,1024]{1,0:T(8,128)(2,1)S(1)}, bf16[224,1024]{1,0:T(8,128)(2,1)S(1)}, u32[]{:S(2)}, u32[]{:S(2)}) %collective-permute-start.17) | collective-permute-done | bytes 458784 | tf_op jit(solution)/shard_map/ppermute | solution.py:60
  408.7 2.3 slice_bitcast_fusion
  411.0 5.4 %copy.157 = f32[4,1024,256]{2,1,0:T(8,128)} copy(f32[4,1024,256]{1,2,0:T(8,128)} %slice_bitcast_fusion) | data formatting | bytes 8388608
  422.0 2.5 copy.159
  424.5 2.8 maximum_convert_fusion.2
  431.8 3.0 copy.155
  (385 shorter events, 134.4 us)
Async XLA Ops:
  0.6 50.0 %copy-start = (bf16[1024,1024]{1,0:T(8,128)(2,1)S(1)}, bf16[1024,1024]{1,0:T(8,128)(2,1)}, u32[]{:S(2)}) copy-start(bf16[1024,1024]{1,0:T(8,128)(2,1)} %param.29) | copy-start | bytes 6291460
  25.9 21.1 %copy-start.40 = (bf16[256,512]{0,1:T(8,128)(2,1)}, bf16[256,512]{0,1:T(8,128)(2,1)S(1)}, u32[]{:S(2)}) copy-start(bf16[256,512]{0,1:T(8,128)(2,1)S(1)} %copy.141) | copy-start | bytes 786436
  53.4 275.1 %copy-start.11 = (f32[256,1024]{1,0:T(8,128)}, f32[256,1024]{1,0:T(8,128)S(1)}, u32[]{:S(2)}) copy-start(f32[256,1024]{1,0:T(8,128)S(1)} %get-tuple-element.163) | copy-start | bytes 3145732
  58.8 29.3 %collective-permute-start = (bf16[256,1152]{1,0:T(8,128)(2,1)}, bf16[256,1152]{1,0:T(8,128)(2,1)}, u32[]{:S(2)}, u32[]{:S(2)}) collective-permute-start(bf16[256,1152]{1,0:T(8,128)(2,1)} %concatenate.96), channel_id=1, source_target_pairs={{0,2},{1,3},{2,0},{3,1},{4,6},{5,7},{6,4},{7,5},{8,10},{9,11},{10,... | collective-permute-start | bytes 1769480 | tf_op jit(solution)/shard_map/ppermute | solution.py:60
  61.8 24.9 %collective-permute-start.3 = (bf16[256,1024]{1,0:T(8,128)(2,1)}, bf16[256,1024]{1,0:T(8,128)(2,1)}, u32[]{:S(2)}, u32[]{:S(2)}) collective-permute-start(bf16[256,1024]{1,0:T(8,128)(2,1)} %param.43), channel_id=1, source_target_pairs={{0,2},{1,3},{2,0},{3,1},{4,6},{5,7},{6,4},{7,5},{8,10},{9,11},{10,... | collective-permute-start | bytes 1572872 | tf_op jit(solution)/shard_map/ppermute | solution.py:60
  61.8 30.9 %collective-permute-start.4 = (bf16[256,1024]{1,0:T(8,128)(2,1)}, bf16[256,1024]{1,0:T(8,128)(2,1)}, u32[]{:S(2)}, u32[]{:S(2)}) collective-permute-start(bf16[256,1024]{1,0:T(8,128)(2,1)} %param.43), channel_id=1, source_target_pairs={{0,1},{1,0},{2,3},{3,2},{4,5},{5,4},{6,7},{7,6},{8,9},{9,8},{10,11... | collective-permute-start | bytes 1572872 | tf_op jit(solution)/shard_map/ppermute | solution.py:60
  86.7 7.9 %collective-permute-start.5 = (bf16[256,1024]{1,0:T(8,128)(2,1)}, bf16[256,1024]{1,0:T(8,128)(2,1)}, u32[]{:S(2)}, u32[]{:S(2)}) collective-permute-start(bf16[256,1024]{1,0:T(8,128)(2,1)} %collective-permute-done.3), channel_id=1, source_target_pairs={{0,1},{1,0},{2,3},{3,2},{4,5},{5,4},{6,7},{7,6},{8,9},{9,8},{10,11... | collective-permute-start | bytes 1572872 | tf_op jit(solution)/shard_map/ppermute | solution.py:60
  86.7 9.8 %collective-permute-start.1 = (bf16[256,1152]{1,0:T(8,128)(2,1)}, bf16[256,1152]{1,0:T(8,128)(2,1)}, u32[]{:S(2)}, u32[]{:S(2)}) collective-permute-start(bf16[256,1152]{1,0:T(8,128)(2,1)} %concatenate.96), channel_id=1, source_target_pairs={{0,1},{1,0},{2,3},{3,2},{4,5},{5,4},{6,7},{7,6},{8,9},{9,8},{10,11... | collective-permute-start | bytes 1769480 | tf_op jit(solution)/shard_map/ppermute | solution.py:60
  88.2 8.3 %collective-permute-start.2 = (bf16[256,1152]{1,0:T(8,128)(2,1)}, bf16[256,1152]{1,0:T(8,128)(2,1)}, u32[]{:S(2)}, u32[]{:S(2)}) collective-permute-start(bf16[256,1152]{1,0:T(8,128)(2,1)} %collective-permute-done), channel_id=1, source_target_pairs={{0,1},{1,0},{2,3},{3,2},{4,5},{5,4},{6,7},{7,6},{8,9},{9,8},{10,11... | collective-permute-start | bytes 1769480 | tf_op jit(solution)/shard_map/ppermute | solution.py:60
  185.7 16.3 %collective-permute-start.37 = (bf16[288,1024]{1,0:T(8,128)(2,1)S(1)}, bf16[288,1024]{1,0:T(8,128)(2,1)S(1)}, u32[]{:S(2)}, u32[]{:S(2)}) collective-permute-start(bf16[288,1024]{1,0:T(8,128)(2,1)S(1)} %dynamic-slice_bitcast_fusion.1), channel_id=1, source_target_pairs={{0,4},{4,0},{8,12},{12,8},{16,20},{20,16},{24,28},{28,24},{1,5},{5... | collective-permute-start | bytes 1769480 | tf_op jit(solution)/shard_map/ppermute | solution.py:60
  189.0 93.5 %collective-permute-start.8 = (bf16[512,1024]{1,0:T(8,128)(2,1)S(1)}, bf16[512,1024]{1,0:T(8,128)(2,1)S(1)}, u32[]{:S(2)}, u32[]{:S(2)}) collective-permute-start(bf16[512,1024]{1,0:T(8,128)(2,1)S(1)} %slice.109), channel_id=1, source_target_pairs={{0,1},{1,0},{2,3},{3,2},{4,5},{5,4},{6,7},{7,6},{8,9},{9,8},{10,11... | collective-permute-start | bytes 3145736 | tf_op jit(solution)/shard_map/ppermute | solution.py:60
  189.4 96.6 %collective-permute-start.6 = (bf16[512,1024]{1,0:T(8,128)(2,1)S(1)}, bf16[512,1024]{1,0:T(8,128)(2,1)S(1)}, u32[]{:S(2)}, u32[]{:S(2)}) collective-permute-start(bf16[512,1024]{1,0:T(8,128)(2,1)S(1)} %slice.105), channel_id=1, source_target_pairs={{0,1},{1,0},{2,3},{3,2},{4,5},{5,4},{6,7},{7,6},{8,9},{9,8},{10,11... | collective-permute-start | bytes 3145736 | tf_op jit(solution)/shard_map/ppermute | solution.py:60
  189.8 24.9 %collective-permute-start.31 = (bf16[288,1024]{1,0:T(8,128)(2,1)S(1)}, bf16[288,1024]{1,0:T(8,128)(2,1)S(1)}, u32[]{:S(2)}, u32[]{:S(2)}) collective-permute-start(bf16[288,1024]{1,0:T(8,128)(2,1)S(1)} %dynamic-slice_bitcast_fusion.2), channel_id=1, source_target_pairs={{0,4},{4,0},{8,12},{12,8},{16,20},{20,16},{24,28},{28,24},{1,5},{5... | collective-permute-start | bytes 1769480 | tf_op jit(solution)/shard_map/ppermute | solution.py:60
  190.3 36.9 %collective-permute-start.25 = (bf16[288,1024]{1,0:T(8,128)(2,1)S(1)}, bf16[288,1024]{1,0:T(8,128)(2,1)S(1)}, u32[]{:S(2)}, u32[]{:S(2)}) collective-permute-start(bf16[288,1024]{1,0:T(8,128)(2,1)S(1)} %dynamic-slice_bitcast_fusion.3), channel_id=1, source_target_pairs={{0,4},{4,0},{8,12},{12,8},{16,20},{20,16},{24,28},{28,24},{1,5},{5... | collective-permute-start | bytes 1769480 | tf_op jit(solution)/shard_map/ppermute | solution.py:60
  202.0 37.5 %collective-permute-start.19 = (bf16[288,1024]{1,0:T(8,128)(2,1)S(1)}, bf16[288,1024]{1,0:T(8,128)(2,1)S(1)}, u32[]{:S(2)}, u32[]{:S(2)}) collective-permute-start(bf16[288,1024]{1,0:T(8,128)(2,1)S(1)} %dynamic-slice_bitcast_fusion.4), channel_id=1, source_target_pairs={{0,4},{4,0},{8,12},{12,8},{16,20},{20,16},{24,28},{28,24},{1,5},{5... | collective-permute-start | bytes 1769480 | tf_op jit(solution)/shard_map/ppermute | solution.py:60
  214.6 26.9 %collective-permute-start.38 = (bf16[144,1024]{1,0:T(8,128)(2,1)S(1)}, bf16[144,1024]{1,0:T(8,128)(2,1)S(1)}, u32[]{:S(2)}, u32[]{:S(2)}) collective-permute-start(bf16[144,1024]{1,0:T(8,128)(2,1)S(1)} %dynamic-slice_bitcast_fusion.6), channel_id=1, source_target_pairs={{0,8},{4,12},{8,0},{12,4},{16,24},{20,28},{24,16},{28,20},{1,9},{5... | collective-permute-start | bytes 884744 | tf_op jit(solution)/shard_map/ppermute | solution.py:60
  227.3 14.7 %collective-permute-start.32 = (bf16[144,1024]{1,0:T(8,128)(2,1)S(1)}, bf16[144,1024]{1,0:T(8,128)(2,1)S(1)}, u32[]{:S(2)}, u32[]{:S(2)}) collective-permute-start(bf16[144,1024]{1,0:T(8,128)(2,1)S(1)} %dynamic-slice_bitcast_fusion.7), channel_id=1, source_target_pairs={{0,8},{4,12},{8,0},{12,4},{16,24},{20,28},{24,16},{28,20},{1,9},{5... | collective-permute-start | bytes 884744 | tf_op jit(solution)/shard_map/ppermute | solution.py:60
  239.5 13.0 %collective-permute-start.26 = (bf16[144,1024]{1,0:T(8,128)(2,1)S(1)}, bf16[144,1024]{1,0:T(8,128)(2,1)S(1)}, u32[]{:S(2)}, u32[]{:S(2)}) collective-permute-start(bf16[144,1024]{1,0:T(8,128)(2,1)S(1)} %dynamic-slice_bitcast_fusion.8), channel_id=1, source_target_pairs={{0,8},{4,12},{8,0},{12,4},{16,24},{20,28},{24,16},{28,20},{1,9},{5... | collective-permute-start | bytes 884744 | tf_op jit(solution)/shard_map/ppermute | solution.py:60
  241.5 18.2 %collective-permute-start.20 = (bf16[144,1024]{1,0:T(8,128)(2,1)S(1)}, bf16[144,1024]{1,0:T(8,128)(2,1)S(1)}, u32[]{:S(2)}, u32[]{:S(2)}) collective-permute-start(bf16[144,1024]{1,0:T(8,128)(2,1)S(1)} %dynamic-slice_bitcast_fusion.9), channel_id=1, source_target_pairs={{0,8},{4,12},{8,0},{12,4},{16,24},{20,28},{24,16},{28,20},{1,9},{5... | collective-permute-start | bytes 884744 | tf_op jit(solution)/shard_map/ppermute | solution.py:60
  242.0 18.6 %collective-permute-start.39 = (bf16[72,1024]{1,0:T(8,128)(2,1)S(1)}, bf16[72,1024]{1,0:T(8,128)(2,1)S(1)}, u32[]{:S(2)}, u32[]{:S(2)}) collective-permute-start(bf16[72,1024]{1,0:T(8,128)(2,1)S(1)} %dynamic-slice_bitcast_fusion.11), channel_id=1, source_target_pairs={{0,16},{4,20},{8,24},{12,28},{16,0},{20,4},{24,8},{28,12},{1,17},{... | collective-permute-start | bytes 442376 | tf_op jit(solution)/shard_map/ppermute | solution.py:60
  244.9 40.5 %copy-start.43 = (bf16[1024,1024]{1,0:T(8,128)(2,1)S(1)}, bf16[1024,1024]{1,0:T(8,128)(2,1)}, u32[]{:S(2)}) copy-start(bf16[1024,1024]{1,0:T(8,128)(2,1)} %get-tuple-element.36) | copy-start | bytes 6291460
  252.5 18.8 %collective-permute-start.33 = (bf16[72,1024]{1,0:T(8,128)(2,1)S(1)}, bf16[72,1024]{1,0:T(8,128)(2,1)S(1)}, u32[]{:S(2)}, u32[]{:S(2)}) collective-permute-start(bf16[72,1024]{1,0:T(8,128)(2,1)S(1)} %dynamic-slice_bitcast_fusion.12), channel_id=1, source_target_pairs={{0,16},{4,20},{8,24},{12,28},{16,0},{20,4},{24,8},{28,12},{1,17},{... | collective-permute-start | bytes 442376 | tf_op jit(solution)/shard_map/ppermute | solution.py:60
  259.7 16.4 %collective-permute-start.27 = (bf16[72,1024]{1,0:T(8,128)(2,1)S(1)}, bf16[72,1024]{1,0:T(8,128)(2,1)S(1)}, u32[]{:S(2)}, u32[]{:S(2)}) collective-permute-start(bf16[72,1024]{1,0:T(8,128)(2,1)S(1)} %dynamic-slice_bitcast_fusion.13), channel_id=1, source_target_pairs={{0,16},{4,20},{8,24},{12,28},{16,0},{20,4},{24,8},{28,12},{1,17},{... | collective-permute-start | bytes 442376 | tf_op jit(solution)/shard_map/ppermute | solution.py:60
  260.6 21.8 %collective-permute-start.21 = (bf16[72,1024]{1,0:T(8,128)(2,1)S(1)}, bf16[72,1024]{1,0:T(8,128)(2,1)S(1)}, u32[]{:S(2)}, u32[]{:S(2)}) collective-permute-start(bf16[72,1024]{1,0:T(8,128)(2,1)S(1)} %dynamic-slice_bitcast_fusion.14), channel_id=1, source_target_pairs={{0,16},{4,20},{8,24},{12,28},{16,0},{20,4},{24,8},{28,12},{1,17},{... | collective-permute-start | bytes 442376 | tf_op jit(solution)/shard_map/ppermute | solution.py:60
  271.3 19.0 %collective-permute-start.40 = (bf16[72,1024]{1,0:T(8,128)(2,1)S(1)}, bf16[72,1024]{1,0:T(8,128)(2,1)S(1)}, u32[]{:S(2)}, u32[]{:S(2)}) collective-permute-start(bf16[72,1024]{1,0:T(8,128)(2,1)S(1)} %fusion.42), channel_id=1, source_target_pairs={{0,16},{4,20},{8,24},{12,28},{16,0},{20,4},{24,8},{28,12},{1,17},{... | collective-permute-start | bytes 442376 | tf_op jit(solution)/shard_map/ppermute | solution.py:60
  276.1 17.4 %collective-permute-start.34 = (bf16[72,1024]{1,0:T(8,128)(2,1)S(1)}, bf16[72,1024]{1,0:T(8,128)(2,1)S(1)}, u32[]{:S(2)}, u32[]{:S(2)}) collective-permute-start(bf16[72,1024]{1,0:T(8,128)(2,1)S(1)} %fusion.43), channel_id=1, source_target_pairs={{0,16},{4,20},{8,24},{12,28},{16,0},{20,4},{24,8},{28,12},{1,17},{... | collective-permute-start | bytes 442376 | tf_op jit(solution)/shard_map/ppermute | solution.py:60
  282.4 17.3 %collective-permute-start.28 = (bf16[72,1024]{1,0:T(8,128)(2,1)S(1)}, bf16[72,1024]{1,0:T(8,128)(2,1)S(1)}, u32[]{:S(2)}, u32[]{:S(2)}) collective-permute-start(bf16[72,1024]{1,0:T(8,128)(2,1)S(1)} %fusion.44), channel_id=1, source_target_pairs={{0,16},{4,20},{8,24},{12,28},{16,0},{20,4},{24,8},{28,12},{1,17},{... | collective-permute-start | bytes 442376 | tf_op jit(solution)/shard_map/ppermute | solution.py:60
  282.5 19.6 %collective-permute-start.22 = (bf16[72,1024]{1,0:T(8,128)(2,1)S(1)}, bf16[72,1024]{1,0:T(8,128)(2,1)S(1)}, u32[]{:S(2)}, u32[]{:S(2)}) collective-permute-start(bf16[72,1024]{1,0:T(8,128)(2,1)S(1)} %fusion.45), channel_id=1, source_target_pairs={{0,16},{4,20},{8,24},{12,28},{16,0},{20,4},{24,8},{28,12},{1,17},{... | collective-permute-start | bytes 442376 | tf_op jit(solution)/shard_map/ppermute | solution.py:60
  285.9 42.2 %collective-permute-start.9 = (bf16[256,1024]{1,0:T(8,128)(2,1)S(1)}, bf16[256,1024]{1,0:T(8,128)(2,1)S(1)}, u32[]{:S(2)}, u32[]{:S(2)}) collective-permute-start(bf16[256,1024]{1,0:T(8,128)(2,1)S(1)} %slice.136), channel_id=1, source_target_pairs={{0,2},{1,3},{2,0},{3,1},{4,6},{5,7},{6,4},{7,5},{8,10},{9,11},{10,... | collective-permute-start | bytes 1572872 | tf_op jit(solution)/shard_map/ppermute | solution.py:60
  290.3 38.5 %collective-permute-start.7 = (bf16[256,1024]{1,0:T(8,128)(2,1)S(1)}, bf16[256,1024]{1,0:T(8,128)(2,1)S(1)}, u32[]{:S(2)}, u32[]{:S(2)}) collective-permute-start(bf16[256,1024]{1,0:T(8,128)(2,1)S(1)} %slice.134), channel_id=1, source_target_pairs={{0,2},{1,3},{2,0},{3,1},{4,6},{5,7},{6,4},{7,5},{8,10},{9,11},{10,... | collective-permute-start | bytes 1572872 | tf_op jit(solution)/shard_map/ppermute | solution.py:60
  293.5 14.0 %collective-permute-start.41 = (bf16[144,1024]{1,0:T(8,128)(2,1)S(1)}, bf16[144,1024]{1,0:T(8,128)(2,1)S(1)}, u32[]{:S(2)}, u32[]{:S(2)}) collective-permute-start(bf16[144,1024]{1,0:T(8,128)(2,1)S(1)} %pad_maximum_fusion.12), channel_id=1, source_target_pairs={{0,8},{4,12},{8,0},{12,4},{16,24},{20,28},{24,16},{28,20},{1,9},{5... | collective-permute-start | bytes 884744 | tf_op jit(solution)/shard_map/ppermute | solution.py:60
  299.7 14.1 %collective-permute-start.35 = (bf16[144,1024]{1,0:T(8,128)(2,1)S(1)}, bf16[144,1024]{1,0:T(8,128)(2,1)S(1)}, u32[]{:S(2)}, u32[]{:S(2)}) collective-permute-start(bf16[144,1024]{1,0:T(8,128)(2,1)S(1)} %pad_maximum_fusion.11), channel_id=1, source_target_pairs={{0,8},{4,12},{8,0},{12,4},{16,24},{20,28},{24,16},{28,20},{1,9},{5... | collective-permute-start | bytes 884744 | tf_op jit(solution)/shard_map/ppermute | solution.py:60
  302.1 18.0 %collective-permute-start.29 = (bf16[144,1024]{1,0:T(8,128)(2,1)S(1)}, bf16[144,1024]{1,0:T(8,128)(2,1)S(1)}, u32[]{:S(2)}, u32[]{:S(2)}) collective-permute-start(bf16[144,1024]{1,0:T(8,128)(2,1)S(1)} %pad_maximum_fusion.10), channel_id=1, source_target_pairs={{0,8},{4,12},{8,0},{12,4},{16,24},{20,28},{24,16},{28,20},{1,9},{5... | collective-permute-start | bytes 884744 | tf_op jit(solution)/shard_map/ppermute | solution.py:60
  307.4 17.3 %collective-permute-start.23 = (bf16[144,1024]{1,0:T(8,128)(2,1)S(1)}, bf16[144,1024]{1,0:T(8,128)(2,1)S(1)}, u32[]{:S(2)}, u32[]{:S(2)}) collective-permute-start(bf16[144,1024]{1,0:T(8,128)(2,1)S(1)} %pad_maximum_fusion.9), channel_id=1, source_target_pairs={{0,8},{4,12},{8,0},{12,4},{16,24},{20,28},{24,16},{28,20},{1,9},{5... | collective-permute-start | bytes 884744 | tf_op jit(solution)/shard_map/ppermute | solution.py:60
  313.8 43.4 %collective-permute-start.42 = (bf16[288,1024]{1,0:T(8,128)(2,1)}, bf16[288,1024]{1,0:T(8,128)(2,1)}, u32[]{:S(2)}, u32[]{:S(2)}) collective-permute-start(bf16[288,1024]{1,0:T(8,128)(2,1)} %pad_maximum_fusion.6), channel_id=1, source_target_pairs={{0,4},{4,0},{8,12},{12,8},{16,20},{20,16},{24,28},{28,24},{1,5},{5... | collective-permute-start | bytes 1769480 | tf_op jit(solution)/shard_map/ppermute | solution.py:60
  320.1 38.5 %collective-permute-start.36 = (bf16[288,1024]{1,0:T(8,128)(2,1)}, bf16[288,1024]{1,0:T(8,128)(2,1)}, u32[]{:S(2)}, u32[]{:S(2)}) collective-permute-start(bf16[288,1024]{1,0:T(8,128)(2,1)} %pad_maximum_fusion.5), channel_id=1, source_target_pairs={{0,4},{4,0},{8,12},{12,8},{16,20},{20,16},{24,28},{28,24},{1,5},{5... | collective-permute-start | bytes 1769480 | tf_op jit(solution)/shard_map/ppermute | solution.py:60
  324.7 44.7 %collective-permute-start.30 = (bf16[288,1024]{1,0:T(8,128)(2,1)}, bf16[288,1024]{1,0:T(8,128)(2,1)}, u32[]{:S(2)}, u32[]{:S(2)}) collective-permute-start(bf16[288,1024]{1,0:T(8,128)(2,1)} %pad_maximum_fusion.4), channel_id=1, source_target_pairs={{0,4},{4,0},{8,12},{12,8},{16,20},{20,16},{24,28},{28,24},{1,5},{5... | collective-permute-start | bytes 1769480 | tf_op jit(solution)/shard_map/ppermute | solution.py:60
  328.1 64.9 %collective-permute-start.24 = (bf16[288,1024]{1,0:T(8,128)(2,1)}, bf16[288,1024]{1,0:T(8,128)(2,1)}, u32[]{:S(2)}, u32[]{:S(2)}) collective-permute-start(bf16[288,1024]{1,0:T(8,128)(2,1)} %pad_maximum_fusion.3), channel_id=1, source_target_pairs={{0,4},{4,0},{8,12},{12,8},{16,20},{20,16},{24,28},{28,24},{1,5},{5... | collective-permute-start | bytes 1769480 | tf_op jit(solution)/shard_map/ppermute | solution.py:60
  351.2 3.9 collective-permute-start.10
  355.5 12.0 %collective-permute-start.11 = (bf16[224,1024]{1,0:T(8,128)(2,1)S(1)}, bf16[224,1024]{1,0:T(8,128)(2,1)S(1)}, u32[]{:S(2)}, u32[]{:S(2)}) collective-permute-start(bf16[224,1024]{1,0:T(8,128)(2,1)S(1)} %dynamic-slice_bitcast_fusion.5), channel_id=1, source_target_pairs={{0,2},{1,3},{2,0},{3,1},{4,6},{5,7},{6,4},{7,5},{8,10},{9,11},{10,... | collective-permute-start | bytes 1376264 | tf_op jit(solution)/shard_map/ppermute | solution.py:60
  367.7 6.2 %collective-permute-start.12 = (bf16[112,1024]{1,0:T(8,128)(2,1)S(1)}, bf16[112,1024]{1,0:T(8,128)(2,1)S(1)}, u32[]{:S(2)}, u32[]{:S(2)}) collective-permute-start(bf16[112,1024]{1,0:T(8,128)(2,1)S(1)} %dynamic-slice_bitcast_fusion.10), channel_id=1, source_target_pairs={{0,4},{4,0},{8,12},{12,8},{16,20},{20,16},{24,28},{28,24},{1,5},{5... | collective-permute-start | bytes 688136 | tf_op jit(solution)/shard_map/ppermute | solution.py:60
  374.0 4.9 %collective-permute-start.13 = (bf16[56,1024]{1,0:T(8,128)(2,1)S(1)}, bf16[56,1024]{1,0:T(8,128)(2,1)S(1)}, u32[]{:S(2)}, u32[]{:S(2)}) collective-permute-start(bf16[56,1024]{1,0:T(8,128)(2,1)S(1)} %dynamic-slice_bitcast_fusion.15), channel_id=1, source_target_pairs={{0,8},{4,12},{8,0},{12,4},{16,24},{20,28},{24,16},{28,20},{1,9},{5... | collective-permute-start | bytes 344072 | tf_op jit(solution)/shard_map/ppermute | solution.py:60
  378.9 8.0 %collective-permute-start.14 = (bf16[56,1024]{1,0:T(8,128)(2,1)S(1)}, bf16[56,1024]{1,0:T(8,128)(2,1)S(1)}, u32[]{:S(2)}, u32[]{:S(2)}) collective-permute-start(bf16[56,1024]{1,0:T(8,128)(2,1)S(1)} %fusion.49), channel_id=1, source_target_pairs={{0,16},{4,20},{8,24},{12,28},{16,0},{20,4},{24,8},{28,12},{1,17},{... | collective-permute-start | bytes 344072 | tf_op jit(solution)/shard_map/ppermute | solution.py:60
  383.0 16.3 %copy-start.3 = (bf16[1,576,1024]{2,1,0:T(8,128)(2,1)}, bf16[1,576,1024]{2,1,0:T(8,128)(2,1)S(1)}, u32[]{:S(2)}) copy-start(bf16[1,576,1024]{2,1,0:T(8,128)(2,1)S(1)} %maximum_bitcast_fusion.2) | copy-start | bytes 3538948
  386.9 4.9 %collective-permute-start.15 = (bf16[56,1024]{1,0:T(8,128)(2,1)S(1)}, bf16[56,1024]{1,0:T(8,128)(2,1)S(1)}, u32[]{:S(2)}, u32[]{:S(2)}) collective-permute-start(bf16[56,1024]{1,0:T(8,128)(2,1)S(1)} %add_convert_fusion.5), channel_id=1, source_target_pairs={{0,8},{4,12},{8,0},{12,4},{16,24},{20,28},{24,16},{28,20},{1,9},{5... | collective-permute-start | bytes 344072 | tf_op jit(solution)/shard_map/ppermute | solution.py:60
  391.8 6.1 %collective-permute-start.16 = (bf16[112,1024]{1,0:T(8,128)(2,1)S(1)}, bf16[112,1024]{1,0:T(8,128)(2,1)S(1)}, u32[]{:S(2)}, u32[]{:S(2)}) collective-permute-start(bf16[112,1024]{1,0:T(8,128)(2,1)S(1)} %pad_maximum_fusion.13), channel_id=1, source_target_pairs={{0,4},{4,0},{8,12},{12,8},{16,20},{20,16},{24,28},{28,24},{1,5},{5... | collective-permute-start | bytes 688136 | tf_op jit(solution)/shard_map/ppermute | solution.py:60
  398.0 8.5 %collective-permute-start.17 = (bf16[224,1024]{1,0:T(8,128)(2,1)S(1)}, bf16[224,1024]{1,0:T(8,128)(2,1)S(1)}, u32[]{:S(2)}, u32[]{:S(2)}) collective-permute-start(bf16[224,1024]{1,0:T(8,128)(2,1)S(1)} %pad_maximum_fusion.8), channel_id=1, source_target_pairs={{0,2},{1,3},{2,0},{3,1},{4,6},{5,7},{6,4},{7,5},{8,10},{9,11},{10,... | collective-permute-start | bytes 1376264 | tf_op jit(solution)/shard_map/ppermute | solution.py:60
  408.7 18.6 %collective-permute-start.18 = (bf16[448,1024]{1,0:T(8,128)(2,1)}, bf16[448,1024]{1,0:T(8,128)(2,1)}, u32[]{:S(2)}, u32[]{:S(2)}) collective-permute-start(bf16[448,1024]{1,0:T(8,128)(2,1)} %pad_maximum_fusion.2), channel_id=1, source_target_pairs={{0,1},{1,0},{2,3},{3,2},{4,5},{5,4},{6,7},{7,6},{8,9},{9,8},{10,11... | collective-permute-start | bytes 2752520 | tf_op jit(solution)/shard_map/ppermute | solution.py:60
  (74 other events, 285.8 us)

commit v2 on v1

v2 whole, which is shorter than its diff:
```python
import functools

import jax
import jax.numpy as jnp
import numpy as np
from jax import lax
from jax.experimental import pallas as pl
from jax.experimental.pallas import tpu as pltpu
from jax.sharding import PartitionSpec as P

MODEL_WIDTH = 1024
HALF_WIDTH = 512
HEAD_WIDTH = 64
ADAPTER_RANK = 16
TOK_DEV = 256
EXP_DEV = 4
LANES = 128
META = MODEL_WIDTH + LANES
PACK_ROWS = 576
ATT_ROWS = 896
NORM_EPS = 1e-06
ROPE_BASE = 10000.0
F32 = jnp.float32
BF = jnp.bfloat16
ANY = pl.BlockSpec(memory_space=pl.ANY)
SMEM = pl.BlockSpec(memory_space=pltpu.SMEM)
VMEM = pl.BlockSpec(memory_space=pltpu.VMEM)
VMEM_LIMIT = 60 * 1024 * 1024


def nn(a, b):
    return lax.dot_general(a, b, (((1,), (0,)), ((), ())), preferred_element_type=F32)


def nt(a, b):
    return lax.dot_general(a, b, (((1,), (1,)), ((), ())), preferred_element_type=F32)


def tn(a, b):
    return lax.dot_general(a, b, (((0,), (0,)), ((), ())), preferred_element_type=F32)


def shape(*dims, dtype=BF):
    return jax.ShapeDtypeStruct(dims, dtype)


def rope_tables():
    inverse = ROPE_BASE ** (-2.0 * np.arange(HEAD_WIDTH // 2, dtype=np.float64) / HEAD_WIDTH)
    angles = np.arange(TOK_DEV, dtype=np.float64)[:, None] * inverse[None, :]
    cosine = np.tile(np.cos(angles), (1, 4)).astype(np.float32)
    sine = np.sin(angles)
    signed = np.concatenate([-sine, sine, -sine, sine], axis=1).astype(np.float32)
    return cosine, signed


def lanes_of(rows):
    return lax.broadcasted_iota(jnp.int32, (rows, LANES), 1)


def swap_halves(block):
    first = lanes_of(block.shape[0]) % HEAD_WIDTH < HEAD_WIDTH // 2
    return jnp.where(first, pltpu.roll(block, LANES - 32, 1), pltpu.roll(block, 32, 1))


def both(block, odd):
    low = lanes_of(block.shape[0]) < HEAD_WIDTH
    wide = block.astype(F32)
    other = pltpu.roll(wide, HEAD_WIDTH, 1)
    return (jnp.where(low, other, wide) if odd else jnp.where(low, wide, other)).astype(BF)


def stacked(block):
    low = lanes_of(block.shape[0]) < HEAD_WIDTH
    wide = block.astype(F32)
    return jnp.concatenate(
        [jnp.where(low, wide, 0.0).astype(BF), jnp.where(low, 0.0, wide).astype(BF)], axis=0
    )


def unstacked(pair):
    low = lanes_of(TOK_DEV) < HEAD_WIDTH
    return jnp.where(low, pair[:TOK_DEV], pair[TOK_DEV:])


def allowed_keys(length):
    row = lax.broadcasted_iota(jnp.int32, (2 * TOK_DEV, TOK_DEV), 0) % TOK_DEV
    col = lax.broadcasted_iota(jnp.int32, (2 * TOK_DEV, TOK_DEV), 1)
    return (col <= row) & (col < length)


def softmax(query_pair, key_both, allowed):
    scores = jnp.where(allowed, nt(query_pair, key_both) * (HEAD_WIDTH**-0.5), -1e30)
    exponent = jnp.exp(scores - jnp.max(scores, axis=1, keepdims=True))
    return exponent * (1.0 / jnp.sum(exponent, axis=1, keepdims=True))


def column(index):
    return slice(index * LANES, (index + 1) * LANES)


def forward_body(
    scalars, x_ref, g1_ref, g2_ref, cos_ref, sin_ref, routes_ref, router_ref,
    aat_h, wq_h, bq_h, wkv_h, bkv_h, ao_h, wo_h, bo_h,
    hidden_ref, payload_ref, normed_ref, lowrank_ref, q_ref, k_ref, v_ref, att_ref, orank_ref, wide_ref,
    aat, wq, bq, wkv, bkv, ao, wo, bo, sems, *, experts,
):
    copies = [
        pltpu.make_async_copy(source, target, sems.at[index])
        for index, (source, target) in enumerate(
            [(aat_h, aat), (wq_h, wq), (bq_h, bq), (wkv_h, wkv), (bkv_h, bkv), (ao_h, ao), (wo_h, wo), (bo_h, bo)]
        )
    ]
    for copy in copies:
        copy.start()
    adapter = scalars[0]
    length = scalars[1]
    lane = lanes_of(TOK_DEV)
    mask = lane // ADAPTER_RANK == adapter
    x = x_ref[...].astype(F32)
    factor = lax.rsqrt(jnp.mean(x * x, axis=1, keepdims=True) + NORM_EPS)
    normed = (x * factor * g1_ref[...]).astype(BF)
    normed_ref[...] = normed
    copies[0].wait()
    low = nn(normed, aat[...])
    ranks = [jnp.where(mask, low[:, column(i)], 0.0).astype(BF) for i in range(3)]
    for i in range(3):
        lowrank_ref[:, column(i)] = ranks[i]
    cosine = cos_ref[...]
    sine = sin_ref[...]
    copies[1].wait()
    copies[2].wait()
    query_pre = nn(normed, wq[...]) + nn(ranks[0], bq[...])
    for j in range(8):
        block = query_pre[:, column(j)]
        q_ref[:, column(j)] = (block * cosine + swap_halves(block) * sine).astype(BF)
    copies[3].wait()
    copies[4].wait()
    pre = nn(normed, wkv[...])
    key_pre = pre[:, :HALF_WIDTH] + nn(ranks[1], bkv[0])
    v_ref[...] = (pre[:, HALF_WIDTH:] + nn(ranks[2], bkv[1])).astype(BF)
    for j in range(4):
        block = key_pre[:, column(j)]
        k_ref[:, column(j)] = (block * cosine + swap_halves(block) * sine).astype(BF)
    allowed = allowed_keys(length)
    for j in range(8):
        pair = stacked(q_ref[:, column(j)])
        probs = softmax(pair, both(k_ref[:, column(j // 2)], j % 2), allowed).astype(BF)
        att_ref[:, column(j)] = unstacked(nn(probs, both(v_ref[:, column(j // 2)], j % 2))).astype(BF)
    attended = att_ref[...]
    for copy in copies[5:]:
        copy.wait()
    orank = jnp.where(mask, nn(attended, ao[...]), 0.0).astype(BF)
    orank_ref[...] = orank
    hidden = x + nn(attended, wo[...]) + nn(orank, bo[...])
    hidden_ref[...] = hidden
    factor2 = lax.rsqrt(jnp.mean(hidden * hidden, axis=1, keepdims=True) + NORM_EPS)
    normed2 = (hidden * factor2 * g2_ref[...]).astype(BF)
    spread = jnp.where(
        lax.broadcasted_iota(jnp.int32, (experts, LANES), 0)
        == lax.broadcasted_iota(jnp.int32, (experts, LANES), 1), 1.0, 0.0,
    ).astype(BF)
    wide = nn(router_ref[...], spread).astype(BF)
    wide_ref[...] = wide
    logits = nn(normed2, wide)
    routes = routes_ref[...]
    selected = routes[:, 0:1] == lane
    for k in range(1, routes.shape[1]):
        selected = selected | (routes[:, k : k + 1] == lane)
    top = jnp.max(jnp.where(selected, logits, -1e30), axis=1, keepdims=True)
    chosen = jnp.where(selected, jnp.exp(jnp.minimum(logits - top, 0.0)), 0.0)
    live = lax.broadcasted_iota(jnp.int32, (TOK_DEV, 1), 0) < length
    gates = chosen * jnp.where(live, 1.0 / jnp.sum(chosen, axis=1, keepdims=True), 0.0)
    high = gates.astype(BF).astype(F32)
    meta = high + pltpu.roll(gates - high, 32, 1) + jnp.where(lane >= 96, adapter.astype(F32), 0.0)
    payload_ref[:, :MODEL_WIDTH] = normed2
    payload_ref[:, MODEL_WIDTH:] = meta.astype(BF)


def attention_forward(scalars, x, g1, g2, cosine, sine, routes, router, weights):
    experts = router.shape[1]
    return pl.pallas_call(
        functools.partial(forward_body, experts=experts),
        out_shape=[
            shape(TOK_DEV, MODEL_WIDTH, dtype=F32),
            shape(TOK_DEV, META),
            shape(TOK_DEV, MODEL_WIDTH),
            shape(TOK_DEV, 3 * LANES),
            shape(TOK_DEV, MODEL_WIDTH),
            shape(TOK_DEV, HALF_WIDTH),
            shape(TOK_DEV, HALF_WIDTH),
            shape(TOK_DEV, MODEL_WIDTH),
            shape(TOK_DEV, LANES),
            shape(MODEL_WIDTH, LANES),
        ],
        in_specs=[SMEM] + [VMEM] * 7 + [ANY] * 8,
        out_specs=[VMEM] * 10,
        scratch_shapes=[pltpu.VMEM(w.shape, BF) for w in weights] + [pltpu.SemaphoreType.DMA((8,))],
        compiler_params=pltpu.CompilerParams(vmem_limit_bytes=VMEM_LIMIT),
        cost_estimate=pl.CostEstimate(flops=3_000_000_000, bytes_accessed=20_000_000, transcendentals=1_000_000),
        name="attention_forward",
    )(scalars, x, g1, g2, cosine, sine, routes, router, *weights)


def backward_body(
    scalars, x_ref, g1_ref, g2_ref, cos_ref, sin_ref, hidden_ref, keep_ref, got_ref, og_ref,
    normed_ref, lowrank_ref, q_ref, k_ref, v_ref, att_ref, orank_ref,
    aat_h, wq_h, bq_h, wkv_h, bkv_h, ao_h, wo_h, bo_h,
    gi_ref, mine_ref, send_ref,
    aat, wq, bq, wkv, bkv, ao, wo, bo, pack, gq_s, gk_s, gv_s, sems,
):
    order = [(bo_h, bo), (wo_h, wo), (ao_h, ao), (bq_h, bq), (bkv_h, bkv), (wq_h, wq), (wkv_h, wkv), (aat_h, aat)]
    copies = [
        pltpu.make_async_copy(source, target, sems.at[index]) for index, (source, target) in enumerate(order)
    ]
    for copy in copies:
        copy.start()
    adapter = scalars[0]
    length = scalars[1]
    side = scalars[2]
    mask = lanes_of(TOK_DEV) // ADAPTER_RANK == adapter

    def masked(values):
        return jnp.where(mask, values, 0.0).astype(BF)

    hidden = hidden_ref[...]
    factor2 = lax.rsqrt(jnp.mean(hidden * hidden, axis=1, keepdims=True) + NORM_EPS)
    live = lax.broadcasted_iota(jnp.int32, (TOK_DEV, 1), 0) < length
    grad_live = jnp.where(live, og_ref[...].astype(F32), 0.0)
    y = (keep_ref[...].astype(F32) + got_ref[...].astype(F32)) * g2_ref[...]
    inner = jnp.mean(y * hidden, axis=1, keepdims=True)
    grad_hidden = grad_live + factor2 * (y - hidden * (factor2 * factor2 * inner))
    gi_ref[...] = grad_hidden
    branch = grad_hidden.astype(BF)
    pack[768:896, :] = tn(orank_ref[...], branch).astype(BF)
    for copy in copies[:3]:
        copy.wait()
    grad_orank = masked(nt(branch, bo[...]))
    pack[640:768, :] = tn(grad_orank, att_ref[...]).astype(BF)
    grad_att = (nt(branch, wo[...]) + nt(grad_orank, ao[...])).astype(BF)
    allowed = allowed_keys(length)
    cosine = cos_ref[...]
    sine = sin_ref[...]
    low = lanes_of(TOK_DEV) < HEAD_WIDTH
    scale = HEAD_WIDTH**-0.5
    kept = None
    for j in range(8):
        pair = stacked(q_ref[:, column(j)])
        key_both = both(k_ref[:, column(j // 2)], j % 2)
        value_both = both(v_ref[:, column(j // 2)], j % 2)
        probs = softmax(pair, key_both, allowed)
        grad_pair = stacked(grad_att[:, column(j)])
        grad_probs = nt(grad_pair, value_both).astype(BF).astype(F32)
        grad_v = tn(probs.astype(BF), grad_pair)
        scores = (probs * (grad_probs - jnp.sum(grad_probs * probs, axis=1, keepdims=True))).astype(BF)
        grad_q = unstacked(nn(scores, key_both)) * scale
        gq_s[:, column(j)] = (grad_q * cosine - swap_halves(grad_q) * sine).astype(BF)
        grad_k = tn(scores, pair) * scale
        grad_v = grad_v + pltpu.roll(grad_v, HEAD_WIDTH, 1)
        grad_k = grad_k + pltpu.roll(grad_k, HEAD_WIDTH, 1)
        if j % 2 == 0:
            kept = (grad_k, grad_v)
        else:
            block = jnp.where(low, kept[0], grad_k)
            gk_s[:, column(j // 2)] = (block * cosine - swap_halves(block) * sine).astype(BF)
            gv_s[:, column(j // 2)] = jnp.where(low, kept[1], grad_v).astype(BF)
    gq = gq_s[...]
    gk = gk_s[...]
    gv = gv_s[...]
    pack[384:512, :] = tn(lowrank_ref[:, column(0)], gq).astype(BF)
    pack[512:640, :HALF_WIDTH] = tn(lowrank_ref[:, column(1)], gk).astype(BF)
    pack[512:640, HALF_WIDTH:] = tn(lowrank_ref[:, column(2)], gv).astype(BF)
    copies[3].wait()
    copies[4].wait()
    grad_rank = jnp.concatenate(
        [masked(nt(gq, bq[...])), masked(nt(gk, bkv[0])), masked(nt(gv, bkv[1]))], axis=1
    )
    pack[0:384, :] = tn(grad_rank, normed_ref[...]).astype(BF)
    for copy in copies[5:]:
        copy.wait()
    grad_normed = (
        nt(gq, wq[...])
        + nt(jnp.concatenate([gk, gv], axis=1), wkv[...])
        + nt(grad_rank, aat[...])
    )
    x = x_ref[...].astype(F32)
    factor = lax.rsqrt(jnp.mean(x * x, axis=1, keepdims=True) + NORM_EPS)
    z = grad_normed * g1_ref[...]
    inner = jnp.mean(z * x, axis=1, keepdims=True)
    gi_ref[...] += factor * (z - x * (factor * factor * inner))
    half = ATT_ROWS // 2
    mine_ref[...] = pack[pl.ds(pl.multiple_of(side * half, 16), half), :]
    send_ref[...] = pack[pl.ds(pl.multiple_of((1 - side) * half, 16), half), :]


def attention_backward(scalars, arrays, weights):
    half = ATT_ROWS // 2
    return pl.pallas_call(
        backward_body,
        out_shape=[shape(TOK_DEV, MODEL_WIDTH, dtype=F32), shape(half, MODEL_WIDTH), shape(half, MODEL_WIDTH)],
        in_specs=[SMEM] + [VMEM] * len(arrays) + [ANY] * 8,
        out_specs=[VMEM] * 3,
        scratch_shapes=[pltpu.VMEM(w.shape, BF) for w in weights]
        + [
            pltpu.VMEM((ATT_ROWS, MODEL_WIDTH), BF),
            pltpu.VMEM((TOK_DEV, MODEL_WIDTH), BF),
            pltpu.VMEM((TOK_DEV, HALF_WIDTH), BF),
            pltpu.VMEM((TOK_DEV, HALF_WIDTH), BF),
            pltpu.SemaphoreType.DMA((8,)),
        ],
        compiler_params=pltpu.CompilerParams(vmem_limit_bytes=VMEM_LIMIT),
        cost_estimate=pl.CostEstimate(flops=6_000_000_000, bytes_accessed=24_000_000, transcendentals=1_000_000),
        name="attention_backward",
    )(scalars, *arrays, *weights)


def expert_body(scalars, *refs, expert, first, last, count, experts):
    refs = list(refs)

    def take(number):
        taken = refs[:number]
        del refs[:number]
        return taken

    x_blocks = take(count)
    g_blocks = take(count)
    ain_h, win_h, bin_h, adn_h, wdn_h, bdn_h = take(6)
    if not first:
        f_in, b_in, c_in = take(3)
    if last:
        (wr_ref,) = take(1)
        f_out, b_out = take(2)
    else:
        f_out, b_out, c_out = take(3)
    mine_ref, send_ref = take(2)
    xs, gs_buf, ain, win, bin_, adn, wdn, bdn, acc_a, acc_bi, acc_ad, acc_bd, pack, xsem, gsem, wsem = refs
    step = pl.program_id(0)
    slot = lax.rem(step, 2)
    early = [
        pltpu.make_async_copy(source.at[expert], target, wsem.at[index])
        for index, (source, target) in enumerate([(ain_h, ain), (win_h, win), (bin_h, bin_)])
    ]
    late = [
        pltpu.make_async_copy(source.at[expert], target, wsem.at[3 + index])
        for index, (source, target) in enumerate([(adn_h, adn), (wdn_h, wdn), (bdn_h, bdn)])
    ]

    def fetch(block):
        pltpu.make_async_copy(x_blocks[block], xs.at[block % 2], xsem.at[block % 2]).start()
        pltpu.make_async_copy(g_blocks[block], gs_buf.at[block % 2], gsem.at[block % 2]).start()

    @pl.when(step == 0)
    def _():
        fetch(0)
        for copy in early + late:
            copy.start()
        for copy in early:
            copy.wait()

    for block in range(1, count):
        @pl.when(step == block - 1)
        def _(block=block):
            fetch(block)

    pltpu.make_async_copy(x_blocks[0], xs.at[slot], xsem.at[slot]).wait()
    pltpu.make_async_copy(g_blocks[0], gs_buf.at[slot], gsem.at[slot]).wait()
    eid = scalars[0]
    side = scalars[1]
    x = xs[slot, :, :MODEL_WIDTH]
    meta = xs[slot, :, MODEL_WIDTH:].astype(F32)
    lane = lanes_of(TOK_DEV)
    adapter = meta[:, 96:97].astype(jnp.int32)
    mask = lane // ADAPTER_RANK == adapter

    def masked(values):
        return jnp.where(mask, values, 0.0).astype(BF)

    gates = jnp.where(lane < experts, meta + pltpu.roll(meta, 96, 1), 0.0)
    here = lane == eid
    gate_e = jnp.sum(jnp.where(here, gates, 0.0), axis=1, keepdims=True)
    low = nn(x, ain[...])
    low_gate = masked(low[:, :LANES])
    low_up = masked(low[:, LANES:])
    gate = nn(x, win[:, :HALF_WIDTH]) + nn(low_gate, bin_[0])
    up = nn(x, win[:, HALF_WIDTH:]) + nn(low_up, bin_[1])
    sig = 1.0 / (1.0 + jnp.exp(-gate))
    silu = gate * sig
    active = (silu * up).astype(BF)

    @pl.when(step == 0)
    def _():
        for copy in late:
            copy.wait()

    down = masked(nn(active, adn[...]))
    grad = gs_buf[slot].astype(F32)
    out = nn(active, wdn[...]) + nn(down, bdn[...])
    grad_gate_e = jnp.sum(out * grad, axis=1, keepdims=True)
    weighted = gate_e * out
    if not first:
        weighted = weighted + f_in[...].astype(F32)
    f_out[...] = weighted.astype(f_out.dtype)
    slot_grad = (gate_e * grad).astype(BF)
    grad_down = masked(nt(slot_grad, bdn[...]))
    grad_active = nt(slot_grad, wdn[...]) + nt(grad_down, adn[...])
    gate_grad = (grad_active * up * sig * (1.0 + gate * (1.0 - sig))).astype(BF)
    up_grad = (grad_active * silu).astype(BF)
    grad_low = jnp.concatenate([masked(nt(gate_grad, bin_[0])), masked(nt(up_grad, bin_[1]))], axis=1)
    both_grads = jnp.concatenate([gate_grad, up_grad], axis=1)
    rows = nt(both_grads, win[...]) + nt(grad_low, ain[...])
    part = (gate_e * grad_gate_e) * (jnp.where(here, 1.0, 0.0) - gates)
    if not first:
        rows = rows + b_in[...].astype(F32)
        part = part + c_in[...]
    if last:
        rows = rows + nt(part.astype(BF), wr_ref[...])
    else:
        c_out[...] = part
    b_out[...] = rows.astype(b_out.dtype)
    grads = [
        tn(grad_low, x),
        jnp.concatenate([tn(low_gate, gate_grad), tn(low_up, up_grad)], axis=1),
        tn(grad_down, active),
        tn(down, slot_grad),
    ]
    sums = [acc_a, acc_bi, acc_ad, acc_bd]

    @pl.when(step == 0)
    def _():
        for total, value in zip(sums, grads):
            total[...] = value

    @pl.when(step > 0)
    def _():
        for total, value in zip(sums, grads):
            total[...] += value

    @pl.when(step == count - 1)
    def _():
        pack[0:256, :] = acc_a[...].astype(BF)
        pack[256:384, :] = acc_bi[...].astype(BF)
        pack[384:512, :] = acc_bd[...].astype(BF)
        pack[512:576, :HALF_WIDTH] = acc_ad[0:64, :].astype(BF)
        pack[512:576, HALF_WIDTH:] = acc_ad[64:128, :].astype(BF)
        half = PACK_ROWS // 2
        mine_ref[...] = pack[pl.ds(pl.multiple_of(side * half, 16), half), :]
        send_ref[...] = pack[pl.ds(pl.multiple_of((1 - side) * half, 16), half), :]


def expert_call(expert, scalars, x_blocks, g_blocks, weights, carried, router_wide, experts):
    count = len(x_blocks)
    total = count * TOK_DEV
    first = carried is None
    last = router_wide is not None
    rows = lambda width: pl.BlockSpec((TOK_DEV, width), lambda i, *_: (i, 0))
    whole = lambda *dims: pl.BlockSpec(dims, lambda i, *_: (0,) * len(dims), pipeline_mode=pl.Buffered(1))
    in_specs = [ANY] * (2 * count + 6)
    args = [*x_blocks, *g_blocks, *weights]
    if not first:
        in_specs += [rows(MODEL_WIDTH), rows(MODEL_WIDTH), rows(LANES)]
        args += list(carried)
    if last:
        in_specs.append(whole(MODEL_WIDTH, LANES))
        args.append(router_wide)
    kind = BF if last else F32
    outs = [shape(total, MODEL_WIDTH, dtype=kind), shape(total, MODEL_WIDTH, dtype=kind)]
    out_specs = [rows(MODEL_WIDTH), rows(MODEL_WIDTH)]
    if not last:
        outs.append(shape(total, LANES, dtype=F32))
        out_specs.append(rows(LANES))
    half = PACK_ROWS // 2
    for _ in range(2):
        outs.append(shape(half, MODEL_WIDTH))
        out_specs.append(pl.BlockSpec((half, MODEL_WIDTH), lambda i, *_: (0, 0)))
    scratch = [pltpu.VMEM((2, TOK_DEV, META), BF), pltpu.VMEM((2, TOK_DEV, MODEL_WIDTH), BF)]
    scratch += [pltpu.VMEM(w.shape[1:], BF) for w in weights]
    scratch += [
        pltpu.VMEM((256, MODEL_WIDTH), F32),
        pltpu.VMEM((128, MODEL_WIDTH), F32),
        pltpu.VMEM((128, HALF_WIDTH), F32),
        pltpu.VMEM((128, MODEL_WIDTH), F32),
        pltpu.VMEM((PACK_ROWS, MODEL_WIDTH), BF),
        pltpu.SemaphoreType.DMA((2,)),
        pltpu.SemaphoreType.DMA((2,)),
        pltpu.SemaphoreType.DMA((6,)),
    ]
    return pl.pallas_call(
        functools.partial(
            expert_body, expert=expert, first=first, last=last, count=count, experts=experts
        ),
        out_shape=outs,
        grid_spec=pltpu.PrefetchScalarGridSpec(
            num_scalar_prefetch=1, grid=(count,), in_specs=in_specs, out_specs=out_specs, scratch_shapes=scratch
        ),
        compiler_params=pltpu.CompilerParams(
            dimension_semantics=("arbitrary",), vmem_limit_bytes=VMEM_LIMIT
        ),
        cost_estimate=pl.CostEstimate(
            flops=total * 9_800_000, bytes_accessed=20_000_000, transcendentals=total * 512
        ),
        name="expert_step",
    )(scalars, *args)


def expert_finish_body(scalars, *refs):
    pieces = refs[: 2 * EXP_DEV]
    a_in, b_in, a_down, b_down, pack = refs[2 * EXP_DEV :]
    side = scalars[0]
    half = PACK_ROWS // 2
    step = pl.program_id(0)
    for expert in range(EXP_DEV):
        @pl.when(step == expert)
        def _(expert=expert):
            pack[pl.ds(pl.multiple_of(side * half, 16), half), :] = pieces[2 * expert][...]
            pack[pl.ds(pl.multiple_of((1 - side) * half, 16), half), :] = pieces[2 * expert + 1][...]
    a_in[0] = pack[0:256, :].astype(F32).T
    b_in[0, 0] = pack[256:384, :HALF_WIDTH].astype(F32)
    b_in[0, 1] = pack[256:384, HALF_WIDTH:].astype(F32)
    b_down[0] = pack[384:512, :].astype(F32)
    a_down[0] = jnp.concatenate([pack[512:576, :HALF_WIDTH], pack[512:576, HALF_WIDTH:]], axis=0).astype(F32).T


def expert_finish(side, pieces):
    half = PACK_ROWS // 2
    block = lambda *dims: pl.BlockSpec((1,) + dims, lambda i, *_: (i,) + (0,) * len(dims))
    dims = [(MODEL_WIDTH, 256), (2, 128, HALF_WIDTH), (HALF_WIDTH, 128), (128, MODEL_WIDTH)]
    return pl.pallas_call(
        expert_finish_body,
        out_shape=[shape(EXP_DEV, *d, dtype=F32) for d in dims],
        grid_spec=pltpu.PrefetchScalarGridSpec(
            num_scalar_prefetch=1,
            grid=(EXP_DEV,),
            in_specs=[
                pl.BlockSpec((half, MODEL_WIDTH), lambda i, *_: (0, 0), pipeline_mode=pl.Buffered(1))
            ] * (2 * EXP_DEV),
            out_specs=[block(*d) for d in dims],
            scratch_shapes=[pltpu.VMEM((PACK_ROWS, MODEL_WIDTH), BF)],
        ),
        compiler_params=pltpu.CompilerParams(
            dimension_semantics=("arbitrary",), vmem_limit_bytes=VMEM_LIMIT
        ),
        cost_estimate=pl.CostEstimate(flops=1_000_000, bytes_accessed=15_000_000, transcendentals=0),
        name="expert_finish",
    )(side, *pieces)


def attention_finish_body(scalars, mine_ref, got_ref, a_ref, bq_ref, bkv_ref, oa_ref, ob_ref, pack):
    side = scalars[0]
    half = ATT_ROWS // 2
    pack[pl.ds(pl.multiple_of(side * half, 16), half), :] = mine_ref[...]
    pack[pl.ds(pl.multiple_of((1 - side) * half, 16), half), :] = got_ref[...]
    a_ref[...] = pack[0:384, :].astype(F32).T
    bq_ref[...] = pack[384:512, :].astype(F32)
    bkv_ref[0] = pack[512:640, :HALF_WIDTH].astype(F32)
    bkv_ref[1] = pack[512:640, HALF_WIDTH:].astype(F32)
    oa_ref[...] = pack[640:768, :].astype(F32).T
    ob_ref[...] = pack[768:896, :].astype(F32)


def attention_finish(side, mine, got):
    dims = [(MODEL_WIDTH, 384), (128, MODEL_WIDTH), (2, 128, HALF_WIDTH), (MODEL_WIDTH, 128), (128, MODEL_WIDTH)]
    return pl.pallas_call(
        attention_finish_body,
        out_shape=[shape(*d, dtype=F32) for d in dims],
        in_specs=[SMEM, VMEM, VMEM],
        out_specs=[VMEM] * 5,
        scratch_shapes=[pltpu.VMEM((ATT_ROWS, MODEL_WIDTH), BF)],
        compiler_params=pltpu.CompilerParams(vmem_limit_bytes=VMEM_LIMIT),
        cost_estimate=pl.CostEstimate(flops=1_000_000, bytes_accessed=6_000_000, transcendentals=0),
        name="attention_finish",
    )(side, mine, got)


def swap(values, axis, bit):
    size = lax.axis_size(axis)
    return lax.ppermute(values, axis, [(i, i ^ (1 << bit)) for i in range(size)])


def axis_bits(axis):
    return lax.axis_size(axis).bit_length() - 1


def gather_blocks(values):
    blocks = [values]
    for bit in reversed(range(axis_bits("expert"))):
        blocks = blocks + [swap(block, "expert", bit) for block in blocks]
    return blocks


def return_stages(partial):
    for bit in range(axis_bits("expert")):
        half = partial.shape[0] // 2
        got = swap(partial[half:], "expert", bit)
        if half == TOK_DEV:
            return partial[:half], got
        partial = (partial[:half].astype(F32) + got.astype(F32)).astype(BF)


class Sum:
    def __init__(self, mine, send, stages):
        self.path = []
        self.stages = list(stages)
        self.mine = mine
        self.send = send
        self.begin(True)

    def begin(self, halved):
        axis, bit = self.stages.pop(0)
        self.path.append((axis, bit, halved))
        self.got = swap(self.send, axis, bit)

    def split(self, values):
        axis, bit = self.stages[0]
        rows, width = values.shape
        if rows % 16:
            self.mine = self.send = values
            return False
        side = (lax.axis_index(axis) >> bit) & 1
        halves = values.reshape(2, rows // 2, width)
        self.mine = lax.dynamic_index_in_dim(halves, side, 0, keepdims=False)
        self.send = lax.dynamic_index_in_dim(halves, 1 - side, 0, keepdims=False)
        return True

    def advance(self):
        if self.stages:
            values = (self.mine.astype(F32) + self.got.astype(F32)).astype(BF)
            halved = self.split(values)
            self.begin(halved)
            return
        if self.path[-1][2] is not None:
            self.values = (self.mine.astype(F32) + self.got.astype(F32)).astype(BF)
            while not self.path[-1][2]:
                self.path.pop()
            self.path.append((None, None, None))
        else:
            self.path.pop()
            axis, bit, _ = self.path.pop()
            side = (lax.axis_index(axis) >> bit) & 1
            low = jnp.where(side == 0, self.values, self.got)
            high = jnp.where(side == 0, self.got, self.values)
            self.values = jnp.concatenate([low, high], axis=0)
            self.path.append((None, None, None))
        axis, bit, _ = self.path[-2]
        self.got = swap(self.values, axis, bit)

    def pending(self):
        return bool(self.stages) or self.path[-1][2] is not None or len(self.path) > 2

    def finish(self):
        while self.pending():
            self.advance()
        return self.values, self.got


def tie(first, second):
    return lax.optimization_barrier((first, second))


def on_device(
    inputs,
    lengths,
    routes,
    adapter_of_sequence,
    first_norm_gain,
    query_weight,
    key_value_weight,
    output_weight,
    second_norm_gain,
    router_weight,
    expert_input_weight,
    expert_down_weight,
    attention_first_factors,
    query_second_factors,
    key_value_second_factors,
    output_first_factors,
    output_second_factors,
    expert_input_first_factors,
    expert_input_second_factors,
    expert_down_first_factors,
    expert_down_second_factors,
    output_gradient,
):
    experts = EXP_DEV * lax.axis_size("expert")
    place = lax.axis_index("expert")
    dp_side = lax.axis_index("dp") & 1
    core_side = place & 1
    grad_blocks = gather_blocks(output_gradient)
    cosine, sine = rope_tables()
    scalars = jnp.stack([adapter_of_sequence[0], lengths[0], core_side]).astype(jnp.int32)
    g1 = first_norm_gain[None]
    g2 = second_norm_gain[None]
    weights = [
        attention_first_factors,
        query_weight,
        query_second_factors,
        key_value_weight,
        key_value_second_factors,
        output_first_factors,
        output_weight,
        output_second_factors,
    ]
    hidden, payload, normed, lowrank, queries, keys, values, attended, out_rank, router_wide = attention_forward(
        scalars, inputs, g1, g2, cosine, sine, routes, router_weight, weights
    )
    row_blocks = gather_blocks(payload)
    expert_weights = [
        expert_input_first_factors,
        expert_input_weight,
        expert_input_second_factors,
        expert_down_first_factors,
        expert_down_weight,
        expert_down_second_factors,
    ]
    dp_stages = [("dp", bit) for bit in range(axis_bits("dp"))]
    carried = None
    sums = []
    for local in range(EXP_DEV):
        number = jnp.stack([EXP_DEV * place + local, dp_side]).astype(jnp.int32)
        for older in sums[: max(local - 1, 0)]:
            older.got, number = tie(older.got, number)
            older.advance()
        *carried, mine, send = expert_call(
            local,
            number,
            row_blocks,
            grad_blocks,
            expert_weights,
            carried,
            router_wide if local == EXP_DEV - 1 else None,
            experts,
        )
        sums.append(Sum(mine, send, dp_stages))
    mixture_part, row_part = carried
    row_mine, row_got = return_stages(row_part)
    grad_input, att_mine, att_send = attention_backward(
        scalars,
        [inputs, g1, g2, cosine, sine, hidden, row_mine, row_got, output_gradient]
        + [normed, lowrank, queries, keys, values, attended, out_rank],
        weights,
    )
    mix_mine, mix_got = return_stages(mixture_part)
    live = (jnp.arange(TOK_DEV, dtype=jnp.int32) < lengths[0]).astype(F32)[:, None]
    output = (live * (hidden + mix_mine.astype(F32) + mix_got.astype(F32))).astype(BF)
    stages = [("expert", bit) for bit in range(axis_bits("expert"))] + dp_stages
    attention_sum = Sum(att_mine, att_send, stages).finish()
    pieces = [piece for one in sums for piece in one.finish()]
    expert_grads = expert_finish(dp_side[None].astype(jnp.int32), pieces)
    attention_grads = attention_finish(core_side[None].astype(jnp.int32), *attention_sum)
    return (output, grad_input, *attention_grads, *expert_grads)


def solution(mesh):
    rows = P(("dp", "expert"), None)
    each = P(("dp", "expert"))
    three = P("expert", None, None)
    four = P("expert", None, None, None)
    return jax.shard_map(
        on_device,
        mesh=mesh,
        in_specs=(
            (rows, each, rows, each)
            + (P(),) * 6
            + (three, three)
            + (P(),) * 5
            + (three, four, three, three, rows)
        ),
        out_specs=(rows, rows) + (P(),) * 5 + (three, four, three, three),
        check_vma=False,
    )
```

time: 445 us -> 337 us (0.76)
  local copies, waits for them, and re-layouts: 66.8 us -> 10.2 us
  Pallas kernels: 84.9 us -> 134 us
  other arithmetic: 47.9 us -> 10.6 us
  matrix products: 28.5 us -> 0 us
  waiting for transfers between devices: 156 us -> 130 us
  starting transfers between devices: 49 us -> 43.6 us
    pallas_call x4 -> x8, Pallas kernels: 84.9 us -> 134 us  [the longest x4 92.4 us: expert_call(): pl.pallas_call(functools.partial(expert_body, expert=expert, first=first,...]
    dot_general x31 -> x0, matrix products: 28.5 us -> none  [the longest x1 3.6 us: on_device(): jnp.einsum('qjgd,kjd->jgqk', grad_heads, value_heads, preferred_element_t...]
    ppermute x43, waiting for transfers between devices: 156 us -> 130 us  [swap(): return lax.ppermute(values, axis, [(i, i ^ 1 << bit) for i in range(size)])]
    unnamed x170 -> x48, local copies, waits for them, and re-layouts: 30 us -> 6.51 us
    mul x6 -> x0, local copies, waits for them, and re-layouts: 11.9 us -> none  [the longest x4 7.31 us: rotate(): head_values * cosine_table[:, None, :] + turned * sine_table[:, None, :]]
    concatenate x12 -> x11, other arithmetic: 7.83 us -> 1.07 us  [advance(): self.values = jnp.concatenate([low, high], axis=0)]
    convert_element_type x29 -> x21, other arithmetic: 11.5 us -> 4.9 us  [the longest x12 2.92 us: advance(): values = (self.mine.astype(F32) + self.got.astype(F32)).astype(BF)]
    select_n x16 -> x11, other arithmetic: 8.09 us -> 1.87 us  [advance(): low = jnp.where(side == 0, self.values, self.got)]
  transfers between devices with their start and end apart: 43 -> 43, of which waited for: 25 -> 18; matrix products, arithmetic and copies ran while one was open for 15% -> 4% of each run, Pallas kernels for 0% -> 30%
where the time goes in v2:
time: 337 us; the launch traced here: 331 us
  Pallas kernels  134 us (40%)
  waiting for transfers between devices  130 us (39%)
  starting transfers between devices  43.6 us (13%)
  other arithmetic  10.6 us (3%)
  local copies, waits for them, and re-layouts  10.2 us (3%)
    ppermute x43, waiting for transfers between devices, swap(): return lax.ppermute(values, axis, [(i, i ^ 1 << bit) for i in range(size)])  130 us
    pallas_call x4, Pallas kernels, expert_call(): pl.pallas_call(functools.partial(expert_body, expert=expert, first=first,...  92.4 us
    ppermute x43, starting transfers between devices, swap(): return lax.ppermute(values, axis, [(i, i ^ 1 << bit) for i in range(size)])  43.6 us
    pallas_call x1, Pallas kernels, attention_backward(): pl.pallas_call(backward_body, out_shape=[shape(TOK_DEV, MODEL_WIDTH, dtyp...  20.4 us
    pallas_call x1, Pallas kernels, attention_forward(): pl.pallas_call(functools.partial(forward_body, experts=experts), out_shap...  10.8 us
  transfers between devices with their start and end apart: 43, of which 18 were waited for; matrix products, arithmetic and copies ran while one was open for 4% of the time, Pallas kernels for 30%

profile of v2, /device:TPU:0, one launch (start us, length us, event | category | flops | bytes accessed | tf_op | source)
XLA Modules:
  0.0 331.0 jit_solution(3097255546422589759)
XLA Ops:
  1.9 1.5 copy.35.routes_ref
  3.4 1.6 copy.36.router_ref
  5.7 10.8 %attention_forward.1 = (f32[256,1024]{1,0:T(8,128)}, bf16[256,1152]{1,0:T(8,128)(2,1)}, bf16[256,1024]{1,0:T(8,128)(2,1)}, bf16[256,384]{1,0:T(8,128)(2,1)}, bf1...) custom-call(s32[3]{0:T(128)} %pad_add_fusion.scalars, ...), custom_call_target="tpu_custom_call" | custom-call | flops 3000000000 | bytes 20000000 | tf_op jit(solution)/shard_map/attention_forward/pallas_call | solution.py:181
  16.5 3.0 collective-permute-start
  19.6 14.3 %collective-permute-done.refs_1_ = bf16[256,1152]{1,0:T(8,128)(2,1)S(1)} collective-permute-done((bf16[256,1152]{1,0:T(8,128)(2,1)}, bf16[256,1152]{1,0:T(8,128)(2,1)S(1)}, u32[]{:S(2)}, u32[]{:S(2)}) %collective-permute-start) | collective-permute-done | bytes 589856 | tf_op jit(solution)/shard_map/ppermute | solution.py:575
  34.5 9.9 %collective-permute-done.3.refs_5_ = bf16[256,1024]{1,0:T(8,128)(2,1)S(1)} collective-permute-done((bf16[256,1024]{1,0:T(8,128)(2,1)S(1)}, bf16[256,1024]{1,0:T(8,128)(2,1)S(1)}, u32[]{:S(2)}, u32[]{:S(2)}) %collective-permute-start.3) | collective-permute-done | bytes 524320 | tf_op jit(solution)/shard_map/ppermute | solution.py:575
  47.4 21.5 %expert_step.4 = (f32[1024,1024]{1,0:T(8,128)}, f32[1024,1024]{1,0:T(8,128)}, f32[1024,128]{1,0:T(8,128)}, bf16[288,1024]{1,0:T(8,128)(2,1)}, bf16[288,1024]{1,0:T(8,128)(2,1)}) custom-call(s32[2]{0:T(128)} %get-tuple-element.130.scalars, bf16[256,1152]{1,0:T(8,128)(2,1)} %get-tuple-element.59.refs_0_, bf16[256,1152]{1,0:T(8,128)(2,1)} %copy-done.16, ...), custom_call_target="tpu_custom_call" | custom-call | flops 10035200000 | bytes 20000000 | tf_op jit(solution)/shard_map/expert_step/pallas_call | solution.py:486
  69.0 1.8 collective-permute-start.7
  70.8 23.4 %expert_step.5 = (f32[1024,1024]{1,0:T(8,128)}, f32[1024,1024]{1,0:T(8,128)}, f32[1024,128]{1,0:T(8,128)}, bf16[288,1024]{1,0:T(8,128)(2,1)}, bf16[288,1024]{1,0:T(8,128)(2,1)}) custom-call(s32[2]{0:T(128)} %get-tuple-element.129.scalars, bf16[256,1152]{1,0:T(8,128)(2,1)} %get-tuple-element.59.refs_0_, bf16[256,1152]{1,0:T(8,128)(2,1)} %copy-done.16, ...), custom_call_target="tpu_custom_call" | custom-call | flops 10035200000 | bytes 20000000 | tf_op jit(solution)/shard_map/expert_step/pallas_call | solution.py:486
  94.8 1.9 collective-permute-start.8
  96.7 23.3 %expert_step.6 = (f32[1024,1024]{1,0:T(8,128)}, f32[1024,1024]{1,0:T(8,128)}, f32[1024,128]{1,0:T(8,128)}, bf16[288,1024]{1,0:T(8,128)(2,1)}, bf16[288,1024]{1,0:T(8,128)(2,1)}) custom-call(s32[2]{0:T(128)} %pad_add_fusion.3.scalars, bf16[256,1152]{1,0:T(8,128)(2,1)} %get-tuple-element.59.refs_0_, bf16[256,1152]{1,0:T(8,128)(2,1)} %copy-done.16, ...), custom_call_target="tpu_custom_call" | custom-call | flops 10035200000 | bytes 20000000 | tf_op jit(solution)/shard_map/expert_step/pallas_call | solution.py:486
  120.1 1.6 collective-permute-start.31
  121.8 2.7 collective-permute-start.22
  125.2 24.2 %expert_step.7 = (bf16[1024,1024]{1,0:T(8,128)(2,1)}, bf16[1024,1024]{1,0:T(8,128)(2,1)}, bf16[288,1024]{1,0:T(8,128)(2,1)}, bf16[288,1024]{1,0:T(8,128)(2,1)}) custom-call(s32[2]{0:T(128)} %pad_add_fusion.4.scalars, bf16[256,1152]{1,0:T(8,128)(2,1)} %get-tuple-element.59.refs_0_, bf16[256,1152]{1,0:T(8,128)(2,1)} %copy-done.16, ...), custom_call_target="tpu_custom_call" | custom-call | flops 10035200000 | bytes 20000000 | tf_op jit(solution)/shard_map/expert_step/pallas_call | solution.py:486
  149.4 2.4 slice.25
  153.3 9.4 %collective-permute-done.23 = bf16[72,1024]{1,0:T(8,128)(2,1)S(1)} collective-permute-done((bf16[72,1024]{1,0:T(8,128)(2,1)S(1)}, bf16[72,1024]{1,0:T(8,128)(2,1)S(1)}, u32[]{:S(2)}, u32[]{:S(2)}) %collective-permute-start.23) | collective-permute-done | bytes 147488 | tf_op jit(solution)/shard_map/ppermute | solution.py:575
  162.8 1.8 collective-permute-start.24
  164.9 6.3 %collective-permute-done.27 = bf16[72,1024]{1,0:T(8,128)(2,1)S(1)} collective-permute-done((bf16[72,1024]{1,0:T(8,128)(2,1)S(1)}, bf16[72,1024]{1,0:T(8,128)(2,1)S(1)}, u32[]{:S(2)}, u32[]{:S(2)}) %collective-permute-start.27) | collective-permute-done | bytes 147488 | tf_op jit(solution)/shard_map/ppermute | solution.py:575
  171.3 4.4 %collective-permute-done.24 = bf16[144,1024]{1,0:T(8,128)(2,1)S(1)} collective-permute-done((bf16[144,1024]{1,0:T(8,128)(2,1)S(1)}, bf16[144,1024]{1,0:T(8,128)(2,1)S(1)}, u32[]{:S(2)}, u32[]{:S(2)}) %collective-permute-start.24) | collective-permute-done | bytes 294944 | tf_op jit(solution)/shard_map/ppermute | solution.py:575
  175.8 1.6 collective-permute-start.25
  178.7 6.0 %collective-permute-done.28 = bf16[72,1024]{1,0:T(8,128)(2,1)S(1)} collective-permute-done((bf16[72,1024]{1,0:T(8,128)(2,1)S(1)}, bf16[72,1024]{1,0:T(8,128)(2,1)S(1)}, u32[]{:S(2)}, u32[]{:S(2)}) %collective-permute-start.28) | collective-permute-done | bytes 147488 | tf_op jit(solution)/shard_map/ppermute | solution.py:575
  184.8 1.5 collective-permute-start.12
  187.1 7.5 %collective-permute-done.12.got_ref = bf16[256,1024]{1,0:T(8,128)(2,1)S(1)} collective-permute-done((bf16[256,1024]{1,0:T(8,128)(2,1)S(1)}, bf16[256,1024]{1,0:T(8,128)(2,1)S(1)}, u32[]{:S(2)}, u32[]{:S(2)}) %collective-permute-start.12) | collective-permute-done | bytes 524320 | tf_op jit(solution)/shard_map/ppermute | solution.py:575
  195.4 20.4 %attention_backward.1 = (f32[256,1024]{1,0:T(8,128)}, bf16[448,1024]{1,0:T(8,128)(2,1)}, bf16[448,1024]{1,0:T(8,128)(2,1)}) custom-call(s32[3]{0:T(128)} %pad_add_fusion.scalars, bf16[256,1024]{1,0:T(8,128)(2,1)} %x_ref.3, f32[1,1024]{1,0:T(1,128)} %bitcast.99, f32[1,1024]{1,0:T(1,128)} %bitcast.101, f32[256,128]{1,0:T(8,128)} %constant.81.clone.cos_ref, ...), custom_call_target="tpu_custom_call" | custom-call | flops 6000000000 | bytes 24000000 | tf_op jit(solution)/shard_map/attention_backward/pallas_call | solution.py:297
  215.9 3.4 %collective-permute-start.33 = (bf16[72,1024]{1,0:T(8,128)(2,1)S(1)}, bf16[72,1024]{1,0:T(8,128)(2,1)S(1)}, u32[]{:S(2)}, u32[]{:S(2)}) collective-permute-start(bf16[72,1024]{1,0:T(8,128)(2,1)S(1)} %dynamic-slice_bitcast_fusion.7), channel_id=1, source_target_pairs={{0,16},{4,20},{8,24},{12,28},{16,0},{20,4},{24,8},{28,12},{1,17},{... | collective-permute-start | bytes 442376 | tf_op jit(solution)/shard_map/ppermute | solution.py:575
  220.8 6.2 %collective-permute-done.33 = bf16[72,1024]{1,0:T(8,128)(2,1)S(1)} collective-permute-done((bf16[72,1024]{1,0:T(8,128)(2,1)S(1)}, bf16[72,1024]{1,0:T(8,128)(2,1)S(1)}, u32[]{:S(2)}, u32[]{:S(2)}) %collective-permute-start.33) | collective-permute-done | bytes 147488 | tf_op jit(solution)/shard_map/ppermute | solution.py:575
  227.1 2.7 collective-permute-start.34
  231.3 1.6 collective-permute-start.14
  232.9 6.1 %collective-permute-done.38 = bf16[144,1024]{1,0:T(8,128)(2,1)S(1)} collective-permute-done((bf16[144,1024]{1,0:T(8,128)(2,1)S(1)}, bf16[144,1024]{1,0:T(8,128)(2,1)S(1)}, u32[]{:S(2)}, u32[]{:S(2)}) %collective-permute-start.38) | collective-permute-done | bytes 294944 | tf_op jit(solution)/shard_map/ppermute | solution.py:575
  239.0 1.5 collective-permute-start.30
  240.6 2.5 collective-permute-done.14
  243.9 1.5 collective-permute-start.15
  245.5 12.7 %collective-permute-done.15 = bf16[112,1024]{1,0:T(8,128)(2,1)S(1)} collective-permute-done((bf16[112,1024]{1,0:T(8,128)(2,1)S(1)}, bf16[112,1024]{1,0:T(8,128)(2,1)S(1)}, u32[]{:S(2)}, u32[]{:S(2)}) %collective-permute-start.15) | collective-permute-done | bytes 229408 | tf_op jit(solution)/shard_map/ppermute | solution.py:575
  258.4 5.1 %collective-permute-done.16 = bf16[56,1024]{1,0:T(8,128)(2,1)S(1)} collective-permute-done((bf16[56,1024]{1,0:T(8,128)(2,1)S(1)}, bf16[56,1024]{1,0:T(8,128)(2,1)S(1)}, u32[]{:S(2)}, u32[]{:S(2)}) %collective-permute-start.16) | collective-permute-done | bytes 114720 | tf_op jit(solution)/shard_map/ppermute | solution.py:575
  263.6 2.7 collective-permute-start.17
  266.3 3.9 %collective-permute-done.17 = bf16[56,1024]{1,0:T(8,128)(2,1)S(1)} collective-permute-done((bf16[56,1024]{1,0:T(8,128)(2,1)S(1)}, bf16[56,1024]{1,0:T(8,128)(2,1)S(1)}, u32[]{:S(2)}, u32[]{:S(2)}) %collective-permute-start.17) | collective-permute-done | bytes 114720 | tf_op jit(solution)/shard_map/ppermute | solution.py:575
  270.1 3.4 %collective-permute-start.40 = (bf16[72,1024]{1,0:T(8,128)(2,1)S(1)}, bf16[72,1024]{1,0:T(8,128)(2,1)S(1)}, u32[]{:S(2)}, u32[]{:S(2)}) collective-permute-start(bf16[72,1024]{1,0:T(8,128)(2,1)S(1)} %fusion.6), channel_id=1, source_target_pairs={{0,16},{4,20},{8,24},{12,28},{16,0},{20,4},{24,8},{28,12},{1,17},{... | collective-permute-start | bytes 442376 | tf_op jit(solution)/shard_map/ppermute | solution.py:575
  274.1 4.3 %collective-permute-done.18 = bf16[56,1024]{1,0:T(8,128)(2,1)S(1)} collective-permute-done((bf16[56,1024]{1,0:T(8,128)(2,1)S(1)}, bf16[56,1024]{1,0:T(8,128)(2,1)S(1)}, u32[]{:S(2)}, u32[]{:S(2)}) %collective-permute-start.18) | collective-permute-done | bytes 114720 | tf_op jit(solution)/shard_map/ppermute | solution.py:575
  278.5 1.4 collective-permute-start.10
  280.0 1.6 collective-permute-start.19
  281.6 4.5 %collective-permute-done.19 = bf16[112,1024]{1,0:T(8,128)(2,1)S(1)} collective-permute-done((bf16[112,1024]{1,0:T(8,128)(2,1)S(1)}, bf16[112,1024]{1,0:T(8,128)(2,1)S(1)}, u32[]{:S(2)}, u32[]{:S(2)}) %collective-permute-start.19) | collective-permute-done | bytes 229408 | tf_op jit(solution)/shard_map/ppermute | solution.py:575
  286.9 1.5 collective-permute-start.41
  288.6 8.9 %collective-permute-done.20 = bf16[224,1024]{1,0:T(8,128)(2,1)S(1)} collective-permute-done((bf16[224,1024]{1,0:T(8,128)(2,1)S(1)}, bf16[224,1024]{1,0:T(8,128)(2,1)S(1)}, u32[]{:S(2)}, u32[]{:S(2)}) %collective-permute-start.20) | collective-permute-done | bytes 458784 | tf_op jit(solution)/shard_map/ppermute | solution.py:575
  297.5 1.5 collective-permute-start.36
  301.9 11.1 %collective-permute-done.36.refs_5_ = bf16[288,1024]{1,0:T(8,128)(2,1)S(1)} collective-permute-done((bf16[288,1024]{1,0:T(8,128)(2,1)S(1)}, bf16[288,1024]{1,0:T(8,128)(2,1)S(1)}, u32[]{:S(2)}, u32[]{:S(2)}) %collective-permute-start.36) | collective-permute-done | bytes 589856 | tf_op jit(solution)/shard_map/ppermute | solution.py:575
  313.9 6.7 %collective-permute-done.42.refs_7_ = bf16[288,1024]{1,0:T(8,128)(2,1)} collective-permute-done((bf16[288,1024]{1,0:T(8,128)(2,1)S(1)}, bf16[288,1024]{1,0:T(8,128)(2,1)}, u32[]{:S(2)}, u32[]{:S(2)}) %collective-permute-start.42) | collective-permute-done | bytes 589856 | tf_op jit(solution)/shard_map/ppermute | solution.py:575
  320.6 6.5 %expert_finish.1 = (f32[4,1024,256]{2,1,0:T(8,128)}, f32[4,2,128,512]{3,2,1,0:T(8,128)}, f32[4,512,128]{2,1,0:T(8,128)}, f32[4,128,1024]{2,1,0:T(8,128)}) custom-call(s32[1]{0:T(128)} %bitcast.5.scalars, bf16[288,1024]{1,0:T(8,128)(2,1)} %copy-done.1, bf16[288,1024]{1,0:T(8,128)(2,1)} %copy-done.9, bf16[288,1024]{1,0:T(8,128)(2,1)} %copy-done.2, ...), custom_call_target="tpu_custom_call" | custom-call | flops 1000000 | bytes 15000000 | tf_op jit(solution)/shard_map/expert_finish/pallas_call | solution.py:526
  327.1 3.7 %attention_finish.1 = (f32[1024,384]{1,0:T(8,128)}, f32[128,1024]{1,0:T(8,128)}, f32[2,128,512]{2,1,0:T(8,128)}, f32[1024,128]{1,0:T(8,128)}, f32[128,1024]{1,0:T(8,128)}) custom-call(s32[1]{0:T(128)} %bitcast.1.scalars, bf16[448,1024]{1,0:T(8,128)(2,1)} %copy-done, bf16[448,1024]{1,0:T(8,128)(2,1)} %collective-permute-done.21.got_ref), custom_call_target="tpu_custom_call" | custom-call | flops 1000000 | bytes 6000000 | tf_op jit(solution)/shard_map/attention_finish/pallas_call | solution.py:561
  (156 shorter events, 20.2 us)
Async XLA Ops:
  16.5 17.4 %collective-permute-start = (bf16[256,1152]{1,0:T(8,128)(2,1)}, bf16[256,1152]{1,0:T(8,128)(2,1)S(1)}, u32[]{:S(2)}, u32[]{:S(2)}) collective-permute-start(bf16[256,1152]{1,0:T(8,128)(2,1)} %get-tuple-element.59.refs_0_), channel_id=1, source_target_pairs={{0,2},{1,3},{2,0},{3,1},{4,6},{5,7},{6,4},{7,5},{8,10},{9,11},{10,... | collective-permute-start | bytes 1769480 | tf_op jit(solution)/shard_map/ppermute | solution.py:575
  19.6 24.8 %collective-permute-start.3 = (bf16[256,1024]{1,0:T(8,128)(2,1)S(1)}, bf16[256,1024]{1,0:T(8,128)(2,1)S(1)}, u32[]{:S(2)}, u32[]{:S(2)}) collective-permute-start(bf16[256,1024]{1,0:T(8,128)(2,1)S(1)} %copy-done.20), channel_id=1, source_target_pairs={{0,2},{1,3},{2,0},{3,1},{4,6},{5,7},{6,4},{7,5},{8,10},{9,11},{10,... | collective-permute-start | bytes 1572872 | tf_op jit(solution)/shard_map/ppermute | solution.py:575
  19.6 26.8 %collective-permute-start.1 = (bf16[256,1152]{1,0:T(8,128)(2,1)}, bf16[256,1152]{1,0:T(8,128)(2,1)S(1)}, u32[]{:S(2)}, u32[]{:S(2)}) collective-permute-start(bf16[256,1152]{1,0:T(8,128)(2,1)} %get-tuple-element.59.refs_0_), channel_id=1, source_target_pairs={{0,1},{1,0},{2,3},{3,2},{4,5},{5,4},{6,7},{7,6},{8,9},{9,8},{10,11... | collective-permute-start | bytes 1769480 | tf_op jit(solution)/shard_map/ppermute | solution.py:575
  33.9 12.5 %collective-permute-start.2 = (bf16[256,1152]{1,0:T(8,128)(2,1)S(1)}, bf16[256,1152]{1,0:T(8,128)(2,1)S(1)}, u32[]{:S(2)}, u32[]{:S(2)}) collective-permute-start(bf16[256,1152]{1,0:T(8,128)(2,1)S(1)} %collective-permute-done.refs_1_), channel_id=1, source_target_pairs={{0,1},{1,0},{2,3},{3,2},{4,5},{5,4},{6,7},{7,6},{8,9},{9,8},{10,11... | collective-permute-start | bytes 1769480 | tf_op jit(solution)/shard_map/ppermute | solution.py:575
  33.9 12.5 %collective-permute-start.4 = (bf16[256,1024]{1,0:T(8,128)(2,1)S(1)}, bf16[256,1024]{1,0:T(8,128)(2,1)}, u32[]{:S(2)}, u32[]{:S(2)}) collective-permute-start(bf16[256,1024]{1,0:T(8,128)(2,1)S(1)} %copy-done.20), channel_id=1, source_target_pairs={{0,1},{1,0},{2,3},{3,2},{4,5},{5,4},{6,7},{7,6},{8,9},{9,8},{10,11... | collective-permute-start | bytes 1572872 | tf_op jit(solution)/shard_map/ppermute | solution.py:575
  44.3 2.1 collective-permute-start.5
  69.0 25.6 %collective-permute-start.7 = (bf16[288,1024]{1,0:T(8,128)(2,1)}, bf16[288,1024]{1,0:T(8,128)(2,1)S(1)}, u32[]{:S(2)}, u32[]{:S(2)}) collective-permute-start(bf16[288,1024]{1,0:T(8,128)(2,1)} %get-tuple-element.65), channel_id=1, source_target_pairs={{0,4},{4,0},{8,12},{12,8},{16,20},{20,16},{24,28},{28,24},{1,5},{5... | collective-permute-start | bytes 1769480 | tf_op jit(solution)/shard_map/ppermute | solution.py:575
  70.8 23.7 %copy-start.15 = (bf16[288,1024]{1,0:T(8,128)(2,1)S(1)}, bf16[288,1024]{1,0:T(8,128)(2,1)}, u32[]{:S(2)}) copy-start(bf16[288,1024]{1,0:T(8,128)(2,1)} %get-tuple-element.64) | copy-start | bytes 1769476
  94.2 27.4 %collective-permute-start.6 = (bf16[288,1024]{1,0:T(8,128)(2,1)}, bf16[288,1024]{1,0:T(8,128)(2,1)S(1)}, u32[]{:S(2)}, u32[]{:S(2)}) collective-permute-start(bf16[288,1024]{1,0:T(8,128)(2,1)} %get-tuple-element.63), channel_id=1, source_target_pairs={{0,4},{4,0},{8,12},{12,8},{16,20},{20,16},{24,28},{28,24},{1,5},{5... | collective-permute-start | bytes 1769480 | tf_op jit(solution)/shard_map/ppermute | solution.py:575
  94.8 26.8 %collective-permute-start.8 = (bf16[144,1024]{1,0:T(8,128)(2,1)S(1)}, bf16[144,1024]{1,0:T(8,128)(2,1)S(1)}, u32[]{:S(2)}, u32[]{:S(2)}) collective-permute-start(bf16[144,1024]{1,0:T(8,128)(2,1)S(1)} %dynamic-slice_bitcast_fusion.4), channel_id=1, source_target_pairs={{0,8},{4,12},{8,0},{12,4},{16,24},{20,28},{24,16},{28,20},{1,9},{5... | collective-permute-start | bytes 884744 | tf_op jit(solution)/shard_map/ppermute | solution.py:575
  96.7 27.7 %copy-start.14 = (bf16[288,1024]{1,0:T(8,128)(2,1)S(1)}, bf16[288,1024]{1,0:T(8,128)(2,1)}, u32[]{:S(2)}) copy-start(bf16[288,1024]{1,0:T(8,128)(2,1)} %get-tuple-element.95) | copy-start | bytes 1769476
  120.1 42.7 %collective-permute-start.31 = (bf16[288,1024]{1,0:T(8,128)(2,1)}, bf16[288,1024]{1,0:T(8,128)(2,1)S(1)}, u32[]{:S(2)}, u32[]{:S(2)}) collective-permute-start(bf16[288,1024]{1,0:T(8,128)(2,1)} %get-tuple-element.98), channel_id=1, source_target_pairs={{0,4},{4,0},{8,12},{12,8},{16,20},{20,16},{24,28},{28,24},{1,5},{5... | collective-permute-start | bytes 1769480 | tf_op jit(solution)/shard_map/ppermute | solution.py:575
  121.8 30.7 %collective-permute-start.22 = (bf16[72,1024]{1,0:T(8,128)(2,1)S(1)}, bf16[72,1024]{1,0:T(8,128)(2,1)S(1)}, u32[]{:S(2)}, u32[]{:S(2)}) collective-permute-start(bf16[72,1024]{1,0:T(8,128)(2,1)S(1)} %dynamic-slice_bitcast_fusion.9), channel_id=1, source_target_pairs={{0,16},{4,20},{8,24},{12,28},{16,0},{20,4},{24,8},{28,12},{1,17},{... | collective-permute-start | bytes 442376 | tf_op jit(solution)/shard_map/ppermute | solution.py:575
  124.7 28.4 %collective-permute-start.26 = (bf16[144,1024]{1,0:T(8,128)(2,1)S(1)}, bf16[144,1024]{1,0:T(8,128)(2,1)S(1)}, u32[]{:S(2)}, u32[]{:S(2)}) collective-permute-start(bf16[144,1024]{1,0:T(8,128)(2,1)S(1)} %dynamic-slice_bitcast_fusion.3), channel_id=1, source_target_pairs={{0,8},{4,12},{8,0},{12,4},{16,24},{20,28},{24,16},{28,20},{1,9},{5... | collective-permute-start | bytes 884744 | tf_op jit(solution)/shard_map/ppermute | solution.py:575
  151.8 121.8 %collective-permute-start.9 = (bf16[512,1024]{1,0:T(8,128)(2,1)}, bf16[512,1024]{1,0:T(8,128)(2,1)S(1)}, u32[]{:S(2)}, u32[]{:S(2)}) collective-permute-start(bf16[512,1024]{1,0:T(8,128)(2,1)} %slice.25), channel_id=1, source_target_pairs={{0,1},{1,0},{2,3},{3,2},{4,5},{5,4},{6,7},{7,6},{8,9},{9,8},{10,11... | collective-permute-start | bytes 3145736 | tf_op jit(solution)/shard_map/ppermute | solution.py:575
  151.9 23.9 %collective-permute-start.11 = (bf16[512,1024]{1,0:T(8,128)(2,1)S(1)}, bf16[512,1024]{1,0:T(8,128)(2,1)S(1)}, u32[]{:S(2)}, u32[]{:S(2)}) collective-permute-start(bf16[512,1024]{1,0:T(8,128)(2,1)S(1)} %slice.29), channel_id=1, source_target_pairs={{0,1},{1,0},{2,3},{3,2},{4,5},{5,4},{6,7},{7,6},{8,9},{9,8},{10,11... | collective-permute-start | bytes 3145736 | tf_op jit(solution)/shard_map/ppermute | solution.py:575
  152.5 63.4 %collective-permute-start.37 = (bf16[288,1024]{1,0:T(8,128)(2,1)S(1)}, bf16[288,1024]{1,0:T(8,128)(2,1)}, u32[]{:S(2)}, u32[]{:S(2)}) collective-permute-start(bf16[288,1024]{1,0:T(8,128)(2,1)S(1)} %copy-done.19), channel_id=1, source_target_pairs={{0,4},{4,0},{8,12},{12,8},{16,20},{20,16},{24,28},{28,24},{1,5},{5... | collective-permute-start | bytes 1769480 | tf_op jit(solution)/shard_map/ppermute | solution.py:575
  153.0 9.7 %collective-permute-start.23 = (bf16[72,1024]{1,0:T(8,128)(2,1)S(1)}, bf16[72,1024]{1,0:T(8,128)(2,1)S(1)}, u32[]{:S(2)}, u32[]{:S(2)}) collective-permute-start(bf16[72,1024]{1,0:T(8,128)(2,1)S(1)} %fusion.9), channel_id=1, source_target_pairs={{0,16},{4,20},{8,24},{12,28},{16,0},{20,4},{24,8},{28,12},{1,17},{... | collective-permute-start | bytes 442376 | tf_op jit(solution)/shard_map/ppermute | solution.py:575
  162.7 8.5 %collective-permute-start.27 = (bf16[72,1024]{1,0:T(8,128)(2,1)S(1)}, bf16[72,1024]{1,0:T(8,128)(2,1)S(1)}, u32[]{:S(2)}, u32[]{:S(2)}) collective-permute-start(bf16[72,1024]{1,0:T(8,128)(2,1)S(1)} %dynamic-slice_bitcast_fusion.8), channel_id=1, source_target_pairs={{0,16},{4,20},{8,24},{12,28},{16,0},{20,4},{24,8},{28,12},{1,17},{... | collective-permute-start | bytes 442376 | tf_op jit(solution)/shard_map/ppermute | solution.py:575
  162.8 12.8 %collective-permute-start.24 = (bf16[144,1024]{1,0:T(8,128)(2,1)S(1)}, bf16[144,1024]{1,0:T(8,128)(2,1)S(1)}, u32[]{:S(2)}, u32[]{:S(2)}) collective-permute-start(bf16[144,1024]{1,0:T(8,128)(2,1)S(1)} %pad_maximum_fusion.6), channel_id=1, source_target_pairs={{0,8},{4,12},{8,0},{12,4},{16,24},{20,28},{24,16},{28,20},{1,9},{5... | collective-permute-start | bytes 884744 | tf_op jit(solution)/shard_map/ppermute | solution.py:575
  171.2 15.8 %collective-permute-start.32 = (bf16[144,1024]{1,0:T(8,128)(2,1)S(1)}, bf16[144,1024]{1,0:T(8,128)(2,1)S(1)}, u32[]{:S(2)}, u32[]{:S(2)}) collective-permute-start(bf16[144,1024]{1,0:T(8,128)(2,1)S(1)} %dynamic-slice_bitcast_fusion.2), channel_id=1, source_target_pairs={{0,8},{4,12},{8,0},{12,4},{16,24},{20,28},{24,16},{28,20},{1,9},{5... | collective-permute-start | bytes 884744 | tf_op jit(solution)/shard_map/ppermute | solution.py:575
  175.6 9.1 %collective-permute-start.28 = (bf16[72,1024]{1,0:T(8,128)(2,1)S(1)}, bf16[72,1024]{1,0:T(8,128)(2,1)S(1)}, u32[]{:S(2)}, u32[]{:S(2)}) collective-permute-start(bf16[72,1024]{1,0:T(8,128)(2,1)S(1)} %fusion.8), channel_id=1, source_target_pairs={{0,16},{4,20},{8,24},{12,28},{16,0},{20,4},{24,8},{28,12},{1,17},{... | collective-permute-start | bytes 442376 | tf_op jit(solution)/shard_map/ppermute | solution.py:575
  175.8 126.1 %collective-permute-start.25 = (bf16[288,1024]{1,0:T(8,128)(2,1)S(1)}, bf16[288,1024]{1,0:T(8,128)(2,1)S(1)}, u32[]{:S(2)}, u32[]{:S(2)}) collective-permute-start(bf16[288,1024]{1,0:T(8,128)(2,1)S(1)} %pad_maximum_fusion.1.refs_0_), channel_id=1, source_target_pairs={{0,4},{4,0},{8,12},{12,8},{16,20},{20,16},{24,28},{28,24},{1,5},{5... | collective-permute-start | bytes 1769480 | tf_op jit(solution)/shard_map/ppermute | solution.py:575
  184.8 9.9 %collective-permute-start.12 = (bf16[256,1024]{1,0:T(8,128)(2,1)S(1)}, bf16[256,1024]{1,0:T(8,128)(2,1)S(1)}, u32[]{:S(2)}, u32[]{:S(2)}) collective-permute-start(bf16[256,1024]{1,0:T(8,128)(2,1)S(1)} %get-tuple-element.105), channel_id=1, source_target_pairs={{0,2},{1,3},{2,0},{3,1},{4,6},{5,7},{6,4},{7,5},{8,10},{9,11},{10,... | collective-permute-start | bytes 1572872 | tf_op jit(solution)/shard_map/ppermute | solution.py:575
  187.0 40.0 %collective-permute-start.29 = (bf16[144,1024]{1,0:T(8,128)(2,1)}, bf16[144,1024]{1,0:T(8,128)(2,1)}, u32[]{:S(2)}, u32[]{:S(2)}) collective-permute-start(bf16[144,1024]{1,0:T(8,128)(2,1)} %pad_maximum_fusion.7), channel_id=1, source_target_pairs={{0,8},{4,12},{8,0},{12,4},{16,24},{20,28},{24,16},{28,20},{1,9},{5... | collective-permute-start | bytes 884744 | tf_op jit(solution)/shard_map/ppermute | solution.py:575
  195.4 24.0 %copy-start.12 = (bf16[288,1024]{1,0:T(8,128)(2,1)S(1)}, bf16[288,1024]{1,0:T(8,128)(2,1)}, u32[]{:S(2)}) copy-start(bf16[288,1024]{1,0:T(8,128)(2,1)} %get-tuple-element.99) | copy-start | bytes 1769476
  215.8 15.0 %collective-permute-start.13 = (bf16[448,1024]{1,0:T(8,128)(2,1)}, bf16[448,1024]{1,0:T(8,128)(2,1)S(1)}, u32[]{:S(2)}, u32[]{:S(2)}) collective-permute-start(bf16[448,1024]{1,0:T(8,128)(2,1)} %get-tuple-element.88), channel_id=1, source_target_pairs={{0,1},{1,0},{2,3},{3,2},{4,5},{5,4},{6,7},{7,6},{8,9},{9,8},{10,11... | collective-permute-start | bytes 2752520 | tf_op jit(solution)/shard_map/ppermute | solution.py:575
  215.9 11.1 %collective-permute-start.33 = (bf16[72,1024]{1,0:T(8,128)(2,1)S(1)}, bf16[72,1024]{1,0:T(8,128)(2,1)S(1)}, u32[]{:S(2)}, u32[]{:S(2)}) collective-permute-start(bf16[72,1024]{1,0:T(8,128)(2,1)S(1)} %dynamic-slice_bitcast_fusion.7), channel_id=1, source_target_pairs={{0,16},{4,20},{8,24},{12,28},{16,0},{20,4},{24,8},{28,12},{1,17},{... | collective-permute-start | bytes 442376 | tf_op jit(solution)/shard_map/ppermute | solution.py:575
  227.0 12.0 %collective-permute-start.38 = (bf16[144,1024]{1,0:T(8,128)(2,1)S(1)}, bf16[144,1024]{1,0:T(8,128)(2,1)S(1)}, u32[]{:S(2)}, u32[]{:S(2)}) collective-permute-start(bf16[144,1024]{1,0:T(8,128)(2,1)S(1)} %dynamic-slice_bitcast_fusion.1), channel_id=1, source_target_pairs={{0,8},{4,12},{8,0},{12,4},{16,24},{20,28},{24,16},{28,20},{1,9},{5... | collective-permute-start | bytes 884744 | tf_op jit(solution)/shard_map/ppermute | solution.py:575
  227.1 16.8 %collective-permute-start.34 = (bf16[72,1024]{1,0:T(8,128)(2,1)S(1)}, bf16[72,1024]{1,0:T(8,128)(2,1)S(1)}, u32[]{:S(2)}, u32[]{:S(2)}) collective-permute-start(bf16[72,1024]{1,0:T(8,128)(2,1)S(1)} %fusion.7), channel_id=1, source_target_pairs={{0,16},{4,20},{8,24},{12,28},{16,0},{20,4},{24,8},{28,12},{1,17},{... | collective-permute-start | bytes 442376 | tf_op jit(solution)/shard_map/ppermute | solution.py:575
  231.3 11.8 %collective-permute-start.14 = (bf16[224,1024]{1,0:T(8,128)(2,1)S(1)}, bf16[224,1024]{1,0:T(8,128)(2,1)S(1)}, u32[]{:S(2)}, u32[]{:S(2)}) collective-permute-start(bf16[224,1024]{1,0:T(8,128)(2,1)S(1)} %dynamic-slice_bitcast_fusion), channel_id=1, source_target_pairs={{0,2},{1,3},{2,0},{3,1},{4,6},{5,7},{6,4},{7,5},{8,10},{9,11},{10,... | collective-permute-start | bytes 1376264 | tf_op jit(solution)/shard_map/ppermute | solution.py:575
  232.9 25.4 %copy-start.2 = (bf16[288,1024]{1,0:T(8,128)(2,1)}, bf16[288,1024]{1,0:T(8,128)(2,1)S(1)}, u32[]{:S(2)}) copy-start(bf16[288,1024]{1,0:T(8,128)(2,1)S(1)} %pad_maximum_fusion.2.refs_2_) | copy-start | bytes 1769476
  239.0 62.9 %collective-permute-start.30 = (bf16[288,1024]{1,0:T(8,128)(2,1)S(1)}, bf16[288,1024]{1,0:T(8,128)(2,1)S(1)}, u32[]{:S(2)}, u32[]{:S(2)}) collective-permute-start(bf16[288,1024]{1,0:T(8,128)(2,1)S(1)} %pad_maximum_fusion.2.refs_2_), channel_id=1, source_target_pairs={{0,4},{4,0},{8,12},{12,8},{16,20},{20,16},{24,28},{28,24},{1,5},{5... | collective-permute-start | bytes 1769480 | tf_op jit(solution)/shard_map/ppermute | solution.py:575
  243.1 20.5 %collective-permute-start.39 = (bf16[72,1024]{1,0:T(8,128)(2,1)S(1)}, bf16[72,1024]{1,0:T(8,128)(2,1)S(1)}, u32[]{:S(2)}, u32[]{:S(2)}) collective-permute-start(bf16[72,1024]{1,0:T(8,128)(2,1)S(1)} %dynamic-slice_bitcast_fusion.6), channel_id=1, source_target_pairs={{0,16},{4,20},{8,24},{12,28},{16,0},{20,4},{24,8},{28,12},{1,17},{... | collective-permute-start | bytes 442376 | tf_op jit(solution)/shard_map/ppermute | solution.py:575
  243.9 29.8 %copy-start.5 = (bf16[1024,1024]{1,0:T(8,128)(2,1)S(1)}, bf16[1024,1024]{1,0:T(8,128)(2,1)}, u32[]{:S(2)}) copy-start(bf16[1024,1024]{1,0:T(8,128)(2,1)} %get-tuple-element.77) | copy-start | bytes 6291460
  243.9 14.3 %collective-permute-start.15 = (bf16[112,1024]{1,0:T(8,128)(2,1)S(1)}, bf16[112,1024]{1,0:T(8,128)(2,1)S(1)}, u32[]{:S(2)}, u32[]{:S(2)}) collective-permute-start(bf16[112,1024]{1,0:T(8,128)(2,1)S(1)} %dynamic-slice_bitcast_fusion.5), channel_id=1, source_target_pairs={{0,4},{4,0},{8,12},{12,8},{16,20},{20,16},{24,28},{28,24},{1,5},{5... | collective-permute-start | bytes 688136 | tf_op jit(solution)/shard_map/ppermute | solution.py:575
  258.3 5.2 %collective-permute-start.16 = (bf16[56,1024]{1,0:T(8,128)(2,1)S(1)}, bf16[56,1024]{1,0:T(8,128)(2,1)S(1)}, u32[]{:S(2)}, u32[]{:S(2)}) collective-permute-start(bf16[56,1024]{1,0:T(8,128)(2,1)S(1)} %dynamic-slice_bitcast_fusion.10), channel_id=1, source_target_pairs={{0,8},{4,12},{8,0},{12,4},{16,24},{20,28},{24,16},{28,20},{1,9},{5... | collective-permute-start | bytes 344072 | tf_op jit(solution)/shard_map/ppermute | solution.py:575
  263.5 23.3 %collective-permute-start.35 = (bf16[144,1024]{1,0:T(8,128)(2,1)S(1)}, bf16[144,1024]{1,0:T(8,128)(2,1)S(1)}, u32[]{:S(2)}, u32[]{:S(2)}) collective-permute-start(bf16[144,1024]{1,0:T(8,128)(2,1)S(1)} %pad_maximum_fusion.8), channel_id=1, source_target_pairs={{0,8},{4,12},{8,0},{12,4},{16,24},{20,28},{24,16},{28,20},{1,9},{5... | collective-permute-start | bytes 884744 | tf_op jit(solution)/shard_map/ppermute | solution.py:575
  263.6 6.6 %collective-permute-start.17 = (bf16[56,1024]{1,0:T(8,128)(2,1)S(1)}, bf16[56,1024]{1,0:T(8,128)(2,1)S(1)}, u32[]{:S(2)}, u32[]{:S(2)}) collective-permute-start(bf16[56,1024]{1,0:T(8,128)(2,1)S(1)} %fusion.10), channel_id=1, source_target_pairs={{0,16},{4,20},{8,24},{12,28},{16,0},{20,4},{24,8},{28,12},{1,17},{... | collective-permute-start | bytes 344072 | tf_op jit(solution)/shard_map/ppermute | solution.py:575
  270.1 9.8 %collective-permute-start.40 = (bf16[72,1024]{1,0:T(8,128)(2,1)S(1)}, bf16[72,1024]{1,0:T(8,128)(2,1)S(1)}, u32[]{:S(2)}, u32[]{:S(2)}) collective-permute-start(bf16[72,1024]{1,0:T(8,128)(2,1)S(1)} %fusion.6), channel_id=1, source_target_pairs={{0,16},{4,20},{8,24},{12,28},{16,0},{20,4},{24,8},{28,12},{1,17},{... | collective-permute-start | bytes 442376 | tf_op jit(solution)/shard_map/ppermute | solution.py:575
  273.6 4.9 %collective-permute-start.18 = (bf16[56,1024]{1,0:T(8,128)(2,1)S(1)}, bf16[56,1024]{1,0:T(8,128)(2,1)S(1)}, u32[]{:S(2)}, u32[]{:S(2)}) collective-permute-start(bf16[56,1024]{1,0:T(8,128)(2,1)S(1)} %add_convert_fusion.7), channel_id=1, source_target_pairs={{0,8},{4,12},{8,0},{12,4},{16,24},{20,28},{24,16},{28,20},{1,9},{5... | collective-permute-start | bytes 344072 | tf_op jit(solution)/shard_map/ppermute | solution.py:575
  278.5 21.1 %collective-permute-start.10 = (bf16[256,1024]{1,0:T(8,128)(2,1)S(1)}, bf16[256,1024]{1,0:T(8,128)(2,1)S(1)}, u32[]{:S(2)}, u32[]{:S(2)}) collective-permute-start(bf16[256,1024]{1,0:T(8,128)(2,1)S(1)} %slice.33), channel_id=1, source_target_pairs={{0,2},{1,3},{2,0},{3,1},{4,6},{5,7},{6,4},{7,5},{8,10},{9,11},{10,... | collective-permute-start | bytes 1572872 | tf_op jit(solution)/shard_map/ppermute | solution.py:575
  280.0 6.1 %collective-permute-start.19 = (bf16[112,1024]{1,0:T(8,128)(2,1)S(1)}, bf16[112,1024]{1,0:T(8,128)(2,1)S(1)}, u32[]{:S(2)}, u32[]{:S(2)}) collective-permute-start(bf16[112,1024]{1,0:T(8,128)(2,1)S(1)} %pad_maximum_fusion.10), channel_id=1, source_target_pairs={{0,4},{4,0},{8,12},{12,8},{16,20},{20,16},{24,28},{28,24},{1,5},{5... | collective-permute-start | bytes 688136 | tf_op jit(solution)/shard_map/ppermute | solution.py:575
  286.2 11.3 %collective-permute-start.20 = (bf16[224,1024]{1,0:T(8,128)(2,1)S(1)}, bf16[224,1024]{1,0:T(8,128)(2,1)S(1)}, u32[]{:S(2)}, u32[]{:S(2)}) collective-permute-start(bf16[224,1024]{1,0:T(8,128)(2,1)S(1)} %pad_maximum_fusion.5), channel_id=1, source_target_pairs={{0,2},{1,3},{2,0},{3,1},{4,6},{5,7},{6,4},{7,5},{8,10},{9,11},{10,... | collective-permute-start | bytes 1376264 | tf_op jit(solution)/shard_map/ppermute | solution.py:575
  286.9 12.4 %collective-permute-start.41 = (bf16[144,1024]{1,0:T(8,128)(2,1)S(1)}, bf16[144,1024]{1,0:T(8,128)(2,1)S(1)}, u32[]{:S(2)}, u32[]{:S(2)}) collective-permute-start(bf16[144,1024]{1,0:T(8,128)(2,1)S(1)} %pad_maximum_fusion.9), channel_id=1, source_target_pairs={{0,8},{4,12},{8,0},{12,4},{16,24},{20,28},{24,16},{28,20},{1,9},{5... | collective-permute-start | bytes 884744 | tf_op jit(solution)/shard_map/ppermute | solution.py:575
  297.5 15.6 %collective-permute-start.36 = (bf16[288,1024]{1,0:T(8,128)(2,1)S(1)}, bf16[288,1024]{1,0:T(8,128)(2,1)S(1)}, u32[]{:S(2)}, u32[]{:S(2)}) collective-permute-start(bf16[288,1024]{1,0:T(8,128)(2,1)S(1)} %pad_maximum_fusion.3.refs_4_), channel_id=1, source_target_pairs={{0,4},{4,0},{8,12},{12,8},{16,20},{20,16},{24,28},{28,24},{1,5},{5... | collective-permute-start | bytes 1769480 | tf_op jit(solution)/shard_map/ppermute | solution.py:575
  299.3 27.8 %collective-permute-start.21 = (bf16[448,1024]{1,0:T(8,128)(2,1)S(1)}, bf16[448,1024]{1,0:T(8,128)(2,1)}, u32[]{:S(2)}, u32[]{:S(2)}) collective-permute-start(bf16[448,1024]{1,0:T(8,128)(2,1)S(1)} %pad_maximum_fusion.mine_ref), channel_id=1, source_target_pairs={{0,1},{1,0},{2,3},{3,2},{4,5},{5,4},{6,7},{7,6},{8,9},{9,8},{10,11... | collective-permute-start | bytes 2752520 | tf_op jit(solution)/shard_map/ppermute | solution.py:575
  299.6 21.1 %collective-permute-start.42 = (bf16[288,1024]{1,0:T(8,128)(2,1)S(1)}, bf16[288,1024]{1,0:T(8,128)(2,1)}, u32[]{:S(2)}, u32[]{:S(2)}) collective-permute-start(bf16[288,1024]{1,0:T(8,128)(2,1)S(1)} %pad_maximum_fusion.4.refs_6_), channel_id=1, source_target_pairs={{0,4},{4,0},{8,12},{12,8},{16,20},{20,16},{24,28},{28,24},{1,5},{5... | collective-permute-start | bytes 1769480 | tf_op jit(solution)/shard_map/ppermute | solution.py:575
  (18 other events, 130.6 us)

commit v3 on v2

--- a/solution.py
+++ b/solution.py
@@ -159,13 +159,15 @@
         lax.broadcasted_iota(jnp.int32, (experts, LANES), 0)
         == lax.broadcasted_iota(jnp.int32, (experts, LANES), 1), 1.0, 0.0,
     ).astype(BF)
-    wide = nn(router_ref[...], spread).astype(BF)
+    wide = tn(router_ref[...], spread).astype(BF)
     wide_ref[...] = wide
     logits = nn(normed2, wide)
     routes = routes_ref[...]
-    selected = routes[:, 0:1] == lane
-    for k in range(1, routes.shape[1]):
-        selected = selected | (routes[:, k : k + 1] == lane)
+    number = lax.broadcasted_iota(jnp.int32, (LANES, TOK_DEV), 0)
+    named = routes[0:1, :] == number
+    for k in range(1, routes.shape[0]):
+        named = named | (routes[k : k + 1, :] == number)
+    selected = jnp.where(named, 1.0, 0.0).T > 0.5
     top = jnp.max(jnp.where(selected, logits, -1e30), axis=1, keepdims=True)
     chosen = jnp.where(selected, jnp.exp(jnp.minimum(logits - top, 0.0)), 0.0)
     live = lax.broadcasted_iota(jnp.int32, (TOK_DEV, 1), 0) < length
@@ -177,7 +179,7 @@
 
 
 def attention_forward(scalars, x, g1, g2, cosine, sine, routes, router, weights):
-    experts = router.shape[1]
+    experts = router.shape[0]
     return pl.pallas_call(
         functools.partial(forward_body, experts=experts),
         out_shape=[
@@ -313,7 +315,9 @@
     )(scalars, *arrays, *weights)
 
 
-def expert_body(scalars, *refs, expert, first, last, count, experts):
+def expert_body(
+    scalars, *refs, expert, start, count, blocks, experts, carried, seeded, emit, last,
+):
     refs = list(refs)
 
     def take(number):
@@ -324,15 +328,21 @@
     x_blocks = take(count)
     g_blocks = take(count)
     ain_h, win_h, bin_h, adn_h, wdn_h, bdn_h = take(6)
-    if not first:
+    if carried:
         f_in, b_in, c_in = take(3)
+    if start:
+        take(3)
+    seeds = take(4) if seeded else None
     if last:
-        (wr_ref,) = take(1)
-        f_out, b_out = take(2)
+        wr_ref, f_top, f_low, b_top, b_low = take(5)
     else:
         f_out, b_out, c_out = take(3)
-    mine_ref, send_ref = take(2)
+    if emit:
+        emitted = take(4)
+    else:
+        mine_ref, send_ref = take(2)
     xs, gs_buf, ain, win, bin_, adn, wdn, bdn, acc_a, acc_bi, acc_ad, acc_bd, pack, xsem, gsem, wsem = refs
+    sums = [acc_a, acc_bi, acc_ad, acc_bd]
     step = pl.program_id(0)
     slot = lax.rem(step, 2)
     early = [
@@ -353,6 +363,8 @@
         fetch(0)
         for copy in early + late:
             copy.start()
+        for index, total in enumerate(sums):
+            total[...] = seeds[index][...] if seeded else jnp.zeros_like(total)
         for copy in early:
             copy.wait()
 
@@ -396,9 +408,18 @@
     out = nn(active, wdn[...]) + nn(down, bdn[...])
     grad_gate_e = jnp.sum(out * grad, axis=1, keepdims=True)
     weighted = gate_e * out
-    if not first:
-        weighted = weighted + f_in[...].astype(F32)
-    f_out[...] = weighted.astype(f_out.dtype)
+    if carried:
+        weighted = weighted + f_in[...]
+    if last:
+        @pl.when(slot == 0)
+        def _():
+            f_top[...] = weighted.astype(BF)
+
+        @pl.when(slot == 1)
+        def _():
+            f_low[...] = weighted.astype(BF)
+    else:
+        f_out[...] = weighted
     slot_grad = (gate_e * grad).astype(BF)
     grad_down = masked(nt(slot_grad, bdn[...]))
     grad_active = nt(slot_grad, wdn[...]) + nt(grad_down, adn[...])
@@ -408,76 +429,92 @@
     both_grads = jnp.concatenate([gate_grad, up_grad], axis=1)
     rows = nt(both_grads, win[...]) + nt(grad_low, ain[...])
     part = (gate_e * grad_gate_e) * (jnp.where(here, 1.0, 0.0) - gates)
-    if not first:
-        rows = rows + b_in[...].astype(F32)
+    if carried:
+        rows = rows + b_in[...]
         part = part + c_in[...]
     if last:
         rows = rows + nt(part.astype(BF), wr_ref[...])
+
+        @pl.when(slot == 0)
+        def _():
+            b_top[...] = rows.astype(BF)
+
+        @pl.when(slot == 1)
+        def _():
+            b_low[...] = rows.astype(BF)
     else:
         c_out[...] = part
-    b_out[...] = rows.astype(b_out.dtype)
-    grads = [
-        tn(grad_low, x),
-        jnp.concatenate([tn(low_gate, gate_grad), tn(low_up, up_grad)], axis=1),
-        tn(grad_down, active),
-        tn(down, slot_grad),
-    ]
-    sums = [acc_a, acc_bi, acc_ad, acc_bd]
-
-    @pl.when(step == 0)
-    def _():
-        for total, value in zip(sums, grads):
-            total[...] = value
-
-    @pl.when(step > 0)
-    def _():
-        for total, value in zip(sums, grads):
-            total[...] += value
+        b_out[...] = rows
+    acc_a[...] += tn(grad_low, x)
+    acc_bi[:, :HALF_WIDTH] += tn(low_gate, gate_grad)
+    acc_bi[:, HALF_WIDTH:] += tn(low_up, up_grad)
+    acc_ad[...] += tn(grad_down, active)
+    acc_bd[...] += tn(down, slot_grad)
 
     @pl.when(step == count - 1)
     def _():
-        pack[0:256, :] = acc_a[...].astype(BF)
-        pack[256:384, :] = acc_bi[...].astype(BF)
-        pack[384:512, :] = acc_bd[...].astype(BF)
-        pack[512:576, :HALF_WIDTH] = acc_ad[0:64, :].astype(BF)
-        pack[512:576, HALF_WIDTH:] = acc_ad[64:128, :].astype(BF)
-        half = PACK_ROWS // 2
-        mine_ref[...] = pack[pl.ds(pl.multiple_of(side * half, 16), half), :]
-        send_ref[...] = pack[pl.ds(pl.multiple_of((1 - side) * half, 16), half), :]
-
-
-def expert_call(expert, scalars, x_blocks, g_blocks, weights, carried, router_wide, experts):
+        if emit:
+            for target, total in zip(emitted, sums):
+                target[...] = total[...]
+        else:
+            pack[0:256, :] = acc_a[...].astype(BF)
+            pack[256:384, :] = acc_bi[...].astype(BF)
+            pack[384:512, :] = acc_bd[...].astype(BF)
+            pack[512:576, :HALF_WIDTH] = acc_ad[0:64, :].astype(BF)
+            pack[512:576, HALF_WIDTH:] = acc_ad[64:128, :].astype(BF)
+            half = PACK_ROWS // 2
+            mine_ref[...] = pack[pl.ds(pl.multiple_of(side * half, 16), half), :]
+            send_ref[...] = pack[pl.ds(pl.multiple_of((1 - side) * half, 16), half), :]
+
+
+def expert_call(
+    expert, scalars, x_blocks, g_blocks, weights, experts, blocks, start=0,
+    carried=None, halves=None, seeds=None, emit=False, router_wide=None,
+):
     count = len(x_blocks)
-    total = count * TOK_DEV
-    first = carried is None
+    total = blocks * TOK_DEV
     last = router_wide is not None
-    rows = lambda width: pl.BlockSpec((TOK_DEV, width), lambda i, *_: (i, 0))
+    rows = lambda width: pl.BlockSpec((TOK_DEV, width), lambda i, *_: (i + start, 0))
+    pair = lambda width: pl.BlockSpec((TOK_DEV, width), lambda i, *_: (i // 2, 0))
     whole = lambda *dims: pl.BlockSpec(dims, lambda i, *_: (0,) * len(dims), pipeline_mode=pl.Buffered(1))
+    fixed = lambda *dims: pl.BlockSpec(dims, lambda i, *_: (0,) * len(dims))
+    sum_dims = [(256, MODEL_WIDTH), (128, MODEL_WIDTH), (128, HALF_WIDTH), (128, MODEL_WIDTH)]
     in_specs = [ANY] * (2 * count + 6)
     args = [*x_blocks, *g_blocks, *weights]
-    if not first:
+    aliases = {}
+    if carried is not None:
         in_specs += [rows(MODEL_WIDTH), rows(MODEL_WIDTH), rows(LANES)]
         args += list(carried)
+    if start:
+        aliases = {1 + len(args) + i: i for i in range(3)}
+        in_specs += [ANY] * 3
+        args += list(halves)
+    if seeds is not None:
+        in_specs += [whole(*d) for d in sum_dims]
+        args += list(seeds)
     if last:
         in_specs.append(whole(MODEL_WIDTH, LANES))
         args.append(router_wide)
-    kind = BF if last else F32
-    outs = [shape(total, MODEL_WIDTH, dtype=kind), shape(total, MODEL_WIDTH, dtype=kind)]
-    out_specs = [rows(MODEL_WIDTH), rows(MODEL_WIDTH)]
-    if not last:
-        outs.append(shape(total, LANES, dtype=F32))
-        out_specs.append(rows(LANES))
+        outs = [shape(total // 2, MODEL_WIDTH)] * 4
+        out_specs = [pair(MODEL_WIDTH)] * 4
+    else:
+        outs = [
+            shape(total, MODEL_WIDTH, dtype=F32),
+            shape(total, MODEL_WIDTH, dtype=F32),
+            shape(total, LANES, dtype=F32),
+        ]
+        out_specs = [rows(MODEL_WIDTH), rows(MODEL_WIDTH), rows(LANES)]
     half = PACK_ROWS // 2
-    for _ in range(2):
-        outs.append(shape(half, MODEL_WIDTH))
-        out_specs.append(pl.BlockSpec((half, MODEL_WIDTH), lambda i, *_: (0, 0)))
+    if emit:
+        outs += [shape(*d, dtype=F32) for d in sum_dims]
+        out_specs += [fixed(*d) for d in sum_dims]
+    else:
+        outs += [shape(half, MODEL_WIDTH)] * 2
+        out_specs += [fixed(half, MODEL_WIDTH)] * 2
     scratch = [pltpu.VMEM((2, TOK_DEV, META), BF), pltpu.VMEM((2, TOK_DEV, MODEL_WIDTH), BF)]
     scratch += [pltpu.VMEM(w.shape[1:], BF) for w in weights]
+    scratch += [pltpu.VMEM(d, F32) for d in sum_dims]
     scratch += [
-        pltpu.VMEM((256, MODEL_WIDTH), F32),
-        pltpu.VMEM((128, MODEL_WIDTH), F32),
-        pltpu.VMEM((128, HALF_WIDTH), F32),
-        pltpu.VMEM((128, MODEL_WIDTH), F32),
         pltpu.VMEM((PACK_ROWS, MODEL_WIDTH), BF),
         pltpu.SemaphoreType.DMA((2,)),
         pltpu.SemaphoreType.DMA((2,)),
@@ -485,17 +522,19 @@
     ]
     return pl.pallas_call(
         functools.partial(
-            expert_body, expert=expert, first=first, last=last, count=count, experts=experts
+            expert_body, expert=expert, start=start, count=count, blocks=blocks, experts=experts,
+            carried=carried is not None, seeded=seeds is not None, emit=emit, last=last,
         ),
         out_shape=outs,
         grid_spec=pltpu.PrefetchScalarGridSpec(
             num_scalar_prefetch=1, grid=(count,), in_specs=in_specs, out_specs=out_specs, scratch_shapes=scratch
         ),
+        input_output_aliases=aliases,
         compiler_params=pltpu.CompilerParams(
             dimension_semantics=("arbitrary",), vmem_limit_bytes=VMEM_LIMIT
         ),
         cost_estimate=pl.CostEstimate(
-            flops=total * 9_800_000, bytes_accessed=20_000_000, transcendentals=total * 512
+            flops=count * TOK_DEV * 9_800_000, bytes_accessed=5_000_000 * count, transcendentals=0
         ),
         name="expert_step",
     )(scalars, *args)
@@ -579,20 +618,44 @@
     return lax.axis_size(axis).bit_length() - 1
 
 
-def gather_blocks(values):
-    blocks = [values]
-    for bit in reversed(range(axis_bits("expert"))):
-        blocks = blocks + [swap(block, "expert", bit) for block in blocks]
+def tie(first, second):
+    return lax.optimization_barrier((first, second))
+
+
+def add(first, second):
+    return (first.astype(F32) + second.astype(F32)).astype(BF)
+
+
+def far_blocks(values):
+    blocks = {0: values}
+    for bit in reversed(range(1, axis_bits("expert"))):
+        for index in list(blocks):
+            blocks[index ^ (1 << bit)] = swap(blocks[index], "expert", bit)
     return blocks
 
 
-def return_stages(partial):
-    for bit in range(axis_bits("expert")):
-        half = partial.shape[0] // 2
-        got = swap(partial[half:], "expert", bit)
-        if half == TOK_DEV:
-            return partial[:half], got
-        partial = (partial[:half].astype(F32) + got.astype(F32)).astype(BF)
+def near_blocks(far):
+    blocks = []
+    for index in sorted(far):
+        if index:
+            blocks += [far[index], swap(far[index], "expert", 0)]
+    return blocks
+
+
+class Return:
+    def __init__(self, top, low):
+        self.bits = list(reversed(range(1, axis_bits("expert"))))
+        self.mine = top
+        self.got = swap(low, "expert", 0)
+
+    def advance(self):
+        half = self.mine.shape[0] // 2
+        send = add(self.mine[half:], self.got[half:])
+        self.mine = add(self.mine[:half], self.got[:half])
+        return send
+
+    def launch(self, send):
+        self.got = swap(send, "expert", self.bits.pop(0))
 
 
 class Sum:
@@ -601,58 +664,55 @@
         self.stages = list(stages)
         self.mine = mine
         self.send = send
-        self.begin(True)
-
-    def begin(self, halved):
-        axis, bit = self.stages.pop(0)
-        self.path.append((axis, bit, halved))
-        self.got = swap(self.send, axis, bit)
-
-    def split(self, values):
-        axis, bit = self.stages[0]
-        rows, width = values.shape
-        if rows % 16:
-            self.mine = self.send = values
-            return False
-        side = (lax.axis_index(axis) >> bit) & 1
-        halves = values.reshape(2, rows // 2, width)
-        self.mine = lax.dynamic_index_in_dim(halves, side, 0, keepdims=False)
-        self.send = lax.dynamic_index_in_dim(halves, 1 - side, 0, keepdims=False)
-        return True
-
-    def advance(self):
-        if self.stages:
-            values = (self.mine.astype(F32) + self.got.astype(F32)).astype(BF)
-            halved = self.split(values)
-            self.begin(halved)
-            return
-        if self.path[-1][2] is not None:
-            self.values = (self.mine.astype(F32) + self.got.astype(F32)).astype(BF)
-            while not self.path[-1][2]:
-                self.path.pop()
-            self.path.append((None, None, None))
+        self.down = True
+        self.target = self.stages.pop(0)
+        self.path.append(self.target)
+        self.launch()
+
+    def launch(self):
+        self.got = swap(self.send, *self.target)
+
+    def prepare(self):
+        if self.down:
+            values = add(self.mine, self.got)
+            if self.stages:
+                self.target = self.stages.pop(0)
+                axis, bit = self.target
+                rows, width = values.shape
+                if rows % 16:
+                    self.mine = self.send = values
+                    return
+                self.path.append(self.target)
+                side = (lax.axis_index(axis) >> bit) & 1
+                halves = values.reshape(2, rows // 2, width)
+                self.mine = lax.dynamic_index_in_dim(halves, side, 0, keepdims=False)
+                self.send = lax.dynamic_index_in_dim(halves, 1 - side, 0, keepdims=False)
+                return
+            self.down = False
         else:
-            self.path.pop()
-            axis, bit, _ = self.path.pop()
+            axis, bit = self.path.pop()
             side = (lax.axis_index(axis) >> bit) & 1
-            low = jnp.where(side == 0, self.values, self.got)
-            high = jnp.where(side == 0, self.got, self.values)
-            self.values = jnp.concatenate([low, high], axis=0)
-            self.path.append((None, None, None))
-        axis, bit, _ = self.path[-2]
-        self.got = swap(self.values, axis, bit)
+            low = jnp.where(side == 0, self.mine, self.got)
+            high = jnp.where(side == 0, self.got, self.mine)
+            values = jnp.concatenate([low, high], axis=0)
+        self.target = self.path[-1]
+        self.mine = self.send = values
 
     def pending(self):
-        return bool(self.stages) or self.path[-1][2] is not None or len(self.path) > 2
-
-    def finish(self):
-        while self.pending():
-            self.advance()
-        return self.values, self.got
-
-
-def tie(first, second):
-    return lax.optimization_barrier((first, second))
+        return self.down or len(self.path) > 1
+
+    def step(self):
+        if self.pending():
+            self.prepare()
+            self.launch()
+
+
+def sync(holders, *extras):
+    arrays = tuple(holder.got for holder in holders) + extras
+    arrays = lax.optimization_barrier(arrays)
+    for holder, got in zip(holders, arrays):
+        holder.got = got
+    return arrays[len(holders) :]
 
 
 def on_device(
@@ -679,11 +739,12 @@
     expert_down_second_factors,
     output_gradient,
 ):
-    experts = EXP_DEV * lax.axis_size("expert")
+    blocks = lax.axis_size("expert")
+    experts = EXP_DEV * blocks
     place = lax.axis_index("expert")
     dp_side = lax.axis_index("dp") & 1
     core_side = place & 1
-    grad_blocks = gather_blocks(output_gradient)
+    grad_far = far_blocks(output_gradient)
     cosine, sine = rope_tables()
     scalars = jnp.stack([adapter_of_sequence[0], lengths[0], core_side]).astype(jnp.int32)
     g1 = first_norm_gain[None]
@@ -699,9 +760,13 @@
         output_second_factors,
     ]
     hidden, payload, normed, lowrank, queries, keys, values, attended, out_rank, router_wide = attention_forward(
-        scalars, inputs, g1, g2, cosine, sine, routes, router_weight, weights
+        scalars, inputs, g1, g2, cosine, sine, routes.T, router_weight.T, weights
     )
-    row_blocks = gather_blocks(payload)
+    for index in grad_far:
+        if index:
+            grad_far[index], payload = tie(grad_far[index], payload)
+    row_far = far_blocks(payload)
+    near = [[values, swap(values, "expert", 0)] for values in (payload, output_gradient)]
     expert_weights = [
         expert_input_first_factors,
         expert_input_weight,
@@ -711,40 +776,81 @@
         expert_down_second_factors,
     ]
     dp_stages = [("dp", bit) for bit in range(axis_bits("dp"))]
-    carried = None
     sums = []
-    for local in range(EXP_DEV):
-        number = jnp.stack([EXP_DEV * place + local, dp_side]).astype(jnp.int32)
-        for older in sums[: max(local - 1, 0)]:
-            older.got, number = tie(older.got, number)
-            older.advance()
+    first_number = EXP_DEV * place
+    number = jnp.stack([first_number, dp_side]).astype(jnp.int32)
+    *halves, s0, s1, s2, s3 = expert_call(
+        0, number, *near, expert_weights, experts, blocks, emit=True
+    )
+    for far in (row_far, grad_far):
+        for index in far:
+            if index:
+                far[index], s0 = tie(far[index], s0)
+    row_blocks = near[0] + near_blocks(row_far)
+    grad_blocks = near[1] + near_blocks(grad_far)
+    *carried, mine, send = expert_call(
+        0, number, row_blocks[2:], grad_blocks[2:], expert_weights, experts, blocks,
+        start=2, halves=halves, seeds=(s0, s1, s2, s3),
+    )
+    sums.append(Sum(mine, send, dp_stages))
+    for local in range(1, EXP_DEV):
+        number = jnp.stack([first_number + local, dp_side]).astype(jnp.int32)
+        (number,) = sync(sums[: local - 1], number)
+        for older in sums[: local - 1]:
+            older.step()
         *carried, mine, send = expert_call(
-            local,
-            number,
-            row_blocks,
-            grad_blocks,
-            expert_weights,
-            carried,
-            router_wide if local == EXP_DEV - 1 else None,
-            experts,
+            local, number, row_blocks, grad_blocks, expert_weights, experts, blocks, carried=carried,
+            router_wide=router_wide if local == EXP_DEV - 1 else None,
         )
-        sums.append(Sum(mine, send, dp_stages))
-    mixture_part, row_part = carried
-    row_mine, row_got = return_stages(row_part)
+        if local < EXP_DEV - 1:
+            sums.append(Sum(mine, send, dp_stages))
+    mix_top, mix_low, row_top, row_low = carried
+    (row_low,) = sync(sums, row_low)
+    row = Return(row_top, row_low)
+    last_sum = Sum(mine, send, dp_stages)
+    for one in sums:
+        one.step()
+    sums.append(last_sum)
+    mix = Return(mix_top, mix_low)
+    while row.bits:
+        row.launch(row.advance())
+    sync(sums + [row, mix])
+    while mix.bits:
+        mix.launch(mix.advance())
+    for one in sums:
+        one.step()
     grad_input, att_mine, att_send = attention_backward(
         scalars,
-        [inputs, g1, g2, cosine, sine, hidden, row_mine, row_got, output_gradient]
+        [inputs, g1, g2, cosine, sine, hidden, row.mine, row.got, output_gradient]
         + [normed, lowrank, queries, keys, values, attended, out_rank],
         weights,
     )
-    mix_mine, mix_got = return_stages(mixture_part)
+    (att_send,) = sync(sums + [mix], att_send)
+    stages = [("expert", bit) for bit in range(axis_bits("expert"))] + dp_stages
+    total = Sum(att_mine, att_send, stages)
+    for one in sums:
+        one.step()
+    turn = 0
+    while total.pending() and (len(total.path) > 2 or total.down):
+        total.step()
+        turn += 1
+        if turn % 2 and any(one.pending() for one in sums):
+            sync(sums + [total])
+            for one in sums:
+                one.step()
+    while any(one.pending() for one in sums):
+        sync(sums)
+        for one in sums:
+            one.step()
+    sync(sums)
+    pieces = [piece for one in sums for piece in (one.mine, one.got)]
+    expert_grads = list(expert_finish(dp_side[None].astype(jnp.int32), pieces))
+    expert_grads[0], total.got = tie(expert_grads[0], total.got)
+    total.step()
     live = (jnp.arange(TOK_DEV, dtype=jnp.int32) < lengths[0]).astype(F32)[:, None]
-    output = (live * (hidden + mix_mine.astype(F32) + mix_got.astype(F32))).astype(BF)
-    stages = [("expert", bit) for bit in range(axis_bits("expert"))] + dp_stages
-    attention_sum = Sum(att_mine, att_send, stages).finish()
-    pieces = [piece for one in sums for piece in one.finish()]
-    expert_grads = expert_finish(dp_side[None].astype(jnp.int32), pieces)
-    attention_grads = attention_finish(core_side[None].astype(jnp.int32), *attention_sum)
+    output = (live * (hidden + mix.mine.astype(F32) + mix.got.astype(F32))).astype(BF)
+    side = core_side[None].astype(jnp.int32)
+    attention_grads = attention_finish(side, total.mine, total.got)
     return (output, grad_input, *attention_grads, *expert_grads)
 
 

time: 337 us -> 287 us (0.85)
  waiting for transfers between devices: 130 us -> 65.8 us
  other arithmetic: 10.6 us -> 19.8 us
  Pallas kernels: 134 us -> 141 us
    ppermute x43, waiting for transfers between devices: 130 us -> 65.8 us  [swap(): return lax.ppermute(values, axis, [(i, i ^ 1 << bit) for i in range(size)])]
    pallas_call x4 -> x5, Pallas kernels: 92.4 us -> 100 us  [expert_call(): pl.pallas_call(functools.partial(expert_body, expert=expert, start=start,...]
    convert_element_type x20, other arithmetic: 4.9 us -> 11.8 us  [the longest x19 9.73 us: add(): return (first.astype(F32) + second.astype(F32)).astype(BF)]
    slice x4 -> x0, local copies, waits for them, and re-layouts: 3.38 us -> none  [return_stages(): got = swap(partial[half:], 'expert', bit)]
    unnamed x48 -> x68, local copies, waits for them, and re-layouts: 6.51 us -> 8.32 us
  transfers between devices with their start and end apart: 43 -> 43, of which waited for: 18 -> 13; matrix products, arithmetic and copies ran while one was open for 4% -> 6% of each run, Pallas kernels for 30% -> 44%
where the time goes in v3:
time: 287 us; the launch traced here: 281 us
  Pallas kernels  141 us (49%)
  waiting for transfers between devices  65.8 us (23%)
  starting transfers between devices  41.8 us (15%)
  other arithmetic  19.8 us (7%)
  local copies, waits for them, and re-layouts  9.35 us (3%)
  between operations  3.02 us (1%)
    pallas_call x5, Pallas kernels, expert_call(): pl.pallas_call(functools.partial(expert_body, expert=expert, start=start,...  100 us
    ppermute x43, waiting for transfers between devices, swap(): return lax.ppermute(values, axis, [(i, i ^ 1 << bit) for i in range(size)])  65.8 us
    ppermute x43, starting transfers between devices, swap(): return lax.ppermute(values, axis, [(i, i ^ 1 << bit) for i in range(size)])  41.8 us
    pallas_call x1, Pallas kernels, attention_backward(): pl.pallas_call(backward_body, out_shape=[shape(TOK_DEV, MODEL_WIDTH, dtyp...  20.4 us
    pallas_call x1, Pallas kernels, attention_forward(): pl.pallas_call(functools.partial(forward_body, experts=experts), out_shap...  10.7 us
    convert_element_type x19, other arithmetic, add(): return (first.astype(F32) + second.astype(F32)).astype(BF)  9.73 us
    unnamed x68, local copies, waits for them, and re-layouts  8.32 us
    pallas_call x1, Pallas kernels, expert_finish(): pl.pallas_call(expert_finish_body, out_shape=[shape(EXP_DEV, *d, dtype=F3...  6.43 us
  transfers between devices with their start and end apart: 43, of which 13 were waited for; matrix products, arithmetic and copies ran while one was open for 6% of the time, Pallas kernels for 44%

profile of v3, /device:TPU:0, one launch (start us, length us, event | category | flops | bytes accessed | tf_op | source)
XLA Modules:
  0.0 281.1 jit_solution(1595657210227090574)
XLA Ops:
  0.6 3.0 %collective-permute-start = (bf16[256,1024]{1,0:T(8,128)(2,1)}, bf16[256,1024]{1,0:T(8,128)(2,1)S(1)}, u32[]{:S(2)}, u32[]{:S(2)}) collective-permute-start(bf16[256,1024]{1,0:T(8,128)(2,1)} %og_ref.1), channel_id=1, source_target_pairs={{0,2},{1,3},{2,0},{3,1},{4,6},{5,7},{6,4},{7,5},{8,10},{9,11},{10,... | collective-permute-start | bytes 1572872 | tf_op jit(solution)/shard_map/ppermute | solution.py:614
  5.6 10.7 %attention_forward.1 = (f32[256,1024]{1,0:T(8,128)}, bf16[256,1152]{1,0:T(8,128)(2,1)}, bf16[256,1024]{1,0:T(8,128)(2,1)}, bf16[256,384]{1,0:T(8,128)(2,1)}, bf1...) custom-call(s32[3]{0:T(128)} %pad_add_fusion.scalars, ...), custom_call_target="tpu_custom_call" | custom-call | flops 3000000000 | bytes 20000000 | tf_op jit(solution)/shard_map/attention_forward/pallas_call | solution.py:183
  16.9 1.2 collective-permute-start.1
  21.0 13.5 %expert_step.5 = (f32[1024,1024]{1,0:T(8,128)}, f32[1024,1024]{1,0:T(8,128)}, f32[1024,128]{1,0:T(8,128)}, f32[256,1024]{1,0:T(8,128)}, f32[128,1024]{1,0:T(8,12...) custom-call(s32[2]{0:T(128)} %pad_add_fusion.1.scalars, bf16[256,1152]{1,0:T(8,128)(2,1)} %get-tuple-element.111.refs_0_, ...), custom_call_target="tpu_custom_call" | custom-call | flops 5017600000 | bytes 10000000 | tf_op jit(solution)/shard_map/expert_step/pallas_call | solution.py:523
  38.3 14.5 %expert_step.6 = (f32[1024,1024]{1,0:T(8,128)}, f32[1024,1024]{1,0:T(8,128)}, f32[1024,128]{1,0:T(8,128)}, bf16[288,1024]{1,0:T(8,128)(2,1)}, bf16[288,1024]{1,0:T(8,128)(2,1)}) custom-call(s32[2]{0:T(128)} %pad_add_fusion.1.scalars, bf16[256,1152]{1,0:T(8,128)(2,1)} %copy-done.20, ...), custom_call_target="tpu_custom_call", output_to_operand_aliasing={{0}: (11, {}), {1}: (12, {}), {2}: (13, {})} | custom-call | flops 5017600000 | bytes 10000000 | tf_op jit(solution)/shard_map/expert_step/pallas_call | solution.py:523
  52.8 1.6 collective-permute-start.6
  54.4 22.5 %expert_step.7 = (f32[1024,1024]{1,0:T(8,128)}, f32[1024,1024]{1,0:T(8,128)}, f32[1024,128]{1,0:T(8,128)}, bf16[288,1024]{1,0:T(8,128)(2,1)}, bf16[288,1024]{1,0:T(8,128)(2,1)}) custom-call(s32[2]{0:T(128)} %pad_add_fusion.3.scalars, bf16[256,1152]{1,0:T(8,128)(2,1)} %get-tuple-element.111.refs_0_, bf16[256,1152]{1,0:T(8,128)(2,1)} %copy-done.12, ...), custom_call_target="tpu_custom_call" | custom-call | flops 10035200000 | bytes 20000000 | tf_op jit(solution)/shard_map/expert_step/pallas_call | solution.py:523
  77.7 1.6 collective-permute-start.7
  79.3 22.9 %expert_step.8 = (f32[1024,1024]{1,0:T(8,128)}, f32[1024,1024]{1,0:T(8,128)}, f32[1024,128]{1,0:T(8,128)}, bf16[288,1024]{1,0:T(8,128)(2,1)}, bf16[288,1024]{1,0:T(8,128)(2,1)}) custom-call(s32[2]{0:T(128)} %pad_add_fusion.2.scalars, bf16[256,1152]{1,0:T(8,128)(2,1)} %get-tuple-element.111.refs_0_, bf16[256,1152]{1,0:T(8,128)(2,1)} %copy-done.12, ...), custom_call_target="tpu_custom_call" | custom-call | flops 10035200000 | bytes 20000000 | tf_op jit(solution)/shard_map/expert_step/pallas_call | solution.py:523
  102.2 1.6 collective-permute-start.11
  103.9 2.6 collective-permute-start.9
  107.3 26.8 %expert_step.9 = (bf16[512,1024]{1,0:T(8,128)(2,1)}, bf16[512,1024]{1,0:T(8,128)(2,1)}, bf16[512,1024]{1,0:T(8,128)(2,1)}, bf16[512,1024]{1,0:T(8,128)(2,1)}, bf...) custom-call(s32[2]{0:T(128)} %pad_add_fusion.4.scalars, bf16[256,1152]{1,0:T(8,128)(2,1)} %get-tuple-element.111.refs_0_, ...), custom_call_target="tpu_custom_call" | custom-call | flops 10035200000 | bytes 20000000 | tf_op jit(solution)/shard_map/expert_step/pallas_call | solution.py:523
  135.8 0.9 fusion.9
  137.2 1.5 add_convert_fusion.2
  138.7 1.4 add_convert_fusion.5
  140.1 1.2 collective-permute-start.17
  141.2 1.6 collective-permute-start.14
  143.0 4.1 %collective-permute-done.12 = bf16[72,1024]{1,0:T(8,128)(2,1)} collective-permute-done((bf16[72,1024]{1,0:T(8,128)(2,1)S(1)}, bf16[72,1024]{1,0:T(8,128)(2,1)}, u32[]{:S(2)}, u32[]{:S(2)}) %collective-permute-start.12) | collective-permute-done | bytes 147488 | tf_op jit(solution)/shard_map/ppermute | solution.py:614
  147.1 9.2 %collective-permute-done.13 = bf16[72,1024]{1,0:T(8,128)(2,1)S(1)} collective-permute-done((bf16[72,1024]{1,0:T(8,128)(2,1)S(1)}, bf16[72,1024]{1,0:T(8,128)(2,1)S(1)}, u32[]{:S(2)}, u32[]{:S(2)}) %collective-permute-start.13) | collective-permute-done | bytes 147488 | tf_op jit(solution)/shard_map/ppermute | solution.py:614
  156.3 0.9 broadcast_select_fusion.19
  157.4 2.4 collective-permute-start.20
  160.6 1.3 add_convert_fusion.1
  161.9 2.1 collective-permute-start.22
  164.0 1.2 add_convert_fusion.6
  165.2 1.2 collective-permute-start.23
  166.5 20.4 %attention_backward.1 = (f32[256,1024]{1,0:T(8,128)}, bf16[448,1024]{1,0:T(8,128)(2,1)}, bf16[448,1024]{1,0:T(8,128)(2,1)}) custom-call(s32[3]{0:T(128)} %pad_add_fusion.scalars, bf16[256,1024]{1,0:T(8,128)(2,1)} %x_ref.3, f32[1,1024]{1,0:T(1,128)} %bitcast.103, f32[1,1024]{1,0:T(1,128)} %bitcast.105, f32[256,128]{1,0:T(8,128)} %constant.81.clone.cos_ref, ...), custom_call_target="tpu_custom_call" | custom-call | flops 6000000000 | bytes 24000000 | tf_op jit(solution)/shard_map/attention_backward/pallas_call | solution.py:299
  188.0 1.6 collective-permute-start.25
  190.3 0.9 fusion.7
  191.3 2.4 collective-permute-start.27
  196.5 4.6 %collective-permute-done.27 = bf16[72,1024]{1,0:T(8,128)(2,1)} collective-permute-done((bf16[72,1024]{1,0:T(8,128)(2,1)S(1)}, bf16[72,1024]{1,0:T(8,128)(2,1)}, u32[]{:S(2)}, u32[]{:S(2)}) %collective-permute-start.27) | collective-permute-done | bytes 147488 | tf_op jit(solution)/shard_map/ppermute | solution.py:614
  201.1 7.2 %collective-permute-done.28 = bf16[72,1024]{1,0:T(8,128)(2,1)S(1)} collective-permute-done((bf16[72,1024]{1,0:T(8,128)(2,1)S(1)}, bf16[72,1024]{1,0:T(8,128)(2,1)S(1)}, u32[]{:S(2)}, u32[]{:S(2)}) %collective-permute-start.28) | collective-permute-done | bytes 147488 | tf_op jit(solution)/shard_map/ppermute | solution.py:614
  209.0 1.3 broadcast_select_fusion.7
  212.0 1.2 fusion
  213.2 1.6 collective-permute-start.30
  214.8 2.6 collective-permute-start.33
  217.4 12.2 %collective-permute-done.30 = bf16[112,1024]{1,0:T(8,128)(2,1)S(1)} collective-permute-done((bf16[112,1024]{1,0:T(8,128)(2,1)S(1)}, bf16[112,1024]{1,0:T(8,128)(2,1)S(1)}, u32[]{:S(2)}, u32[]{:S(2)}) %collective-permute-start.30) | collective-permute-done | bytes 229408 | tf_op jit(solution)/shard_map/ppermute | solution.py:614
  229.9 4.8 %collective-permute-done.34 = bf16[56,1024]{1,0:T(8,128)(2,1)S(1)} collective-permute-done((bf16[56,1024]{1,0:T(8,128)(2,1)S(1)}, bf16[56,1024]{1,0:T(8,128)(2,1)S(1)}, u32[]{:S(2)}, u32[]{:S(2)}) %collective-permute-start.34) | collective-permute-done | bytes 114720 | tf_op jit(solution)/shard_map/ppermute | solution.py:614
  236.1 2.1 collective-permute-start.37
  238.2 4.1 %collective-permute-done.35 = bf16[56,1024]{1,0:T(8,128)(2,1)S(1)} collective-permute-done((bf16[56,1024]{1,0:T(8,128)(2,1)S(1)}, bf16[56,1024]{1,0:T(8,128)(2,1)S(1)}, u32[]{:S(2)}, u32[]{:S(2)}) %collective-permute-start.35) | collective-permute-done | bytes 114720 | tf_op jit(solution)/shard_map/ppermute | solution.py:614
  242.5 4.6 %collective-permute-done.38 = bf16[56,1024]{1,0:T(8,128)(2,1)S(1)} collective-permute-done((bf16[56,1024]{1,0:T(8,128)(2,1)S(1)}, bf16[56,1024]{1,0:T(8,128)(2,1)S(1)}, u32[]{:S(2)}, u32[]{:S(2)}) %collective-permute-start.38) | collective-permute-done | bytes 114720 | tf_op jit(solution)/shard_map/ppermute | solution.py:614
  247.7 1.1 collective-permute-start.39
  249.0 1.1 collective-permute-start.40
  250.1 6.2 %collective-permute-done.39 = bf16[112,1024]{1,0:T(8,128)(2,1)S(1)} collective-permute-done((bf16[112,1024]{1,0:T(8,128)(2,1)S(1)}, bf16[112,1024]{1,0:T(8,128)(2,1)S(1)}, u32[]{:S(2)}, u32[]{:S(2)}) %collective-permute-start.39) | collective-permute-done | bytes 229408 | tf_op jit(solution)/shard_map/ppermute | solution.py:614
  256.4 1.4 collective-permute-start.41
  257.8 7.0 %collective-permute-done.40.refs_7_ = bf16[288,1024]{1,0:T(8,128)(2,1)S(1)} collective-permute-done((bf16[288,1024]{1,0:T(8,128)(2,1)S(1)}, bf16[288,1024]{1,0:T(8,128)(2,1)S(1)}, u32[]{:S(2)}, u32[]{:S(2)}) %collective-permute-start.40) | collective-permute-done | bytes 589856 | tf_op jit(solution)/shard_map/ppermute | solution.py:614
  265.7 6.4 %expert_finish.1 = (f32[4,1024,256]{2,1,0:T(8,128)}, f32[4,2,128,512]{3,2,1,0:T(8,128)}, f32[4,512,128]{2,1,0:T(8,128)}, f32[4,128,1024]{2,1,0:T(8,128)}) custom-call(s32[1]{0:T(128)} %bitcast.7.scalars, bf16[288,1024]{1,0:T(8,128)(2,1)} %copy-done.1, bf16[288,1024]{1,0:T(8,128)(2,1)} %copy-done.11, bf16[288,1024]{1,0:T(8,128)(2,1)} %copy-done.2, ...), custom_call_target="tpu_custom_call" | custom-call | flops 1000000 | bytes 15000000 | tf_op jit(solution)/shard_map/expert_finish/pallas_call | solution.py:565
  274.1 2.1 multiply_convert_fusion
  277.1 3.7 %attention_finish.1 = (f32[1024,384]{1,0:T(8,128)}, f32[128,1024]{1,0:T(8,128)}, f32[2,128,512]{2,1,0:T(8,128)}, f32[1024,128]{1,0:T(8,128)}, f32[128,1024]{1,0:T(8,128)}) custom-call(s32[1]{0:T(128)} %bitcast.1.scalars, bf16[448,1024]{1,0:T(8,128)(2,1)} %copy-done, bf16[448,1024]{1,0:T(8,128)(2,1)} %copy-done.9), custom_call_target="tpu_custom_call" | custom-call | flops 1000000 | bytes 6000000 | tf_op jit(solution)/shard_map/attention_finish/pallas_call | solution.py:600
  (174 shorter events, 26.0 us)
Async XLA Ops:
  0.6 15.7 %collective-permute-start = (bf16[256,1024]{1,0:T(8,128)(2,1)}, bf16[256,1024]{1,0:T(8,128)(2,1)S(1)}, u32[]{:S(2)}, u32[]{:S(2)}) collective-permute-start(bf16[256,1024]{1,0:T(8,128)(2,1)} %og_ref.1), channel_id=1, source_target_pairs={{0,2},{1,3},{2,0},{3,1},{4,6},{5,7},{6,4},{7,5},{8,10},{9,11},{10,... | collective-permute-start | bytes 1572872 | tf_op jit(solution)/shard_map/ppermute | solution.py:614
  16.3 18.3 %copy-start.22 = (bf16[256,1024]{1,0:T(8,128)(2,1)}, bf16[256,1024]{1,0:T(8,128)(2,1)S(1)}, u32[]{:S(2)}) copy-start(bf16[256,1024]{1,0:T(8,128)(2,1)S(1)} %collective-permute-done.refs_2_.refs_6_) | copy-start | bytes 1572868
  16.3 3.0 %collective-permute-start.2 = (bf16[256,1152]{1,0:T(8,128)(2,1)}, bf16[256,1152]{1,0:T(8,128)(2,1)S(1)}, u32[]{:S(2)}, u32[]{:S(2)}) collective-permute-start(bf16[256,1152]{1,0:T(8,128)(2,1)} %get-tuple-element.111.refs_0_), channel_id=1, source_target_pairs={{0,1},{1,0},{2,3},{3,2},{4,5},{5,4},{6,7},{7,6},{8,9},{9,8},{10,11... | collective-permute-start | bytes 1769480 | tf_op jit(solution)/shard_map/ppermute | solution.py:614
  16.4 2.9 %collective-permute-start.3 = (bf16[256,1024]{1,0:T(8,128)(2,1)S(1)}, bf16[256,1024]{1,0:T(8,128)(2,1)S(1)}, u32[]{:S(2)}, u32[]{:S(2)}) collective-permute-start(bf16[256,1024]{1,0:T(8,128)(2,1)S(1)} %copy-done.24), channel_id=1, source_target_pairs={{0,1},{1,0},{2,3},{3,2},{4,5},{5,4},{6,7},{7,6},{8,9},{9,8},{10,11... | collective-permute-start | bytes 1572872 | tf_op jit(solution)/shard_map/ppermute | solution.py:614
  16.9 17.5 %collective-permute-start.1 = (bf16[256,1152]{1,0:T(8,128)(2,1)}, bf16[256,1152]{1,0:T(8,128)(2,1)S(1)}, u32[]{:S(2)}, u32[]{:S(2)}) collective-permute-start(bf16[256,1152]{1,0:T(8,128)(2,1)} %get-tuple-element.111.refs_0_), channel_id=1, source_target_pairs={{0,2},{1,3},{2,0},{3,1},{4,6},{5,7},{6,4},{7,5},{8,10},{9,11},{10,... | collective-permute-start | bytes 1769480 | tf_op jit(solution)/shard_map/ppermute | solution.py:614
  34.4 2.8 %collective-permute-start.4 = (bf16[256,1152]{1,0:T(8,128)(2,1)S(1)}, bf16[256,1152]{1,0:T(8,128)(2,1)S(1)}, u32[]{:S(2)}, u32[]{:S(2)}) collective-permute-start(bf16[256,1152]{1,0:T(8,128)(2,1)S(1)} %collective-permute-done.1.refs_0_.refs_2_), channel_id=1, source_target_pairs={{0,1},{1,0},{2,3},{3,2},{4,5},{5,4},{6,7},{7,6},{8,9},{9,8},{10,11... | collective-permute-start | bytes 1769480 | tf_op jit(solution)/shard_map/ppermute | solution.py:614
  34.6 2.6 collective-permute-start.5
  52.8 24.6 %collective-permute-start.6 = (bf16[288,1024]{1,0:T(8,128)(2,1)}, bf16[288,1024]{1,0:T(8,128)(2,1)S(1)}, u32[]{:S(2)}, u32[]{:S(2)}) collective-permute-start(bf16[288,1024]{1,0:T(8,128)(2,1)} %get-tuple-element.125), channel_id=1, source_target_pairs={{0,4},{4,0},{8,12},{12,8},{16,20},{20,16},{24,28},{28,24},{1,5},{5... | collective-permute-start | bytes 1769480 | tf_op jit(solution)/shard_map/ppermute | solution.py:614
  54.4 23.1 %copy-start.19 = (bf16[288,1024]{1,0:T(8,128)(2,1)S(1)}, bf16[288,1024]{1,0:T(8,128)(2,1)}, u32[]{:S(2)}) copy-start(bf16[288,1024]{1,0:T(8,128)(2,1)} %get-tuple-element.124) | copy-start | bytes 1769476
  76.8 27.0 %collective-permute-start.8 = (bf16[288,1024]{1,0:T(8,128)(2,1)}, bf16[288,1024]{1,0:T(8,128)(2,1)S(1)}, u32[]{:S(2)}, u32[]{:S(2)}) collective-permute-start(bf16[288,1024]{1,0:T(8,128)(2,1)} %get-tuple-element.130), channel_id=1, source_target_pairs={{0,4},{4,0},{8,12},{12,8},{16,20},{20,16},{24,28},{28,24},{1,5},{5... | collective-permute-start | bytes 1769480 | tf_op jit(solution)/shard_map/ppermute | solution.py:614
  77.7 26.1 %collective-permute-start.7 = (bf16[144,1024]{1,0:T(8,128)(2,1)S(1)}, bf16[144,1024]{1,0:T(8,128)(2,1)S(1)}, u32[]{:S(2)}, u32[]{:S(2)}) collective-permute-start(bf16[144,1024]{1,0:T(8,128)(2,1)S(1)} %dynamic-slice_bitcast_fusion.4), channel_id=1, source_target_pairs={{0,8},{4,12},{8,0},{12,4},{16,24},{20,28},{24,16},{28,20},{1,9},{5... | collective-permute-start | bytes 884744 | tf_op jit(solution)/shard_map/ppermute | solution.py:614
  102.2 32.0 %collective-permute-start.11 = (bf16[288,1024]{1,0:T(8,128)(2,1)}, bf16[288,1024]{1,0:T(8,128)(2,1)S(1)}, u32[]{:S(2)}, u32[]{:S(2)}) collective-permute-start(bf16[288,1024]{1,0:T(8,128)(2,1)} %get-tuple-element.144), channel_id=1, source_target_pairs={{0,4},{4,0},{8,12},{12,8},{16,20},{20,16},{24,28},{28,24},{1,5},{5... | collective-permute-start | bytes 1769480 | tf_op jit(solution)/shard_map/ppermute | solution.py:614
  103.9 30.3 %collective-permute-start.9 = (bf16[72,1024]{1,0:T(8,128)(2,1)S(1)}, bf16[72,1024]{1,0:T(8,128)(2,1)}, u32[]{:S(2)}, u32[]{:S(2)}) collective-permute-start(bf16[72,1024]{1,0:T(8,128)(2,1)S(1)} %dynamic-slice_bitcast_fusion.9), channel_id=1, source_target_pairs={{0,16},{4,20},{8,24},{12,28},{16,0},{20,4},{24,8},{28,12},{1,17},{... | collective-permute-start | bytes 442376 | tf_op jit(solution)/shard_map/ppermute | solution.py:614
  106.8 27.4 %collective-permute-start.10 = (bf16[144,1024]{1,0:T(8,128)(2,1)S(1)}, bf16[144,1024]{1,0:T(8,128)(2,1)S(1)}, u32[]{:S(2)}, u32[]{:S(2)}) collective-permute-start(bf16[144,1024]{1,0:T(8,128)(2,1)S(1)} %dynamic-slice_bitcast_fusion.3), channel_id=1, source_target_pairs={{0,8},{4,12},{8,0},{12,4},{16,24},{20,28},{24,16},{28,20},{1,9},{5... | collective-permute-start | bytes 884744 | tf_op jit(solution)/shard_map/ppermute | solution.py:614
  135.1 3.6 %collective-permute-start.16 = (bf16[512,1024]{1,0:T(8,128)(2,1)}, bf16[512,1024]{1,0:T(8,128)(2,1)S(1)}, u32[]{:S(2)}, u32[]{:S(2)}) collective-permute-start(bf16[512,1024]{1,0:T(8,128)(2,1)} %get-tuple-element.152), channel_id=1, source_target_pairs={{0,1},{1,0},{2,3},{3,2},{4,5},{5,4},{6,7},{7,6},{8,9},{9,8},{10,11... | collective-permute-start | bytes 3145736 | tf_op jit(solution)/shard_map/ppermute | solution.py:614
  135.1 21.2 %collective-permute-start.15 = (bf16[288,1024]{1,0:T(8,128)(2,1)}, bf16[288,1024]{1,0:T(8,128)(2,1)}, u32[]{:S(2)}, u32[]{:S(2)}) collective-permute-start(bf16[288,1024]{1,0:T(8,128)(2,1)} %get-tuple-element.150), channel_id=1, source_target_pairs={{0,4},{4,0},{8,12},{12,8},{16,20},{20,16},{24,28},{28,24},{1,5},{5... | collective-permute-start | bytes 1769480 | tf_op jit(solution)/shard_map/ppermute | solution.py:614
  135.6 20.7 %collective-permute-start.18 = (bf16[512,1024]{1,0:T(8,128)(2,1)}, bf16[512,1024]{1,0:T(8,128)(2,1)}, u32[]{:S(2)}, u32[]{:S(2)}) collective-permute-start(bf16[512,1024]{1,0:T(8,128)(2,1)} %get-tuple-element.153), channel_id=1, source_target_pairs={{0,1},{1,0},{2,3},{3,2},{4,5},{5,4},{6,7},{7,6},{8,9},{9,8},{10,11... | collective-permute-start | bytes 3145736 | tf_op jit(solution)/shard_map/ppermute | solution.py:614
  136.8 10.4 %collective-permute-start.12 = (bf16[72,1024]{1,0:T(8,128)(2,1)S(1)}, bf16[72,1024]{1,0:T(8,128)(2,1)}, u32[]{:S(2)}, u32[]{:S(2)}) collective-permute-start(bf16[72,1024]{1,0:T(8,128)(2,1)S(1)} %fusion.9), channel_id=1, source_target_pairs={{0,16},{4,20},{8,24},{12,28},{16,0},{20,4},{24,8},{28,12},{1,17},{... | collective-permute-start | bytes 442376 | tf_op jit(solution)/shard_map/ppermute | solution.py:614
  140.1 16.3 %collective-permute-start.17 = (bf16[256,1024]{1,0:T(8,128)(2,1)}, bf16[256,1024]{1,0:T(8,128)(2,1)}, u32[]{:S(2)}, u32[]{:S(2)}) collective-permute-start(bf16[256,1024]{1,0:T(8,128)(2,1)} %get-tuple-element.208), channel_id=1, source_target_pairs={{0,2},{1,3},{2,0},{3,1},{4,6},{5,7},{6,4},{7,5},{8,10},{9,11},{10,... | collective-permute-start | bytes 1572872 | tf_op jit(solution)/shard_map/ppermute | solution.py:614
  141.2 15.1 %collective-permute-start.14 = (bf16[144,1024]{1,0:T(8,128)(2,1)S(1)}, bf16[144,1024]{1,0:T(8,128)(2,1)S(1)}, u32[]{:S(2)}, u32[]{:S(2)}) collective-permute-start(bf16[144,1024]{1,0:T(8,128)(2,1)S(1)} %dynamic-slice_bitcast_fusion.2), channel_id=1, source_target_pairs={{0,8},{4,12},{8,0},{12,4},{16,24},{20,28},{24,16},{28,20},{1,9},{5... | collective-permute-start | bytes 884744 | tf_op jit(solution)/shard_map/ppermute | solution.py:614
  142.9 17.7 %copy-start.16 = (bf16[288,1024]{1,0:T(8,128)(2,1)S(1)}, bf16[288,1024]{1,0:T(8,128)(2,1)}, u32[]{:S(2)}) copy-start(bf16[288,1024]{1,0:T(8,128)(2,1)} %get-tuple-element.158) | copy-start | bytes 1769476
  147.1 9.2 %collective-permute-start.13 = (bf16[72,1024]{1,0:T(8,128)(2,1)S(1)}, bf16[72,1024]{1,0:T(8,128)(2,1)S(1)}, u32[]{:S(2)}, u32[]{:S(2)}) collective-permute-start(bf16[72,1024]{1,0:T(8,128)(2,1)S(1)} %dynamic-slice_bitcast_fusion.8), channel_id=1, source_target_pairs={{0,16},{4,20},{8,24},{12,28},{16,0},{20,4},{24,8},{28,12},{1,17},{... | collective-permute-start | bytes 442376 | tf_op jit(solution)/shard_map/ppermute | solution.py:614
  157.3 29.6 %collective-permute-start.19 = (bf16[144,1024]{1,0:T(8,128)(2,1)S(1)}, bf16[144,1024]{1,0:T(8,128)(2,1)S(1)}, u32[]{:S(2)}, u32[]{:S(2)}) collective-permute-start(bf16[144,1024]{1,0:T(8,128)(2,1)S(1)} %pad_maximum_fusion.6), channel_id=1, source_target_pairs={{0,8},{4,12},{8,0},{12,4},{16,24},{20,28},{24,16},{28,20},{1,9},{5... | collective-permute-start | bytes 884744 | tf_op jit(solution)/shard_map/ppermute | solution.py:614
  157.4 29.4 %collective-permute-start.20 = (bf16[72,1024]{1,0:T(8,128)(2,1)S(1)}, bf16[72,1024]{1,0:T(8,128)(2,1)S(1)}, u32[]{:S(2)}, u32[]{:S(2)}) collective-permute-start(bf16[72,1024]{1,0:T(8,128)(2,1)S(1)} %fusion.8), channel_id=1, source_target_pairs={{0,16},{4,20},{8,24},{12,28},{16,0},{20,4},{24,8},{28,12},{1,17},{... | collective-permute-start | bytes 442376 | tf_op jit(solution)/shard_map/ppermute | solution.py:614
  160.0 26.9 %collective-permute-start.21 = (bf16[72,1024]{1,0:T(8,128)(2,1)S(1)}, bf16[72,1024]{1,0:T(8,128)(2,1)}, u32[]{:S(2)}, u32[]{:S(2)}) collective-permute-start(bf16[72,1024]{1,0:T(8,128)(2,1)S(1)} %dynamic-slice_bitcast_fusion.7), channel_id=1, source_target_pairs={{0,16},{4,20},{8,24},{12,28},{16,0},{20,4},{24,8},{28,12},{1,17},{... | collective-permute-start | bytes 442376 | tf_op jit(solution)/shard_map/ppermute | solution.py:614
  161.9 24.9 %collective-permute-start.22 = (bf16[144,1024]{1,0:T(8,128)(2,1)S(1)}, bf16[144,1024]{1,0:T(8,128)(2,1)S(1)}, u32[]{:S(2)}, u32[]{:S(2)}) collective-permute-start(bf16[144,1024]{1,0:T(8,128)(2,1)S(1)} %dynamic-slice_bitcast_fusion.1), channel_id=1, source_target_pairs={{0,8},{4,12},{8,0},{12,4},{16,24},{20,28},{24,16},{28,20},{1,9},{5... | collective-permute-start | bytes 884744 | tf_op jit(solution)/shard_map/ppermute | solution.py:614
  165.2 21.7 %collective-permute-start.23 = (bf16[256,1024]{1,0:T(8,128)(2,1)S(1)}, bf16[256,1024]{1,0:T(8,128)(2,1)S(1)}, u32[]{:S(2)}, u32[]{:S(2)}) collective-permute-start(bf16[256,1024]{1,0:T(8,128)(2,1)S(1)} %add_convert_fusion.6), channel_id=1, source_target_pairs={{0,2},{1,3},{2,0},{3,1},{4,6},{5,7},{6,4},{7,5},{8,10},{9,11},{10,... | collective-permute-start | bytes 1572872 | tf_op jit(solution)/shard_map/ppermute | solution.py:614
  187.7 5.9 %collective-permute-start.24 = (bf16[448,1024]{1,0:T(8,128)(2,1)}, bf16[448,1024]{1,0:T(8,128)(2,1)S(1)}, u32[]{:S(2)}, u32[]{:S(2)}) collective-permute-start(bf16[448,1024]{1,0:T(8,128)(2,1)} %get-tuple-element.172), channel_id=1, source_target_pairs={{0,1},{1,0},{2,3},{3,2},{4,5},{5,4},{6,7},{7,6},{8,9},{9,8},{10,11... | collective-permute-start | bytes 2752520 | tf_op jit(solution)/shard_map/ppermute | solution.py:614
  188.0 20.4 %collective-permute-start.25 = (bf16[288,1024]{1,0:T(8,128)(2,1)S(1)}, bf16[288,1024]{1,0:T(8,128)(2,1)S(1)}, u32[]{:S(2)}, u32[]{:S(2)}) collective-permute-start(bf16[288,1024]{1,0:T(8,128)(2,1)S(1)} %pad_maximum_fusion.1.refs_0_), channel_id=1, source_target_pairs={{0,4},{4,0},{8,12},{12,8},{16,20},{20,16},{24,28},{28,24},{1,5},{5... | collective-permute-start | bytes 1769480 | tf_op jit(solution)/shard_map/ppermute | solution.py:614
  190.3 18.0 %collective-permute-start.26 = (bf16[144,1024]{1,0:T(8,128)(2,1)}, bf16[144,1024]{1,0:T(8,128)(2,1)}, u32[]{:S(2)}, u32[]{:S(2)}) collective-permute-start(bf16[144,1024]{1,0:T(8,128)(2,1)} %pad_maximum_fusion.7), channel_id=1, source_target_pairs={{0,8},{4,12},{8,0},{12,4},{16,24},{20,28},{24,16},{28,20},{1,9},{5... | collective-permute-start | bytes 884744 | tf_op jit(solution)/shard_map/ppermute | solution.py:614
  191.3 9.9 %collective-permute-start.27 = (bf16[72,1024]{1,0:T(8,128)(2,1)S(1)}, bf16[72,1024]{1,0:T(8,128)(2,1)}, u32[]{:S(2)}, u32[]{:S(2)}) collective-permute-start(bf16[72,1024]{1,0:T(8,128)(2,1)S(1)} %fusion.7), channel_id=1, source_target_pairs={{0,16},{4,20},{8,24},{12,28},{16,0},{20,4},{24,8},{28,12},{1,17},{... | collective-permute-start | bytes 442376 | tf_op jit(solution)/shard_map/ppermute | solution.py:614
  194.9 14.1 %collective-permute-start.29 = (bf16[224,1024]{1,0:T(8,128)(2,1)}, bf16[224,1024]{1,0:T(8,128)(2,1)}, u32[]{:S(2)}, u32[]{:S(2)}) collective-permute-start(bf16[224,1024]{1,0:T(8,128)(2,1)} %dynamic-slice_bitcast_fusion), channel_id=1, source_target_pairs={{0,2},{1,3},{2,0},{3,1},{4,6},{5,7},{6,4},{7,5},{8,10},{9,11},{10,... | collective-permute-start | bytes 1376264 | tf_op jit(solution)/shard_map/ppermute | solution.py:614
  195.9 12.4 %collective-permute-start.28 = (bf16[72,1024]{1,0:T(8,128)(2,1)S(1)}, bf16[72,1024]{1,0:T(8,128)(2,1)S(1)}, u32[]{:S(2)}, u32[]{:S(2)}) collective-permute-start(bf16[72,1024]{1,0:T(8,128)(2,1)S(1)} %dynamic-slice_bitcast_fusion.6), channel_id=1, source_target_pairs={{0,16},{4,20},{8,24},{12,28},{16,0},{20,4},{24,8},{28,12},{1,17},{... | collective-permute-start | bytes 442376 | tf_op jit(solution)/shard_map/ppermute | solution.py:614
  210.3 24.3 %collective-permute-start.31 = (bf16[288,1024]{1,0:T(8,128)(2,1)S(1)}, bf16[288,1024]{1,0:T(8,128)(2,1)S(1)}, u32[]{:S(2)}, u32[]{:S(2)}) collective-permute-start(bf16[288,1024]{1,0:T(8,128)(2,1)S(1)} %pad_maximum_fusion.2.refs_2_), channel_id=1, source_target_pairs={{0,4},{4,0},{8,12},{12,8},{16,20},{20,16},{24,28},{28,24},{1,5},{5... | collective-permute-start | bytes 1769480 | tf_op jit(solution)/shard_map/ppermute | solution.py:614
  211.9 18.0 %collective-permute-start.32 = (bf16[144,1024]{1,0:T(8,128)(2,1)S(1)}, bf16[144,1024]{1,0:T(8,128)(2,1)S(1)}, u32[]{:S(2)}, u32[]{:S(2)}) collective-permute-start(bf16[144,1024]{1,0:T(8,128)(2,1)S(1)} %pad_maximum_fusion.8), channel_id=1, source_target_pairs={{0,8},{4,12},{8,0},{12,4},{16,24},{20,28},{24,16},{28,20},{1,9},{5... | collective-permute-start | bytes 884744 | tf_op jit(solution)/shard_map/ppermute | solution.py:614
  213.2 16.5 %collective-permute-start.30 = (bf16[112,1024]{1,0:T(8,128)(2,1)S(1)}, bf16[112,1024]{1,0:T(8,128)(2,1)S(1)}, u32[]{:S(2)}, u32[]{:S(2)}) collective-permute-start(bf16[112,1024]{1,0:T(8,128)(2,1)S(1)} %dynamic-slice_bitcast_fusion.5), channel_id=1, source_target_pairs={{0,4},{4,0},{8,12},{12,8},{16,20},{20,16},{24,28},{28,24},{1,5},{5... | collective-permute-start | bytes 688136 | tf_op jit(solution)/shard_map/ppermute | solution.py:614
  214.8 15.0 %collective-permute-start.33 = (bf16[72,1024]{1,0:T(8,128)(2,1)S(1)}, bf16[72,1024]{1,0:T(8,128)(2,1)S(1)}, u32[]{:S(2)}, u32[]{:S(2)}) collective-permute-start(bf16[72,1024]{1,0:T(8,128)(2,1)S(1)} %fusion.6), channel_id=1, source_target_pairs={{0,16},{4,20},{8,24},{12,28},{16,0},{20,4},{24,8},{28,12},{1,17},{... | collective-permute-start | bytes 442376 | tf_op jit(solution)/shard_map/ppermute | solution.py:614
  229.8 4.9 %collective-permute-start.34 = (bf16[56,1024]{1,0:T(8,128)(2,1)S(1)}, bf16[56,1024]{1,0:T(8,128)(2,1)S(1)}, u32[]{:S(2)}, u32[]{:S(2)}) collective-permute-start(bf16[56,1024]{1,0:T(8,128)(2,1)S(1)} %dynamic-slice_bitcast_fusion.10), channel_id=1, source_target_pairs={{0,8},{4,12},{8,0},{12,4},{16,24},{20,28},{24,16},{28,20},{1,9},{5... | collective-permute-start | bytes 344072 | tf_op jit(solution)/shard_map/ppermute | solution.py:614
  234.8 14.1 %copy-start.3 = (bf16[288,1024]{1,0:T(8,128)(2,1)}, bf16[288,1024]{1,0:T(8,128)(2,1)S(1)}, u32[]{:S(2)}) copy-start(bf16[288,1024]{1,0:T(8,128)(2,1)S(1)} %pad_maximum_fusion.3.refs_4_) | copy-start | bytes 1769476
  234.8 12.8 %collective-permute-start.36 = (bf16[288,1024]{1,0:T(8,128)(2,1)S(1)}, bf16[288,1024]{1,0:T(8,128)(2,1)S(1)}, u32[]{:S(2)}, u32[]{:S(2)}) collective-permute-start(bf16[288,1024]{1,0:T(8,128)(2,1)S(1)} %pad_maximum_fusion.3.refs_4_), channel_id=1, source_target_pairs={{0,4},{4,0},{8,12},{12,8},{16,20},{20,16},{24,28},{28,24},{1,5},{5... | collective-permute-start | bytes 1769480 | tf_op jit(solution)/shard_map/ppermute | solution.py:614
  235.5 6.8 %collective-permute-start.35 = (bf16[56,1024]{1,0:T(8,128)(2,1)S(1)}, bf16[56,1024]{1,0:T(8,128)(2,1)S(1)}, u32[]{:S(2)}, u32[]{:S(2)}) collective-permute-start(bf16[56,1024]{1,0:T(8,128)(2,1)S(1)} %fusion.10), channel_id=1, source_target_pairs={{0,16},{4,20},{8,24},{12,28},{16,0},{20,4},{24,8},{28,12},{1,17},{... | collective-permute-start | bytes 344072 | tf_op jit(solution)/shard_map/ppermute | solution.py:614
  236.1 11.1 %collective-permute-start.37 = (bf16[144,1024]{1,0:T(8,128)(2,1)S(1)}, bf16[144,1024]{1,0:T(8,128)(2,1)S(1)}, u32[]{:S(2)}, u32[]{:S(2)}) collective-permute-start(bf16[144,1024]{1,0:T(8,128)(2,1)S(1)} %pad_maximum_fusion.9), channel_id=1, source_target_pairs={{0,8},{4,12},{8,0},{12,4},{16,24},{20,28},{24,16},{28,20},{1,9},{5... | collective-permute-start | bytes 884744 | tf_op jit(solution)/shard_map/ppermute | solution.py:614
  242.3 4.9 %collective-permute-start.38 = (bf16[56,1024]{1,0:T(8,128)(2,1)S(1)}, bf16[56,1024]{1,0:T(8,128)(2,1)S(1)}, u32[]{:S(2)}, u32[]{:S(2)}) collective-permute-start(bf16[56,1024]{1,0:T(8,128)(2,1)S(1)} %add_convert_fusion.9), channel_id=1, source_target_pairs={{0,8},{4,12},{8,0},{12,4},{16,24},{20,28},{24,16},{28,20},{1,9},{5... | collective-permute-start | bytes 344072 | tf_op jit(solution)/shard_map/ppermute | solution.py:614
  247.7 8.5 %collective-permute-start.39 = (bf16[112,1024]{1,0:T(8,128)(2,1)S(1)}, bf16[112,1024]{1,0:T(8,128)(2,1)S(1)}, u32[]{:S(2)}, u32[]{:S(2)}) collective-permute-start(bf16[112,1024]{1,0:T(8,128)(2,1)S(1)} %pad_maximum_fusion.10), channel_id=1, source_target_pairs={{0,4},{4,0},{8,12},{12,8},{16,20},{20,16},{24,28},{28,24},{1,5},{5... | collective-permute-start | bytes 688136 | tf_op jit(solution)/shard_map/ppermute | solution.py:614
  249.0 15.8 %copy-start.4 = (bf16[288,1024]{1,0:T(8,128)(2,1)}, bf16[288,1024]{1,0:T(8,128)(2,1)S(1)}, u32[]{:S(2)}) copy-start(bf16[288,1024]{1,0:T(8,128)(2,1)S(1)} %pad_maximum_fusion.4.refs_6_) | copy-start | bytes 1769476
  249.0 15.8 %collective-permute-start.40 = (bf16[288,1024]{1,0:T(8,128)(2,1)S(1)}, bf16[288,1024]{1,0:T(8,128)(2,1)S(1)}, u32[]{:S(2)}, u32[]{:S(2)}) collective-permute-start(bf16[288,1024]{1,0:T(8,128)(2,1)S(1)} %pad_maximum_fusion.4.refs_6_), channel_id=1, source_target_pairs={{0,4},{4,0},{8,12},{12,8},{16,20},{20,16},{24,28},{28,24},{1,5},{5... | collective-permute-start | bytes 1769480 | tf_op jit(solution)/shard_map/ppermute | solution.py:614
  256.4 15.7 %collective-permute-start.41 = (bf16[224,1024]{1,0:T(8,128)(2,1)S(1)}, bf16[224,1024]{1,0:T(8,128)(2,1)S(1)}, u32[]{:S(2)}, u32[]{:S(2)}) collective-permute-start(bf16[224,1024]{1,0:T(8,128)(2,1)S(1)} %pad_maximum_fusion.5), channel_id=1, source_target_pairs={{0,2},{1,3},{2,0},{3,1},{4,6},{5,7},{6,4},{7,5},{8,10},{9,11},{10,... | collective-permute-start | bytes 1376264 | tf_op jit(solution)/shard_map/ppermute | solution.py:614
  272.5 3.8 %collective-permute-start.42 = (bf16[448,1024]{1,0:T(8,128)(2,1)S(1)}, bf16[448,1024]{1,0:T(8,128)(2,1)S(1)}, u32[]{:S(2)}, u32[]{:S(2)}) collective-permute-start(bf16[448,1024]{1,0:T(8,128)(2,1)S(1)} %pad_maximum_fusion.mine_ref), channel_id=1, source_target_pairs={{0,1},{1,0},{2,3},{3,2},{4,5},{5,4},{6,7},{7,6},{8,9},{9,8},{10,11... | collective-permute-start | bytes 2752520 | tf_op jit(solution)/shard_map/ppermute | solution.py:614
  (29 other events, 88.0 us)
